TPU v7x, 32 devices: a whole 2x2x4 slice. The times are simulated.
32 devices in a mesh: wide: 8 (over z, x), narrow: 4 (over y, core).
Axes of the slice: x: 2, y: 2, z: 4, core: 2. Of those that a mesh axis runs over, the one named last changes fastest.
Arguments:
- tokens: bfloat16 [2, 2048, 2048], P(None, ('wide', 'narrow')), may hold values from -6 to 6
- lengths: int32 [2, 32], P(None, ('wide', 'narrow')), may hold values from 48 to 64, as said below
- cotangent: bfloat16 [2, 2048, 2048], P(None, ('wide', 'narrow')), may hold values from -6 to 6
- norm1_gain: bfloat16 [2048], P(('wide', 'narrow')), may hold values from 0.5 to 1.5
- query_weight: bfloat16 [2048, 2048], P(('wide', 'narrow')), may hold values from -0.125 to 0.125
- key_weight: bfloat16 [2048, 2048], P(('wide', 'narrow')), may hold values from -0.125 to 0.125
- value_weight: bfloat16 [2048, 2048], P(('wide', 'narrow')), may hold values from -0.125 to 0.125
- out_weight: bfloat16 [2048, 2048], P(('wide', 'narrow')), may hold values from -0.375 to 0.375
- norm2_gain: bfloat16 [2048], P(('wide', 'narrow')), may hold values from 0.5 to 1.5
- gate_weight: bfloat16 [2048, 8192], P(('wide', 'narrow')), may hold values from -0.125 to 0.125
- up_weight: bfloat16 [2048, 8192], P(('wide', 'narrow')), may hold values from -0.125 to 0.125
- down_weight: bfloat16 [8192, 2048], P(('wide', 'narrow')), may hold values from -0.0625 to 0.0625
Outputs:
- layer_output: bfloat16 [2, 2048, 2048], P(None, ('wide', 'narrow'))
- input_grad: float32 [2, 2048, 2048], P(None, ('wide', 'narrow'))
- norm1_gain_grad: float32 [2048], P(('wide', 'narrow'))
- query_grad: float32 [2048, 2048], P(('wide', 'narrow'))
- key_grad: float32 [2048, 2048], P(('wide', 'narrow'))
- value_grad: float32 [2048, 2048], P(('wide', 'narrow'))
- out_grad: float32 [2048, 2048], P(('wide', 'narrow'))
- norm2_gain_grad: float32 [2048], P(('wide', 'narrow'))
- gate_grad: float32 [2048, 8192], P(('wide', 'narrow'))
- up_grad: float32 [2048, 8192], P(('wide', 'narrow'))
- down_grad: float32 [8192, 2048], P(('wide', 'narrow'))
Inputs may be any that keep to these rules, and one draw needn't show every extreme that they name: `lengths`: in every micro-batch one sequence has all 64 tokens valid and another has 48.
All inputs are finite; a program needn't handle non-finite values.
Results may differ from a plain program's by a relative error of at most 0.014.
Values may be sent and summed in bfloat16 or wider, within the bound.
A program may use at most 512 MiB of HBM per device.

v0:
```python
import math

import jax
import jax.numpy as jnp
from jax import lax
from jax.sharding import PartitionSpec as P

HEAD_DIM = 128


epsilon = 1e-05
rope_base = 10000.0


def mixed_dot(left, right):
    return jnp.dot(left, right, preferred_element_type=jnp.float32)


def outer_dot(left, right):
    return lax.dot_general(
        left, right, (((0,), (0,)), ((), ())), preferred_element_type=jnp.float32
    )


def back_dot(left, right):
    return lax.dot_general(
        left, right, (((1,), (1,)), ((), ())), preferred_element_type=jnp.float32
    )


def joined(pieces):
    return jnp.concatenate(pieces, axis=0)


def rotation_tables(length):
    half_size = HEAD_DIM // 2
    position = jnp.arange(length).astype(jnp.float32)
    frequency = rope_base ** (-jnp.arange(half_size).astype(jnp.float32) / half_size)
    angles = position[:, None] * frequency[None, :]
    return (jnp.cos(angles), jnp.sin(angles))


def rotate(values, cosine, sine_table):
    half_size = values.shape[-1] // 2
    front_half = values[..., :half_size]
    back_half = values[..., half_size:]
    cos_wide = cosine[:, None, :]
    sin_wide = sine_table[:, None, :]
    return jnp.concatenate(
        [
            front_half * cos_wide - back_half * sin_wide,
            back_half * cos_wide + front_half * sin_wide,
        ],
        axis=-1,
    )


def norm_back(grad_normed, normed, inverse):
    return inverse * (grad_normed - normed * jnp.mean(grad_normed * normed, axis=-1, keepdims=True))


def score_gates(queries, keys_rot):
    length = queries.shape[0]
    scores = jnp.einsum(
        "qhd,khd->hqk", queries, keys_rot, preferred_element_type=jnp.float32
    ) * HEAD_DIM ** (-0.5) - math.log(length)
    causal = (jnp.arange(length)[:, None] >= jnp.arange(length)[None, :]).astype(jnp.float32)
    return (jax.nn.sigmoid(scores), causal)


def attention_forward(inputs, attend_full):
    norm_gain, query_weight, key_weight, value_weight, out_weight = attend_full
    length, model_width = inputs.shape
    heads_count = model_width // HEAD_DIM
    floats = inputs.astype(jnp.float32)
    inverse = lax.rsqrt(jnp.mean(floats * floats, axis=-1, keepdims=True) + epsilon)
    normed = floats * inverse
    lowered = (normed * norm_gain.astype(jnp.float32)).astype(jnp.bfloat16)
    cosine, sine_table = rotation_tables(length)
    queries = rotate(
        mixed_dot(lowered, query_weight).reshape(length, heads_count, HEAD_DIM), cosine, sine_table
    ).astype(jnp.bfloat16)
    keys_rot = rotate(
        mixed_dot(lowered, key_weight).reshape(length, heads_count, HEAD_DIM), cosine, sine_table
    ).astype(jnp.bfloat16)
    values_all = (
        mixed_dot(lowered, value_weight).astype(jnp.bfloat16).reshape(length, heads_count, HEAD_DIM)
    )
    gates_sig, causal = score_gates(queries, keys_rot)
    weights_low = (gates_sig * causal).astype(jnp.bfloat16)
    attended = jnp.einsum(
        "hqk,khd->qhd", weights_low, values_all, preferred_element_type=jnp.float32
    )
    attended = attended.astype(jnp.bfloat16).reshape(length, model_width)
    middle = floats + mixed_dot(attended, out_weight)
    return (middle, (inverse, normed, lowered, queries, keys_rot, values_all, attended))


def feed_front(middle, front_full):
    norm_gain, gate_weight, up_weight = front_full
    inverse = lax.rsqrt(jnp.mean(middle * middle, axis=-1, keepdims=True) + epsilon)
    normed = middle * inverse
    lowered = (normed * norm_gain.astype(jnp.float32)).astype(jnp.bfloat16)
    gate_value = mixed_dot(lowered, gate_weight)
    up_value = mixed_dot(lowered, up_weight)
    hidden = (jax.nn.silu(gate_value) * up_value).astype(jnp.bfloat16)
    return (hidden, (inverse, normed, lowered, gate_value, up_value, hidden))


def attention_backward(grad_middle, saved_state, attend_full):
    norm_gain, query_weight, key_weight, value_weight, out_weight = attend_full
    inverse, normed, lowered, queries, keys_rot, values_all, attended = saved_state
    length, model_width = grad_middle.shape
    heads_count = model_width // HEAD_DIM
    grad_low = grad_middle.astype(jnp.bfloat16)
    grad_attended = (
        back_dot(grad_low, out_weight).astype(jnp.bfloat16).reshape(length, heads_count, HEAD_DIM)
    )
    gates_sig, causal = score_gates(queries, keys_rot)
    weights_low = (gates_sig * causal).astype(jnp.bfloat16)
    grad_weights = jnp.einsum(
        "qhd,khd->hqk", grad_attended, values_all, preferred_element_type=jnp.float32
    )
    grad_values = jnp.einsum(
        "hqk,qhd->khd", weights_low, grad_attended, preferred_element_type=jnp.float32
    )
    grad_values = grad_values.astype(jnp.bfloat16).reshape(length, model_width)
    grad_scores = (grad_weights * gates_sig * (1.0 - gates_sig) * causal).astype(jnp.bfloat16)
    scale_factor = HEAD_DIM ** (-0.5)
    cosine, sine_table = rotation_tables(length)
    query_rot = (
        jnp.einsum("hqk,khd->qhd", grad_scores, keys_rot, preferred_element_type=jnp.float32)
        * scale_factor
    )
    key_rot = (
        jnp.einsum("hqk,qhd->khd", grad_scores, queries, preferred_element_type=jnp.float32)
        * scale_factor
    )
    grad_queries = (
        rotate(query_rot, cosine, -sine_table).astype(jnp.bfloat16).reshape(length, model_width)
    )
    grad_keys = (
        rotate(key_rot, cosine, -sine_table).astype(jnp.bfloat16).reshape(length, model_width)
    )
    grad_lowered = (
        back_dot(grad_queries, query_weight)
        + back_dot(grad_keys, key_weight)
        + back_dot(grad_values, value_weight)
    )
    gain_term = jnp.sum(grad_lowered * normed, axis=0)
    grad_inputs = grad_middle + norm_back(
        grad_lowered * norm_gain.astype(jnp.float32), normed, inverse
    )
    return (grad_inputs, gain_term, (grad_queries, grad_keys, grad_values, grad_low))


def local(
    tokens,
    lengths,
    cotangent,
    norm1_gain,
    query_weight,
    key_weight,
    value_weight,
    out_weight,
    norm2_gain,
    gate_weight,
    up_weight,
    down_weight,
):
    micro_count = tokens.shape[0]
    length = tokens.shape[1]
    position = jnp.arange(length, dtype=jnp.int32)
    row_masks = [
        (position < lengths[micro_index, 0]).astype(jnp.float32)
        for micro_index in range(micro_count)
    ]
    attend_full = (
        lax.all_gather(norm1_gain, ("wide", "narrow"), axis=0, tiled=True),
        lax.all_gather(query_weight, ("wide", "narrow"), axis=0, tiled=True),
        lax.all_gather(key_weight, ("wide", "narrow"), axis=0, tiled=True),
        lax.all_gather(value_weight, ("wide", "narrow"), axis=0, tiled=True),
        lax.all_gather(out_weight, ("wide", "narrow"), axis=0, tiled=True),
    )
    middles = []
    attend_states = []
    for micro_index in range(micro_count):
        middle, attend_state = attention_forward(tokens[micro_index], attend_full)
        middles.append(middle)
        attend_states.append(attend_state)
    front_full = (
        lax.all_gather(norm2_gain, ("wide", "narrow"), axis=0, tiled=True),
        lax.all_gather(gate_weight, ("wide", "narrow"), axis=0, tiled=True),
        lax.all_gather(up_weight, ("wide", "narrow"), axis=0, tiled=True),
    )
    feed_states = []
    for micro_index in range(micro_count):
        hidden, feed_state = feed_front(middles[micro_index], front_full)
        feed_states.append(feed_state)
    down_full = lax.all_gather(down_weight, ("wide", "narrow"), axis=0, tiled=True)
    layer_rows = []
    for micro_index in range(micro_count):
        result = (
            middles[micro_index] + mixed_dot(feed_states[micro_index][5], down_full)
        ) * row_masks[micro_index][:, None]
        layer_rows.append(result.astype(jnp.bfloat16))
    down_back = lax.all_gather(down_weight, ("wide", "narrow"), axis=0, tiled=True)
    upstreams = []
    upstream_lows = []
    grad_gates = []
    grad_ups = []
    for micro_index in range(micro_count):
        inverse, normed, lowered, gate_value, up_value, hidden = feed_states[micro_index]
        upstream = cotangent[micro_index].astype(jnp.float32) * row_masks[micro_index][:, None]
        upstream_low = upstream.astype(jnp.bfloat16)
        grad_hidden = back_dot(upstream_low, down_back)
        gate_sig = jax.nn.sigmoid(gate_value)
        grad_gates.append(
            (grad_hidden * up_value * gate_sig * (1.0 + gate_value * (1.0 - gate_sig))).astype(
                jnp.bfloat16
            )
        )
        grad_ups.append((grad_hidden * gate_value * gate_sig).astype(jnp.bfloat16))
        upstreams.append(upstream)
        upstream_lows.append(upstream_low)
    hidden_rows = joined([state[5] for state in feed_states])
    lowered_rows = joined([state[2] for state in feed_states])
    down_sum = lax.psum_scatter(
        outer_dot(hidden_rows, joined(upstream_lows)),
        ("wide", "narrow"),
        scatter_dimension=0,
        tiled=True,
    )
    gain_two, gate_back = (
        lax.all_gather(norm2_gain, ("wide", "narrow"), axis=0, tiled=True),
        lax.all_gather(gate_weight, ("wide", "narrow"), axis=0, tiled=True),
    )
    grad_loweds = [
        back_dot(grad_gates[micro_index], gate_back) for micro_index in range(micro_count)
    ]
    gate_sum = lax.psum_scatter(
        outer_dot(lowered_rows, joined(grad_gates)),
        ("wide", "narrow"),
        scatter_dimension=0,
        tiled=True,
    )
    up_back = lax.all_gather(up_weight, ("wide", "narrow"), axis=0, tiled=True)
    gain_total = jnp.zeros((tokens.shape[2],), jnp.float32)
    grad_middles = []
    for micro_index in range(micro_count):
        inverse, normed, lowered, gate_value, up_value, hidden = feed_states[micro_index]
        grad_lowered = grad_loweds[micro_index] + back_dot(grad_ups[micro_index], up_back)
        gain_total = gain_total + jnp.sum(grad_lowered * normed, axis=0)
        grad_middles.append(
            upstreams[micro_index]
            + norm_back(grad_lowered * gain_two.astype(jnp.float32), normed, inverse)
        )
    up_total = outer_dot(lowered_rows, joined(grad_ups))
    gain_two_sum, up_sum = (
        lax.psum_scatter(gain_total, ("wide", "narrow"), scatter_dimension=0, tiled=True),
        lax.psum_scatter(up_total, ("wide", "narrow"), scatter_dimension=0, tiled=True),
    )
    attend_back = (
        lax.all_gather(norm1_gain, ("wide", "narrow"), axis=0, tiled=True),
        lax.all_gather(query_weight, ("wide", "narrow"), axis=0, tiled=True),
        lax.all_gather(key_weight, ("wide", "narrow"), axis=0, tiled=True),
        lax.all_gather(value_weight, ("wide", "narrow"), axis=0, tiled=True),
        lax.all_gather(out_weight, ("wide", "narrow"), axis=0, tiled=True),
    )
    input_rows = []
    gain_first = jnp.zeros((tokens.shape[2],), jnp.float32)
    grad_lists = ([], [], [], [])
    for micro_index in range(micro_count):
        grad_inputs, gain_term, row_grads = attention_backward(
            grad_middles[micro_index], attend_states[micro_index], attend_back
        )
        input_rows.append(grad_inputs)
        gain_first = gain_first + gain_term
        for slot_index in range(4):
            grad_lists[slot_index].append(row_grads[slot_index])
    first_rows = joined([state[2] for state in attend_states])
    attended_rows = joined([state[6] for state in attend_states])
    query_total = outer_dot(first_rows, joined(grad_lists[0]))
    key_total = outer_dot(first_rows, joined(grad_lists[1]))
    value_total = outer_dot(first_rows, joined(grad_lists[2]))
    out_total = outer_dot(attended_rows, joined(grad_lists[3]))
    attend_sums = (
        lax.psum_scatter(gain_first, ("wide", "narrow"), scatter_dimension=0, tiled=True),
        lax.psum_scatter(query_total, ("wide", "narrow"), scatter_dimension=0, tiled=True),
        lax.psum_scatter(key_total, ("wide", "narrow"), scatter_dimension=0, tiled=True),
        lax.psum_scatter(value_total, ("wide", "narrow"), scatter_dimension=0, tiled=True),
        lax.psum_scatter(out_total, ("wide", "narrow"), scatter_dimension=0, tiled=True),
    )
    layer_output = jnp.stack(layer_rows)
    input_grad = jnp.stack(input_rows)
    return (
        layer_output,
        input_grad,
        attend_sums[0],
        attend_sums[1],
        attend_sums[2],
        attend_sums[3],
        attend_sums[4],
        gain_two_sum,
        gate_sum,
        up_sum,
        down_sum,
    )


def solution(mesh):
    in_specs = (
        P(None, ("wide", "narrow"), None),
        P(None, ("wide", "narrow")),
        P(None, ("wide", "narrow"), None),
        P(("wide", "narrow")),
        P(("wide", "narrow"), None),
        P(("wide", "narrow"), None),
        P(("wide", "narrow"), None),
        P(("wide", "narrow"), None),
        P(("wide", "narrow")),
        P(("wide", "narrow"), None),
        P(("wide", "narrow"), None),
        P(("wide", "narrow"), None),
    )
    out_specs = (
        P(None, ("wide", "narrow"), None),
        P(None, ("wide", "narrow"), None),
        P(("wide", "narrow")),
        P(("wide", "narrow"), None),
        P(("wide", "narrow"), None),
        P(("wide", "narrow"), None),
        P(("wide", "narrow"), None),
        P(("wide", "narrow")),
        P(("wide", "narrow"), None),
        P(("wide", "narrow"), None),
        P(("wide", "narrow"), None),
    )
    return jax.shard_map(local, mesh=mesh, in_specs=in_specs, out_specs=out_specs, check_vma=False)
```

profile of v0, /device:TPU:0, one launch (start us, length us, event | category | flops | bytes accessed | tf_op | source)
XLA Modules:
  0.0 3941.3 jit_solution(5961018587822393749)
XLA Ops:
  13.6 42.6 %all-reduce.5 = (bf16[2048]{0:T(1024)(128)(2,1)S(1)}, bf16[2048]{0:T(1024)(128)(2,1)S(1)}) all-reduce(bf16[2048]{0:T(1024)(128)(2,1)S(1)} %dynamic-update-slice, bf16[2048]{0:T(1024)(128)(2,1)S(1)} %dynamic-update-slice.1), channel_id=1, replica_groups=mesh['wide'=8,'narrow'=4] {'wide','narrow'}, use_global_device_ids=true, to_apply=%add | all-reduce | flops 4096 | bytes 16384
  56.2 1.3 fusion.151
  57.5 1.3 compare_convert_fusion
  58.9 1.2 fusion.65
  61.0 2.0 fusion.103
  63.0 1.3 fusion.58
  64.3 26.5 all-gather.10.cloned.1.call-done
  90.7 12.3 copy.59
  103.0 66.3 %all-gather.12.cloned.1.call-done = bf16[2048,2048]{1,0:T(8,128)(2,1)} async-done(((bf16[64,2048]{1,0:T(8,128)(2,1)}), bf16[2048,2048]{1,0:T(8,128)(2,1)}) %all-gather.12.cloned.1.call-update) | async-done | bytes 8388624 | tf_op jit(solution)/shard_map/all_gather | solution.py:181
  169.3 12.5 copy.60
  181.9 6.2 fusion.124
  188.2 2.7 fusion.128
  190.8 2.7 fusion.122
  193.5 2.7 fusion.126
  198.8 49.2 %all-gather.8.cloned.1.call-done = bf16[2048,2048]{1,0:T(8,128)(2,1)} async-done(((bf16[64,2048]{1,0:T(8,128)(2,1)}), bf16[2048,2048]{1,0:T(8,128)(2,1)}) %all-gather.8.cloned.1.call-update) | async-done | bytes 8388624 | tf_op jit(solution)/shard_map/all_gather | solution.py:182
  248.0 5.1 fusion.43
  253.8 1.6 fusion.42
  256.1 70.3 %all-gather.14.cloned.1.call-done = bf16[2048,2048]{1,0:T(8,128)(2,1)} async-done(((bf16[64,2048]{1,0:T(8,128)(2,1)}), bf16[2048,2048]{1,0:T(8,128)(2,1)}) %all-gather.14.cloned.1.call-update) | async-done | bytes 8388624 | tf_op jit(solution)/shard_map/all_gather | solution.py:183
  326.4 5.4 multiply_reduce_fusion.5
  332.2 1.7 multiply_reduce_fusion.4
  334.1 187.9 %all-gather.16.cloned.1.call-done = bf16[2048,8192]{1,0:T(8,128)(2,1)} async-done(((bf16[64,8192]{1,0:T(8,128)(2,1)}), bf16[2048,8192]{1,0:T(8,128)(2,1)}) %all-gather.16.cloned.1.call-update) | async-done | bytes 33554448 | tf_op jit(solution)/shard_map/all_gather | solution.py:193
  521.9 15.7 fusion.152
  537.6 179.4 %all-gather.18.cloned.1.call-done = bf16[2048,8192]{1,0:T(8,128)(2,1)} async-done(((bf16[64,8192]{1,0:T(8,128)(2,1)}), bf16[2048,8192]{1,0:T(8,128)(2,1)}) %all-gather.18.cloned.1.call-update) | async-done | bytes 33554448 | tf_op jit(solution)/shard_map/all_gather | solution.py:194
  717.0 15.6 fusion.153
  732.7 179.6 %all-gather.20.cloned.1.call-done = bf16[8192,2048]{1,0:T(8,128)(2,1)} async-done(((bf16[256,2048]{1,0:T(8,128)(2,1)}), bf16[8192,2048]{1,0:T(8,128)(2,1)}) %all-gather.20.cloned.1.call-update) | async-done | bytes 33554448 | tf_op jit(solution)/shard_map/all_gather | solution.py:200
  912.3 17.1 multiply_convert_fusion.2
  929.4 16.2 fusion.156
  945.6 16.7 multiply_reduce_fusion.1
  962.3 14.9 fusion.154
  977.1 14.9 fusion.155
  992.1 17.2 multiply_convert_fusion
  1009.2 15.8 fusion.157
  1025.1 16.4 multiply_reduce_fusion
  1041.6 1.3 fusion.147
  1042.9 6.9 fusion.45
  1051.0 2.6 fusion.44
  1056.4 8.1 fusion.78
  1065.4 8.3 fusion.82
  1073.8 1.0 copy-done.25
  1075.2 1.3 fusion.38
  1076.5 8.2 fusion.86
  1085.9 8.1 fusion.90
  1094.1 1.2 copy-done.15
  1095.3 25.1 fusion.6
  1120.5 1.2 copy-done.13
  1121.7 23.9 fusion.10
  1145.8 1.0 copy-done.10
  1147.3 23.9 fusion.14
  1172.2 6.3 fusion.146
  1178.5 6.3 fusion.145
  1184.8 2.7 convolution_add_fusion.1
  1187.6 2.7 convolution_add_fusion.3
  1190.3 2.7 convolution_add_fusion
  1193.1 3.6 fusion.64
  1196.8 43.8 %all-reduce.4 = (f32[2048]{0:T(1024)S(1)}, f32[2048]{0:T(1024)S(1)}) all-reduce(f32[2048]{0:T(1024)S(1)} %add.179, f32[2048]{0:T(1024)S(1)} %add.180), channel_id=2, replica_groups=mesh['wide'=8,'narrow'=4] {'wide','narrow'}, use_global_device_ids=true, to_apply=%region_10.11.clone | all-reduce | flops 4096 | bytes 32768
  1241.8 13.9 fusion.4
  1255.8 14.3 fusion.5
  1271.3 1.0 pad_maximum_fusion
  1272.4 162.8 %reduce-scatter.10.cloned.1.call-done = f32[64,2048]{1,0:T(8,128)} async-done(((f32[2048,2048]{1,0:T(8,128)}), f32[64,2048]{1,0:T(8,128)}) %reduce-scatter.10.cloned.1.call-update) | async-done | bytes 524304 | tf_op jit(solution)/shard_map/reduce_scatter | solution.py:290
  1435.2 187.3 %reduce-scatter.12.cloned.1.call-done = f32[64,2048]{1,0:T(8,128)} async-done(((f32[2048,2048]{1,0:T(8,128)}), f32[64,2048]{1,0:T(8,128)}) %reduce-scatter.12.cloned.1.call-update) | async-done | bytes 524304 | tf_op jit(solution)/shard_map/reduce_scatter | solution.py:291
  1622.5 187.5 %reduce-scatter.14.cloned.1.call-done = f32[64,2048]{1,0:T(8,128)} async-done(((f32[2048,2048]{1,0:T(8,128)}), f32[64,2048]{1,0:T(8,128)}) %reduce-scatter.14.cloned.1.call-update) | async-done | bytes 524304 | tf_op jit(solution)/shard_map/reduce_scatter | solution.py:292
  1810.0 706.9 %reduce-scatter.16.cloned.1.call-done = f32[64,8192]{1,0:T(8,128)} async-done(((f32[2048,8192]{1,0:T(8,128)}), f32[64,8192]{1,0:T(8,128)}) %reduce-scatter.16.cloned.1.call-update) | async-done | bytes 2097168 | tf_op jit(solution)/shard_map/reduce_scatter | solution.py:241
  2516.9 708.9 %reduce-scatter.18.cloned.1.call-done = f32[64,8192]{1,0:T(8,128)} async-done(((f32[2048,8192]{1,0:T(8,128)}), f32[64,8192]{1,0:T(8,128)}) %reduce-scatter.18.cloned.1.call-update) | async-done | bytes 2097168 | tf_op jit(solution)/shard_map/reduce_scatter | solution.py:261
  3225.8 708.8 %reduce-scatter.20.cloned.1.call-done = f32[256,2048]{1,0:T(8,128)} async-done(((f32[8192,2048]{1,0:T(8,128)}), f32[256,2048]{1,0:T(8,128)}) %reduce-scatter.20.cloned.1.call-update) | async-done | bytes 2097168 | tf_op jit(solution)/shard_map/reduce_scatter | solution.py:228
  (285 shorter events, 21.9 us)
Async XLA Ops:
  7.2 83.6 %all-gather.10.cloned.1.call-start = ((), (), s32[]{:S(2)}) async-start(), calls=%async_computation.8 | async-start | bytes 8650752 | tf_op jit(solution)/shard_map/all_gather | solution.py:180
  7.9 161.4 %all-gather.12.cloned.1.call-start = ((), (), s32[]{:S(2)}) async-start(), calls=%async_computation.9 | async-start | bytes 8650752 | tf_op jit(solution)/shard_map/all_gather | solution.py:181
  8.7 239.3 %all-gather.8.cloned.1.call-start = ((), (), s32[]{:S(2)}) async-start(), calls=%async_computation.7 | async-start | bytes 8650752 | tf_op jit(solution)/shard_map/all_gather | solution.py:182
  9.4 317.0 %all-gather.14.cloned.1.call-start = ((), (), s32[]{:S(2)}) async-start(), calls=%async_computation.10 | async-start | bytes 8650752 | tf_op jit(solution)/shard_map/all_gather | solution.py:183
  10.0 512.0 %all-gather.16.cloned.1.call-start = ((), (), s32[]{:S(2)}) async-start(), calls=%async_computation.11 | async-start | bytes 34603008 | tf_op jit(solution)/shard_map/all_gather | solution.py:193
  10.6 706.5 %all-gather.18.cloned.1.call-start = ((), (), s32[]{:S(2)}) async-start(), calls=%async_computation.12 | async-start | bytes 34603008 | tf_op jit(solution)/shard_map/all_gather | solution.py:194
  11.1 901.1 %all-gather.20.cloned.1.call-start = ((), (), s32[]{:S(2)}) async-start(), calls=%async_computation.13 | async-start | bytes 34603008 | tf_op jit(solution)/shard_map/all_gather | solution.py:200
  11.9 1260.5 %reduce-scatter.8.cloned.1.call-start = ((), (), s32[]{:S(2)}) async-start(), calls=%async_computation.14 | async-start | bytes 17301504 | tf_op jit(solution)/shard_map/reduce_scatter | solution.py:289
  56.2 137.3 %copy-start.85 = (f32[2048]{0:T(1024)}, f32[2048]{0:T(1024)S(1)}, u32[]{:S(2)}) copy-start(f32[2048]{0:T(1024)S(1)} %convert_element_type.290) | copy-start | bytes 24580
  58.8 44.2 %copy-start.94 = (f32[64]{0:T(128)}, f32[64]{0:T(128)S(1)}, u32[]{:S(2)}) copy-start(f32[64]{0:T(128)S(1)} %get-tuple-element.89) | copy-start | bytes 772
  58.9 44.2 %copy-start.97 = (f32[64]{0:T(128)}, f32[64]{0:T(128)S(1)}, u32[]{:S(2)}) copy-start(f32[64]{0:T(128)S(1)} %get-tuple-element.88) | copy-start | bytes 772
  60.1 130.7 %copy-start.92 = (f32[64]{0:T(128)}, f32[64]{0:T(128)S(1)}, u32[]{:S(2)}) copy-start(f32[64]{0:T(128)S(1)} %get-tuple-element.87) | copy-start | bytes 772
  60.1 133.4 %copy-start.90 = (f32[64]{0:T(128)}, f32[64]{0:T(128)S(1)}, u32[]{:S(2)}) copy-start(f32[64]{0:T(128)S(1)} %get-tuple-element.86) | copy-start | bytes 772
  63.0 849.3 %copy-start.30 = (bf16[64,2048]{1,0:T(8,128)(2,1)}, bf16[64,2048]{1,0:T(8,128)(2,1)S(1)}, u32[]{:S(2)}) copy-start(bf16[64,2048]{1,0:T(8,128)(2,1)S(1)} %get-tuple-element.59) | copy-start | bytes 786436
  169.3 12.6 copy-start.4
  181.9 8.9 copy-start.3
  197.5 55.5 %copy-start.23 = (f32[16,64,64]{2,1,0:T(8,128)}, f32[16,64,64]{2,1,0:T(8,128)S(1)}, u32[]{:S(2)}) copy-start(f32[16,64,64]{2,1,0:T(8,128)S(1)} %fusion.30) | copy-start | bytes 786436
  198.8 56.6 %copy-start.21 = (f32[16,64,64]{2,1,0:T(8,128)}, f32[16,64,64]{2,1,0:T(8,128)S(1)}, u32[]{:S(2)}) copy-start(f32[16,64,64]{2,1,0:T(8,128)S(1)} %fusion.35) | copy-start | bytes 786436
  253.3 78.5 %copy-start.26 = (bf16[16,8,8,128]{3,2,1,0:T(8,128)(2,1)}, bf16[16,8,8,128]{3,2,1,0:T(8,128)(2,1)S(1)}, u32[]{:S(2)}) copy-start(bf16[16,8,8,128]{3,2,1,0:T(8,128)(2,1)S(1)} %fusion.41) | copy-start | bytes 786436
  256.1 77.8 %copy-start.28 = (bf16[16,8,8,128]{3,2,1,0:T(8,128)(2,1)}, bf16[16,8,8,128]{3,2,1,0:T(8,128)(2,1)S(1)}, u32[]{:S(2)}) copy-start(bf16[16,8,8,128]{3,2,1,0:T(8,128)(2,1)S(1)} %fusion.40) | copy-start | bytes 786436
  331.8 709.7 %copy-start.8 = (f32[64,2048]{1,0:T(8,128)}, f32[64,2048]{1,0:T(8,128)S(1)}, u32[]{:S(2)}) copy-start(f32[64,2048]{1,0:T(8,128)S(1)} %get-tuple-element.80) | copy-start | bytes 1572868
  333.9 707.6 %copy-start.6 = (f32[64,2048]{1,0:T(8,128)}, f32[64,2048]{1,0:T(8,128)S(1)}, u32[]{:S(2)}) copy-start(f32[64,2048]{1,0:T(8,128)S(1)} %get-tuple-element.82) | copy-start | bytes 1572868
  334.1 383.0 %copy-start.17 = (bf16[64,2048]{1,0:T(8,128)(2,1)}, bf16[64,2048]{1,0:T(8,128)(2,1)S(1)}, u32[]{:S(2)}) copy-start(bf16[64,2048]{1,0:T(8,128)(2,1)S(1)} %multiply_convert_fusion.8) | copy-start | bytes 786436
  929.4 16.2 copy-start.14
  929.4 16.2 copy-start.12
  977.1 14.9 copy-start.32
  1009.2 15.8 copy-start.16
  1025.0 16.5 copy-start.65
  1025.0 16.5 copy-start.95
  1025.0 16.5 copy-start.98
  1041.5 8.4 copy-start.24
  1041.5 8.4 copy-start.41
  1041.5 8.8 copy-start.82
  1041.5 8.8 copy-start.84
  1041.5 9.1 copy-start.78
  1041.5 9.1 copy-start.80
  1041.5 9.4 slice-start.2
  1042.9 10.7 copy-start.34
  1042.9 8.0 slice-start.3
  1055.5 9.6 copy-start.46
  1055.5 9.6 copy-start.48
  1055.5 9.8 copy-start.42
  1055.5 9.8 copy-start.44
  1064.6 370.6 %reduce-scatter.10.cloned.1.call-start = ((), (), s32[]{:S(2)}) async-start(), calls=%async_computation.15 | async-start | bytes 17301504 | tf_op jit(solution)/shard_map/reduce_scatter | solution.py:290
  1073.8 548.8 %reduce-scatter.12.cloned.1.call-start = ((), (), s32[]{:S(2)}) async-start(), calls=%async_computation.16 | async-start | bytes 17301504 | tf_op jit(solution)/shard_map/reduce_scatter | solution.py:291
  1075.1 9.6 copy-start.60
  1076.4 8.3 copy-start.58
  1084.8 725.2 %reduce-scatter.14.cloned.1.call-start = ((), (), s32[]{:S(2)}) async-start(), calls=%async_computation.17 | async-start | bytes 17301504 | tf_op jit(solution)/shard_map/reduce_scatter | solution.py:292
  1094.0 1422.9 %reduce-scatter.16.cloned.1.call-start = ((), (), s32[]{:S(2)}) async-start(), calls=%async_computation.18 | async-start | bytes 69206016 | tf_op jit(solution)/shard_map/reduce_scatter | solution.py:241
  1120.5 2105.3 %reduce-scatter.18.cloned.1.call-start = ((), (), s32[]{:S(2)}) async-start(), calls=%async_computation.19 | async-start | bytes 69206016 | tf_op jit(solution)/shard_map/reduce_scatter | solution.py:261
  1145.6 2788.9 %reduce-scatter.20.cloned.1.call-start = ((), (), s32[]{:S(2)}) async-start(), calls=%async_computation.20 | async-start | bytes 69206016 | tf_op jit(solution)/shard_map/reduce_scatter | solution.py:228
  1172.1 12.6 slice-start.4
  1172.1 12.6 copy-start.47
  1172.1 12.6 copy-start.49
  1178.4 9.1 copy-start.43
  1178.5 9.1 copy-start.45
  1190.3 51.4 %copy-start.7 = (f32[64,2048]{1,0:T(8,128)S(1)}, f32[64,2048]{1,0:T(8,128)}, u32[]{:S(2)}) copy-start(f32[64,2048]{1,0:T(8,128)} %copy-done.6) | copy-start | bytes 1572868
  1190.3 51.4 %copy-start.99 = (f32[64]{0:T(128)S(1)}, f32[64]{0:T(128)}, u32[]{:S(2)}) copy-start(f32[64]{0:T(128)} %copy-done.97) | copy-start | bytes 772
  1241.8 13.9 copy-start.9
  1241.8 13.9 copy-start.96
  1255.7 15.2 copy-start.20
  1255.7 15.2 copy-start.66
  1255.7 15.2 copy-start.67
  1255.7 15.2 copy-start.68
  (56 other events, 169.5 us)
Sparse Core Ops, SparseCore 0:
  10.8 79.8 all-gather.9
  93.6 75.6 all-gather.11
  172.2 75.6 all-gather.7
  250.7 75.6 all-gather.13
  329.1 192.7 all-gather.15
  524.6 192.3 all-gather.17
  719.9 192.3 all-gather.19
  1064.7 182.5 reduce-scatter.7
  1250.2 184.9 reduce-scatter.9
  1437.9 184.5 reduce-scatter.11
  1625.4 184.5 reduce-scatter.13
  1812.8 704.0 reduce-scatter.15
  2519.8 705.8 reduce-scatter.17
  3228.6 705.9 reduce-scatter.19
where the time goes:
time: 3950 us; the launch traced here: 3940 us
  waiting for transfers between devices  3430 us (87%)
  matrix products  361 us (9%)
  blocking collectives  86.3 us (2%)
    reduce_scatter x1, waiting for transfers between devices, local(): lax.psum_scatter(up_total, ('wide', 'narrow'), scatter_dimension=0, tiled...  709 us
    reduce_scatter x1, waiting for transfers between devices, local(): lax.psum_scatter(outer_dot(hidden_rows, joined(upstream_lows)), ('wide',...  709 us
    reduce_scatter x1, waiting for transfers between devices, local(): lax.psum_scatter(outer_dot(lowered_rows, joined(grad_gates)), ('wide', 'n...  707 us
    all_gather x1, waiting for transfers between devices, local(): lax.all_gather(gate_weight, ('wide', 'narrow'), axis=0, tiled=True)  188 us
    reduce_scatter x1, waiting for transfers between devices, local(): lax.psum_scatter(out_total, ('wide', 'narrow'), scatter_dimension=0, tile...  188 us
    reduce_scatter x1, waiting for transfers between devices, local(): lax.psum_scatter(value_total, ('wide', 'narrow'), scatter_dimension=0, ti...  187 us
    all_gather x1, waiting for transfers between devices, local(): lax.all_gather(down_weight, ('wide', 'narrow'), axis=0, tiled=True)  180 us
    all_gather x1, waiting for transfers between devices, local(): lax.all_gather(up_weight, ('wide', 'narrow'), axis=0, tiled=True)  179 us
  transfers between devices with their start and end apart: 14, of which 13 were waited for; matrix products, arithmetic and copies ran while one was open for 6% of the time, Pallas kernels for 0%

commit v1 on v0

--- a/solution.py
+++ b/solution.py
@@ -1,3 +1,4 @@
+import functools
 import math
 
 import jax
@@ -154,7 +155,7 @@
     return (grad_inputs, gain_term, (grad_queries, grad_keys, grad_values, grad_low))
 
 
-def local(
+def gathered_plan(
     tokens,
     lengths,
     cotangent,
@@ -308,6 +309,206 @@
     )
 
 
+def gather_rows(block):
+    return lax.all_gather(block, "wide", axis=0, tiled=True)
+
+
+def scatter_rows(partial):
+    return lax.psum_scatter(
+        partial.astype(jnp.bfloat16), "wide", scatter_dimension=0, tiled=True
+    ).astype(jnp.float32)
+
+
+def to_columns(weights, wide):
+    pieces = [w.reshape(w.shape[0], wide, w.shape[1] // wide) for w in weights]
+    block = jnp.swapaxes(jnp.concatenate(pieces, axis=2), 0, 1)
+    block = lax.all_to_all(block, "wide", split_axis=0, concat_axis=0, tiled=True)
+    full = lax.all_gather(block, "narrow", axis=1, tiled=True)
+    return full.reshape(-1, full.shape[2])
+
+
+def to_rows(columns, wide, narrow):
+    rows, width = columns.shape
+    block = columns.astype(jnp.bfloat16).reshape(wide, rows // wide, width)
+    block = lax.psum_scatter(block, "narrow", scatter_dimension=1, tiled=True)
+    return lax.all_to_all(block, "wide", split_axis=0, concat_axis=0, tiled=True)
+
+
+def own_rows(block, start, width):
+    piece = block[:, :, start : start + width]
+    return jnp.swapaxes(piece, 0, 1).reshape(piece.shape[1], -1).astype(jnp.float32)
+
+
+def gather_narrow(weight):
+    return lax.all_gather(weight, "narrow", axis=0, tiled=True)
+
+
+def sum_narrow(partial):
+    return lax.psum_scatter(
+        partial.astype(jnp.bfloat16), "narrow", scatter_dimension=0, tiled=True
+    ).astype(jnp.float32)
+
+
+def rotate_heads(values, cosine, sine_table):
+    half_size = HEAD_DIM // 2
+    front_half = values[..., :half_size]
+    back_half = values[..., half_size:]
+    return jnp.concatenate(
+        [
+            front_half * cosine - back_half * sine_table,
+            back_half * cosine + front_half * sine_table,
+        ],
+        axis=-1,
+    )
+
+
+def split_plan(
+    wide,
+    narrow,
+    tokens,
+    lengths,
+    cotangent,
+    norm1_gain,
+    query_weight,
+    key_weight,
+    value_weight,
+    out_weight,
+    norm2_gain,
+    gate_weight,
+    up_weight,
+    down_weight,
+):
+    micro_count, length, width = tokens.shape
+    rows = micro_count * length
+    sequences = wide * micro_count
+    heads = width // HEAD_DIM // wide
+    head_width = heads * HEAD_DIM
+    hidden_width = gate_weight.shape[1] // wide
+    position = jnp.arange(length, dtype=jnp.int32)
+    row_mask = (position[None, :] < lengths).astype(jnp.float32).reshape(rows, 1)
+
+    gains = lax.all_gather(
+        jnp.stack([norm1_gain, norm2_gain]), ("wide", "narrow"), axis=1, tiled=True
+    ).astype(jnp.float32)
+    attend_columns = to_columns((query_weight, key_weight, value_weight), wide)
+
+    floats = tokens.reshape(rows, width).astype(jnp.float32)
+    inverse_one = lax.rsqrt(jnp.mean(floats * floats, axis=-1, keepdims=True) + epsilon)
+    normed_one = floats * inverse_one
+    first_all = gather_rows((normed_one * gains[0]).astype(jnp.bfloat16))
+    feed_columns = to_columns((gate_weight, up_weight), wide)
+    out_rows = gather_narrow(out_weight)
+    down_rows = gather_narrow(down_weight)
+
+    cosine, sine_table = rotation_tables(length)
+    cosine, sine_table = cosine[None, :, None, :], sine_table[None, :, None, :]
+    joint = mixed_dot(first_all, attend_columns)
+    by_head = (sequences, length, heads, HEAD_DIM)
+    queries = rotate_heads(joint[:, :head_width].reshape(by_head), cosine, sine_table).astype(
+        jnp.bfloat16
+    )
+    keys_rot = rotate_heads(
+        joint[:, head_width : 2 * head_width].reshape(by_head), cosine, sine_table
+    ).astype(jnp.bfloat16)
+    values_all = joint[:, 2 * head_width :].reshape(by_head).astype(jnp.bfloat16)
+    scores = jnp.einsum(
+        "sqhd,skhd->shqk", queries, keys_rot, preferred_element_type=jnp.float32
+    ) * HEAD_DIM ** (-0.5) - math.log(length)
+    causal = (position[:, None] >= position[None, :]).astype(jnp.float32)
+    gates_sig = jax.nn.sigmoid(scores)
+    weights_low = (gates_sig * causal).astype(jnp.bfloat16)
+    attended = (
+        jnp.einsum("shqk,skhd->sqhd", weights_low, values_all, preferred_element_type=jnp.float32)
+        .astype(jnp.bfloat16)
+        .reshape(sequences * length, head_width)
+    )
+    middle = floats + scatter_rows(mixed_dot(attended, out_rows))
+
+    inverse_two = lax.rsqrt(jnp.mean(middle * middle, axis=-1, keepdims=True) + epsilon)
+    normed_two = middle * inverse_two
+    second_all = gather_rows((normed_two * gains[1]).astype(jnp.bfloat16))
+    upstream = cotangent.reshape(rows, width).astype(jnp.float32) * row_mask
+    upstream_all = gather_rows(upstream.astype(jnp.bfloat16))
+
+    front = mixed_dot(second_all, feed_columns)
+    gate_value = front[:, :hidden_width]
+    up_value = front[:, hidden_width:]
+    gate_sig = jax.nn.sigmoid(gate_value)
+    hidden = (gate_value * gate_sig * up_value).astype(jnp.bfloat16)
+    feed_out = scatter_rows(mixed_dot(hidden, down_rows))
+    layer_output = ((middle + feed_out) * row_mask).astype(jnp.bfloat16)
+
+    grad_hidden = back_dot(upstream_all, down_rows)
+    grad_gate = (
+        grad_hidden * up_value * gate_sig * (1.0 + gate_value * (1.0 - gate_sig))
+    ).astype(jnp.bfloat16)
+    grad_up = (grad_hidden * gate_value * gate_sig).astype(jnp.bfloat16)
+    grad_front = jnp.concatenate([grad_gate, grad_up], axis=1)
+    grad_second = scatter_rows(back_dot(grad_front, feed_columns))
+    down_grad = sum_narrow(outer_dot(hidden, upstream_all))
+    front_block = to_rows(outer_dot(second_all, grad_front), wide, narrow)
+    gate_grad = own_rows(front_block, 0, hidden_width)
+    up_grad = own_rows(front_block, hidden_width, hidden_width)
+
+    gain_two = jnp.sum(grad_second * normed_two, axis=0)
+    grad_middle = upstream + norm_back(grad_second * gains[1], normed_two, inverse_two)
+    middle_all = gather_rows(grad_middle.astype(jnp.bfloat16))
+
+    grad_attended = back_dot(middle_all, out_rows).astype(jnp.bfloat16).reshape(by_head)
+    out_grad = sum_narrow(outer_dot(attended, middle_all))
+    grad_weights = jnp.einsum(
+        "sqhd,skhd->shqk", grad_attended, values_all, preferred_element_type=jnp.float32
+    )
+    grad_values = jnp.einsum(
+        "shqk,sqhd->skhd", weights_low, grad_attended, preferred_element_type=jnp.float32
+    ).astype(jnp.bfloat16)
+    grad_scores = (grad_weights * gates_sig * (1.0 - gates_sig) * causal).astype(jnp.bfloat16)
+    scale_factor = HEAD_DIM ** (-0.5)
+    query_rot = (
+        jnp.einsum("shqk,skhd->sqhd", grad_scores, keys_rot, preferred_element_type=jnp.float32)
+        * scale_factor
+    )
+    key_rot = (
+        jnp.einsum("shqk,sqhd->skhd", grad_scores, queries, preferred_element_type=jnp.float32)
+        * scale_factor
+    )
+    flat = (sequences * length, head_width)
+    grad_joint = jnp.concatenate(
+        [
+            rotate_heads(query_rot, cosine, -sine_table).astype(jnp.bfloat16).reshape(flat),
+            rotate_heads(key_rot, cosine, -sine_table).astype(jnp.bfloat16).reshape(flat),
+            grad_values.reshape(flat),
+        ],
+        axis=1,
+    )
+    grad_first = scatter_rows(back_dot(grad_joint, attend_columns))
+    attend_block = to_rows(outer_dot(first_all, grad_joint), wide, narrow)
+    gain_one = jnp.sum(grad_first * normed_one, axis=0)
+    input_grad = grad_middle + norm_back(grad_first * gains[0], normed_one, inverse_one)
+    gain_sums = lax.psum_scatter(
+        jnp.stack([gain_one, gain_two]), ("wide", "narrow"), scatter_dimension=1, tiled=True
+    )
+    return (
+        layer_output.reshape(tokens.shape),
+        input_grad.reshape(tokens.shape),
+        gain_sums[0],
+        own_rows(attend_block, 0, head_width),
+        own_rows(attend_block, head_width, head_width),
+        own_rows(attend_block, 2 * head_width, head_width),
+        out_grad,
+        gain_sums[1],
+        gate_grad,
+        up_grad,
+        down_grad,
+    )
+
+
+def local(wide, narrow, *arrays):
+    if arrays[0].shape[2] // HEAD_DIM % wide == 0:
+        return split_plan(wide, narrow, *arrays)
+    return gathered_plan(*arrays)
+
+
 def solution(mesh):
     in_specs = (
         P(None, ("wide", "narrow"), None),
@@ -336,4 +537,5 @@
         P(("wide", "narrow"), None),
         P(("wide", "narrow"), None),
     )
-    return jax.shard_map(local, mesh=mesh, in_specs=in_specs, out_specs=out_specs, check_vma=False)
+    body = functools.partial(local, mesh.shape["wide"], mesh.shape["narrow"])
+    return jax.shard_map(body, mesh=mesh, in_specs=in_specs, out_specs=out_specs, check_vma=False)

time: 3950 us -> 1260 us (0.32)
  waiting for transfers between devices: 3430 us -> 844 us
  matrix products: 361 us -> 107 us
  blocking collectives: 86.3 us -> 203 us
    reduce_scatter x7 -> x8, waiting for transfers between devices: 2660 us -> 371 us  [the longest x4 294 us: scatter_rows(): lax.psum_scatter(partial.astype(jnp.bfloat16), 'wide', scatter_dimension=...]
    all_gather x7 -> x8, waiting for transfers between devices: 759 us -> 336 us  [the longest x4 262 us: gather_rows(): return lax.all_gather(block, 'wide', axis=0, tiled=True)]
    all_to_all x0 -> x3, blocking collectives: none -> 163 us  [the longest x2 110 us: to_columns(): lax.all_to_all(block, 'wide', split_axis=0, concat_axis=0, tiled=True)]
    unnamed x14 -> x18, waiting for transfers between devices: 4.45 us -> 137 us
    dot_general x14 -> x4, matrix products: 133 us -> 37.6 us  [back_dot(): lax.dot_general(left, right, (((1,), (1,)), ((), ())), preferred_element_...]
    unnamed x2 -> x0, blocking collectives: 86.3 us -> none
    dot_general x14 -> x4, matrix products: 117 us -> 34.1 us  [mixed_dot(): return jnp.dot(left, right, preferred_element_type=jnp.float32)]
    dot_general x7 -> x4, matrix products: 106 us -> 32.8 us  [outer_dot(): lax.dot_general(left, right, (((0,), (0,)), ((), ())), preferred_element_...]
  transfers between devices with their start and end apart: 14 -> 18, of which waited for: 13 -> 14; matrix products, arithmetic and copies ran while one was open for 6% -> 11% of each run, Pallas kernels for 0% -> 0%
where the time goes in v1:
time: 1260 us; the launch traced here: 1250 us
  waiting for transfers between devices  844 us (67%)
  blocking collectives  203 us (16%)
  matrix products  107 us (8%)
  local copies, waits for them, and re-layouts  55.9 us (4%)
  other arithmetic  23 us (2%)
  between operations  14.9 us (1%)
    reduce_scatter x4, waiting for transfers between devices, scatter_rows(): lax.psum_scatter(partial.astype(jnp.bfloat16), 'wide', scatter_dimension=...  294 us
    all_gather x4, waiting for transfers between devices, gather_rows(): return lax.all_gather(block, 'wide', axis=0, tiled=True)  262 us
    unnamed x18, waiting for transfers between devices  137 us
    all_to_all x2, blocking collectives, to_columns(): lax.all_to_all(block, 'wide', split_axis=0, concat_axis=0, tiled=True)  110 us
    all_gather x2, waiting for transfers between devices, to_columns(): full = lax.all_gather(block, 'narrow', axis=1, tiled=True)  54.6 us
    reduce_scatter x2, waiting for transfers between devices, sum_narrow(): lax.psum_scatter(partial.astype(jnp.bfloat16), 'narrow', scatter_dimensio...  54.6 us
    all_to_all x1, blocking collectives, to_rows(): lax.all_to_all(block, 'wide', split_axis=0, concat_axis=0, tiled=True)  53.6 us
    all_gather x1, blocking collectives, split_plan(): lax.all_gather(jnp.stack([norm1_gain, norm2_gain]), ('wide', 'narrow'), a...  39.6 us
  transfers between devices with their start and end apart: 18, of which 14 were waited for; matrix products, arithmetic and copies ran while one was open for 11% of the time, Pallas kernels for 0%

profile of v1, /device:TPU:0, one launch (start us, length us, event | category | flops | bytes accessed | tf_op | source)
XLA Modules:
  0.0 1253.3 jit_solution(4223452709165951600)
XLA Ops:
  7.2 1.0 copy.158
  8.2 1.1 copy.159
  9.3 1.0 copy.160
  10.5 27.2 %all_to_all.20 = bf16[8,64,768]{2,1,0:T(8,128)(2,1)S(1)} all-to-all(bf16[8,64,768]{2,1,0:T(8,128)(2,1)S(1)} %copy.115), channel_id=1, replica_groups=mesh['wide'=8,'narrow'=4] {'wide'}, dimensions={0} | all-to-all | bytes 1572864 | tf_op jit(solution)/shard_map/all_to_all | solution.py:325
  37.8 1.3 copy.116
  39.5 39.6 %all-gather = bf16[32,64,2]{1,2,0:T(2,128)(2,1)S(1)} all-gather(bf16[1,64,2]{1,2,0:T(2,128)(2,1)S(1)} %maximum_bitcast_fusion.2), channel_id=1, replica_groups=mesh['wide'=8,'narrow'=4] {'wide','narrow'}, dimensions={0}, use_global_device_ids=true | all-gather | bytes 8448 | tf_op jit(solution)/shard_map/all_gather | solution.py:390
  79.8 1.0 fusion.27
  81.9 4.2 copy.117
  86.1 63.8 %all-gather.10.cloned.1.call-done = bf16[1024,2048]{1,0:T(8,128)(2,1)} async-done(((bf16[128,2048]{1,0:T(8,128)(2,1)}), bf16[1024,2048]{1,0:T(8,128)(2,1)}) %all-gather.10.cloned.1.call-update) | async-done | bytes 4194320 | tf_op jit(solution)/shard_map/all_gather | solution.py:313
  149.9 6.1 fusion.51
  156.0 1.6 copy-done.7
  157.8 2.7 fusion.46
  161.0 1.8 reshape.259
  162.8 2.4 fusion.47
  167.7 4.7 convolution_convert_fusion.2
  172.7 1.8 copy.162
  174.5 1.8 copy.163
  176.5 1.2 copy.124
  177.7 82.5 %all_to_all.21 = bf16[8,64,2048]{2,1,0:T(8,128)(2,1)S(1)} all-to-all(bf16[8,64,2048]{2,1,0:T(8,128)(2,1)S(1)} %copy.124), channel_id=1, replica_groups=mesh['wide'=8,'narrow'=4] {'wide'}, dimensions={0} | all-to-all | bytes 4194304 | tf_op jit(solution)/shard_map/all_to_all | solution.py:325
  260.1 2.5 copy.125
  262.7 35.7 %reduce-scatter.12.cloned.1.call-done = bf16[128,2048]{1,0:T(8,128)(2,1)} async-done(((bf16[1024,2048]{1,0:T(8,128)(2,1)}), bf16[128,2048]{1,0:T(8,128)(2,1)}) %reduce-scatter.12.cloned.1.call-update) | async-done | bytes 524304 | tf_op jit(solution)/shard_map/reduce_scatter | solution.py:317
  298.4 1.3 multiply_reduce_fusion
  299.7 2.0 multiply_convert_fusion.4
  302.7 0.9 fusion.24
  303.7 54.6 %all-gather.18.cloned.1.call-done = bf16[8,256,2048]{2,0,1:T(8,128)(2,1)} async-done(((bf16[8,64,2048]{2,0,1:T(8,128)(2,1)}), bf16[8,256,2048]{2,0,1:T(8,128)(2,1)}) %all-gather.18.cloned.1.call-update) | async-done | bytes 8388624 | tf_op jit(solution)/shard_map/all_gather | solution.py:326
  358.3 11.3 copy.126
  369.6 64.1 %all-gather.16.cloned.1.call-done = bf16[1024,2048]{1,0:T(8,128)(2,1)} async-done(((bf16[128,2048]{1,0:T(8,128)(2,1)}), bf16[1024,2048]{1,0:T(8,128)(2,1)}) %all-gather.16.cloned.1.call-update) | async-done | bytes 4194320 | tf_op jit(solution)/shard_map/all_gather | solution.py:313
  433.7 15.0 %fusion.52 = f32[1024,2048]{1,0:T(8,128)} fusion(bf16[1024,2048]{1,0:T(8,128)(2,1)} %all-gather.16.cloned.1.call-done, bf16[2048,2048]{1,0:T(8,128)(2,1)} %bitcast.149), kind=kOutput, calls=%fused_computation.120 | convolution fusion | flops 8589934592 | bytes 20971520 | tf_op jit(solution)/shard_map/dot_general | solution.py:17
  448.6 19.6 %all-gather.20.cloned.1.call-done = bf16[1024,2048]{1,0:T(8,128)(2,1)} async-done(((bf16[256,2048]{1,0:T(8,128)(2,1)}), bf16[1024,2048]{1,0:T(8,128)(2,1)}) %all-gather.20.cloned.1.call-update) | async-done | bytes 4194320 | tf_op jit(solution)/shard_map/all_gather | solution.py:343
  468.3 75.5 %all-gather.22.cloned.1.call-done = bf16[1024,2048]{1,0:T(8,128)(2,1)} async-done(((bf16[128,2048]{1,0:T(8,128)(2,1)}), bf16[1024,2048]{1,0:T(8,128)(2,1)}) %all-gather.22.cloned.1.call-update) | async-done | bytes 4194320 | tf_op jit(solution)/shard_map/all_gather | solution.py:313
  543.8 13.2 %multiply_convert_fusion.1 = (bf16[1024,1024]{1,0:T(8,128)(2,1)S(1)}, bf16[1024,1024]{1,0:T(8,128)(2,1)S(1)}, bf16[1024,1024]{1,0:T(8,128)(2,1)}) fusion(f32[1024,2048]{1,0:T(8,128)} %fusion.52, bf16[1024,2048]{1,0:T(8,128)(2,1)} %all-gather.22.cloned.1.call-done, bf16[1024,2048]{1,0:T(8,128)(2,1)} %all-gather.20.cloned.1.call-done), kind=kOutput, calls=%fused_computation.3 | convolution fusion | flops 4311744512 | bytes 23068672 | tf_op jit(solution)/shard_map/dot_general | solution.py:27
  557.0 1.3 copy-done.25
  559.0 12.7 %convolution_convert_fusion.1 = bf16[1024,2048]{1,0:T(8,128)(2,1)} fusion(bf16[2048,2048]{1,0:T(8,128)(2,1)} %bitcast.150, bf16[1024,1024]{1,0:T(8,128)(2,1)S(1)} %get-tuple-element.16, bf16[1024,1024]{1,0:T(8,128)(2,1)S(1)} %get-tuple-element.15), kind=kOutput, calls=%fused_computation.6 | convolution fusion | flops 8600420352 | bytes 16777216 | tf_op jit(solution)/shard_map/dot_general | solution.py:27
  571.9 86.8 %reduce-scatter.16.cloned.1.call-done = bf16[128,2048]{1,0:T(8,128)(2,1)} async-done(((bf16[1024,2048]{1,0:T(8,128)(2,1)}), bf16[128,2048]{1,0:T(8,128)(2,1)}) %reduce-scatter.16.cloned.1.call-update) | async-done | bytes 524304 | tf_op jit(solution)/shard_map/reduce_scatter | solution.py:317
  658.7 1.5 fusion.22
  660.3 2.3 fusion.45
  662.6 14.1 %convolution_convert_fusion = bf16[2048,2048]{1,0:T(8,128)(2,1)} fusion(bf16[1024,2048]{1,0:T(8,128)(2,1)} %all-gather.16.cloned.1.call-done, bf16[1024,1024]{1,0:T(8,128)(2,1)} %copy-done.26, bf16[1024,1024]{1,0:T(8,128)(2,1)} %copy-done.25), kind=kOutput, calls=%fused_computation | convolution fusion | flops 8602517504 | bytes 16777216 | tf_op jit(solution)/shard_map/dot_general | solution.py:21
  676.8 58.4 %all-gather.24.cloned.1.call-done = bf16[1024,2048]{1,0:T(8,128)(2,1)} async-done(((bf16[128,2048]{1,0:T(8,128)(2,1)}), bf16[1024,2048]{1,0:T(8,128)(2,1)}) %all-gather.24.cloned.1.call-update) | async-done | bytes 4194320 | tf_op jit(solution)/shard_map/all_gather | solution.py:313
  735.1 4.6 convolution_convert_fusion.10
  739.7 1.2 reshape.265
  746.2 1.4 copy-done.20
  747.6 4.9 convolution_convert_fusion.6
  752.8 9.3 convolution_convert_fusion.4
  762.2 1.0 copy-done.6
  763.2 4.4 convolution_convert_fusion.7
  767.7 7.2 convolution_convert_fusion.3
  775.0 1.5 copy-done.24
  776.5 8.3 convolution_convert_fusion.5
  784.8 22.8 %reduce-scatter.24.cloned.1.call-done = bf16[8,64,2048]{2,1,0:T(8,128)(2,1)} async-done(((bf16[8,256,2048]{2,1,0:T(8,128)(2,1)}), bf16[8,64,2048]{2,1,0:T(8,128)(2,1)}) %reduce-scatter.24.cloned.1.call-update) | async-done | bytes 2097168 | tf_op jit(solution)/shard_map/reduce_scatter | solution.py:333
  807.6 53.6 %all_to_all.22 = bf16[8,64,2048]{2,1,0:T(8,128)(2,1)S(1)} all-to-all(bf16[8,64,2048]{2,1,0:T(8,128)(2,1)} %reduce-scatter.24.cloned.1.call-done), channel_id=1, replica_groups=mesh['wide'=8,'narrow'=4] {'wide'}, dimensions={0} | all-to-all | bytes 4194304 | tf_op jit(solution)/shard_map/all_to_all | solution.py:334
  861.2 4.2 all-to-all-start.2
  865.5 29.6 %reduce-scatter.26.cloned.1.call-done = bf16[256,2048]{1,0:T(8,128)(2,1)} async-done(((bf16[1024,2048]{1,0:T(8,128)(2,1)}), bf16[256,2048]{1,0:T(8,128)(2,1)}) %reduce-scatter.26.cloned.1.call-update) | async-done | bytes 1048592 | tf_op jit(solution)/shard_map/reduce_scatter | solution.py:347
  895.0 2.8 convert_element_type.283
  897.8 25.0 %reduce-scatter.22.cloned.1.call-done = bf16[64,2048]{1,0:T(8,128)(2,1)} async-done(((bf16[256,2048]{1,0:T(8,128)(2,1)}), bf16[64,2048]{1,0:T(8,128)(2,1)}) %reduce-scatter.22.cloned.1.call-update) | async-done | bytes 262160 | tf_op jit(solution)/shard_map/reduce_scatter | solution.py:347
  922.8 1.8 convert_element_type.274
  925.1 1.5 copy.157
  926.5 1.5 copy.156
  928.0 1.4 convert_bitcast_fusion.2
  931.9 82.7 %reduce-scatter.18.cloned.1.call-done = bf16[128,2048]{1,0:T(8,128)(2,1)} async-done(((bf16[1024,2048]{1,0:T(8,128)(2,1)}), bf16[128,2048]{1,0:T(8,128)(2,1)}) %reduce-scatter.18.cloned.1.call-update) | async-done | bytes 524304 | tf_op jit(solution)/shard_map/reduce_scatter | solution.py:317
  1014.7 1.5 fusion.23
  1016.1 1.4 copy.145
  1017.6 88.5 %reduce-scatter.14.cloned.1.call-done = bf16[128,2048]{1,0:T(8,128)(2,1)} async-done(((bf16[1024,2048]{1,0:T(8,128)(2,1)}), bf16[128,2048]{1,0:T(8,128)(2,1)}) %reduce-scatter.14.cloned.1.call-update) | async-done | bytes 524304 | tf_op jit(solution)/shard_map/reduce_scatter | solution.py:317
  1106.1 3.3 fusion.18
  1109.4 135.0 %reduce-scatter.28.cloned.1.call-done = f32[64,2]{1,0:T(8,128)} async-done(((f32[2048,2]{1,0:T(8,128)}), f32[64,2]{1,0:T(8,128)}) %reduce-scatter.28.cloned.1.call-update) | async-done | bytes 528
  (134 shorter events, 18.8 us)
Async XLA Ops:
  7.2 74.7 %all-gather.12.cloned.1.call-start = ((), (), s32[]{:S(2)}) async-start(), calls=%async_computation.14 | async-start | bytes 3932160 | tf_op jit(solution)/shard_map/all_gather | solution.py:326
  8.2 30.9 %copy-start = (bf16[2,64,2048]{2,1,0:T(8,128)(2,1)S(1)}, bf16[2,64,2048]{2,1,0:T(8,128)(2,1)}, u32[]{:S(2)}) copy-start(bf16[2,64,2048]{2,1,0:T(8,128)(2,1)} %param.12) | copy-start | bytes 1572868
  9.3 30.2 %copy-start.21 = (bf16[64]{0:T(256)(128)(2,1)S(1)}, bf16[64]{0:T(256)(128)(2,1)}, u32[]{:S(2)}) copy-start(bf16[64]{0:T(256)(128)(2,1)} %param.20) | copy-start | bytes 388
  9.3 30.1 %copy-start.22 = (bf16[64]{0:T(256)(128)(2,1)S(1)}, bf16[64]{0:T(256)(128)(2,1)}, u32[]{:S(2)}) copy-start(bf16[64]{0:T(256)(128)(2,1)} %param.15) | copy-start | bytes 388
  39.1 110.8 %all-gather.10.cloned.1.call-start = ((), (), s32[]{:S(2)}) async-start(), calls=%async_computation.13 | async-start | bytes 4718592 | tf_op jit(solution)/shard_map/all_gather | solution.py:313
  39.5 46.6 %copy-start.18 = (f32[128]{0:T(128)}, f32[128]{0:T(128)S(1)}, u32[]{:S(2)}) copy-start(f32[128]{0:T(128)S(1)} %rsqrt.20) | copy-start | bytes 1540
  79.2 0.6 copy-start.16
  80.8 86.8 %all-gather.14.cloned.1.call-start = ((), (), s32[]{:S(2)}) async-start(), calls=%async_computation.15 | async-start | bytes 1310720 | tf_op jit(solution)/shard_map/all_gather | solution.py:343
  81.6 216.8 %reduce-scatter.12.cloned.1.call-start = ((), (), s32[]{:S(2)}) async-start(), calls=%async_computation.16 | async-start | bytes 4718592 | tf_op jit(solution)/shard_map/reduce_scatter | solution.py:317
  156.0 1.6 copy-start.7
  165.8 1.2 copy-start.8
  165.8 1.2 copy-start.10
  165.8 1.2 copy-start.12
  165.8 1.3 copy-start.14
  167.6 4.8 copy-start.5
  172.4 185.9 %all-gather.18.cloned.1.call-start = ((), (), s32[]{:S(2)}) async-start(), calls=%async_computation.18 | async-start | bytes 10485760 | tf_op jit(solution)/shard_map/all_gather | solution.py:326
  262.6 39.9 %copy-start.23 = (s32[2,1]{0,1:T(1,128)S(1)}, s32[2,1]{0,1:T(1,128)}, u32[]{:S(2)}) copy-start(s32[2,1]{0,1:T(1,128)} %param.13) | copy-start | bytes 28
  262.6 40.1 %copy-start.2 = (bf16[2,64,2048]{2,1,0:T(8,128)(2,1)S(1)}, bf16[2,64,2048]{2,1,0:T(8,128)(2,1)}, u32[]{:S(2)}) copy-start(bf16[2,64,2048]{2,1,0:T(8,128)(2,1)} %param.14) | copy-start | bytes 1572868
  262.6 171.0 %all-gather.16.cloned.1.call-start = ((), (), s32[]{:S(2)}) async-start(), calls=%async_computation.17 | async-start | bytes 4718592 | tf_op jit(solution)/shard_map/all_gather | solution.py:313
  301.7 166.5 %all-gather.20.cloned.1.call-start = ((), (), s32[]{:S(2)}) async-start(), calls=%async_computation.19 | async-start | bytes 5242880 | tf_op jit(solution)/shard_map/all_gather | solution.py:343
  302.5 241.3 %all-gather.22.cloned.1.call-start = ((), (), s32[]{:S(2)}) async-start(), calls=%async_computation.21 | async-start | bytes 4718592 | tf_op jit(solution)/shard_map/all_gather | solution.py:313
  303.7 355.0 %reduce-scatter.16.cloned.1.call-start = ((), (), s32[]{:S(2)}) async-start(), calls=%async_computation.22 | async-start | bytes 4718592 | tf_op jit(solution)/shard_map/reduce_scatter | solution.py:317
  557.0 1.3 copy-start.25
  557.0 2.0 copy-start.26
  571.7 87.1 %copy-start.1 = (bf16[128,2048]{1,0:T(8,128)(2,1)S(1)}, bf16[128,2048]{1,0:T(8,128)(2,1)}, u32[]{:S(2)}) copy-start(bf16[128,2048]{1,0:T(8,128)(2,1)} %reduce-scatter.12.cloned.1.call-done) | copy-start | bytes 1572868
  571.7 163.5 %all-gather.24.cloned.1.call-start = ((), (), s32[]{:S(2)}) async-start(), calls=%async_computation.23 | async-start | bytes 4718592 | tf_op jit(solution)/shard_map/all_gather | solution.py:313
  662.6 145.0 %reduce-scatter.24.cloned.1.call-start = ((), (), s32[]{:S(2)}) async-start(), calls=%async_computation.27 | async-start | bytes 10485760 | tf_op jit(solution)/shard_map/reduce_scatter | solution.py:333
  676.7 184.4 %reduce-scatter.20.cloned.1.call-start = ((), (), s32[]{:S(2)}) async-start(), calls=%async_computation.25 | async-start | bytes 3932160 | tf_op jit(solution)/shard_map/reduce_scatter | solution.py:333
  740.9 1.4 copy-start.13
  740.9 1.5 copy-start.15
  740.9 2.0 copy-start.9
  740.9 2.0 copy-start.11
  744.2 3.4 copy-start.20
  752.5 142.5 %reduce-scatter.26.cloned.1.call-start = ((), (), s32[]{:S(2)}) async-start(), calls=%async_computation.28 | async-start | bytes 5242880 | tf_op jit(solution)/shard_map/reduce_scatter | solution.py:347
  762.1 1.0 copy-start.6
  762.2 160.7 %reduce-scatter.22.cloned.1.call-start = ((), (), s32[]{:S(2)}) async-start(), calls=%async_computation.26 | async-start | bytes 1310720 | tf_op jit(solution)/shard_map/reduce_scatter | solution.py:347
  767.6 247.0 %reduce-scatter.18.cloned.1.call-start = ((), (), s32[]{:S(2)}) async-start(), calls=%async_computation.24 | async-start | bytes 4718592 | tf_op jit(solution)/shard_map/reduce_scatter | solution.py:317
  774.9 1.6 copy-start.24
  774.9 331.2 %reduce-scatter.14.cloned.1.call-start = ((), (), s32[]{:S(2)}) async-start(), calls=%async_computation.20 | async-start | bytes 4718592 | tf_op jit(solution)/shard_map/reduce_scatter | solution.py:317
  861.2 66.8 %all-to-all-start.2 = ((bf16[8,64,768]{2,1,0:T(8,128)(2,1)}), bf16[8,64,768]{2,1,0:T(8,128)(2,1)}, u32[]{:S(2)}, u32[]{:S(2)}) async-start(bf16[8,64,768]{2,1,0:T(8,128)(2,1)} %reduce-scatter.20.cloned.1.call-done), calls=%async_computation.7 | async-start | bytes 1572864 | tf_op jit(solution)/shard_map/all_to_all | solution.py:334
  865.4 378.9 %reduce-scatter.28.cloned.1.call-start = ((), (), s32[]{:S(2)}) async-start(), calls=%async_computation.29 | async-start | bytes 1081344
  926.5 88.1 %copy-start.17 = (f32[1,2048]{1,0:T(1,128)S(1)}, f32[1,2048]{1,0:T(1,128)}, u32[]{:S(2)}) copy-start(f32[1,2048]{1,0:T(1,128)} %copy-done.16) | copy-start | bytes 24580
  926.5 88.1 %copy-start.19 = (f32[128]{0:T(128)S(1)}, f32[128]{0:T(128)}, u32[]{:S(2)}) copy-start(f32[128]{0:T(128)} %copy-done.18) | copy-start | bytes 1540
  928.0 178.1 %copy-start.3 = (bf16[2,64,2048]{2,1,0:T(8,128)(2,1)S(1)}, bf16[2,64,2048]{2,1,0:T(8,128)(2,1)}, u32[]{:S(2)}) copy-start(bf16[2,64,2048]{2,1,0:T(8,128)(2,1)} %param.14) | copy-start | bytes 1572868
  928.0 178.1 %copy-start.4 = (bf16[128,2048]{1,0:T(8,128)(2,1)S(1)}, bf16[128,2048]{1,0:T(8,128)(2,1)}, u32[]{:S(2)}) copy-start(bf16[128,2048]{1,0:T(8,128)(2,1)} %reduce-scatter.16.cloned.1.call-done) | copy-start | bytes 1572868
Sparse Core Ops, SparseCore 0:
  39.2 27.6 all-gather.11
  80.9 68.8 all-gather.9
  151.4 15.2 all-gather.13
  172.5 125.8 reduce-scatter.11
  300.4 57.9 all-gather.17
  360.9 72.7 all-gather.15
  435.2 32.9 all-gather.19
  471.0 72.7 all-gather.21
  571.8 86.8 reduce-scatter.15
  662.7 72.3 all-gather.23
  737.7 69.8 reduce-scatter.23
  810.0 37.8 reduce-scatter.19
  850.4 44.5 reduce-scatter.25
  898.0 24.8 reduce-scatter.21
  926.3 88.2 reduce-scatter.17
  1018.1 87.9 reduce-scatter.13
  1108.2 136.1 reduce-scatter.27

commit v2 on v1

--- a/solution.py
+++ b/solution.py
@@ -4,9 +4,13 @@
 import jax
 import jax.numpy as jnp
 from jax import lax
+from jax.experimental import pallas as pl
+from jax.experimental.pallas import tpu as pltpu
 from jax.sharding import PartitionSpec as P
 
 HEAD_DIM = 128
+MESH = pl.DeviceIdType.MESH
+RING_COST = pl.CostEstimate(flops=0, bytes_accessed=150_000_000, transcendentals=0)
 
 
 epsilon = 1e-05
@@ -309,14 +313,148 @@
     )
 
 
-def gather_rows(block):
-    return lax.all_gather(block, "wide", axis=0, tiled=True)
-
-
-def scatter_rows(partial):
-    return lax.psum_scatter(
-        partial.astype(jnp.bfloat16), "wide", scatter_dimension=0, tiled=True
-    ).astype(jnp.float32)
+def ring_place(device, size):
+    height, side = device // 2, device % 2
+    return height * (1 - side) + (size - 1 - height) * side
+
+
+def ring_device(place, size):
+    back = place // (size // 2)
+    return (1 - back) * 2 * place + back * (2 * (size - 1 - place) + 1)
+
+
+def enter_ring(left, right):
+    barrier = pltpu.get_barrier_semaphore()
+    for device in (left, right):
+        pl.semaphore_signal(barrier, inc=1, device_id={"wide": device}, device_id_type=MESH)
+    pl.semaphore_wait(barrier, 2)
+
+
+def gather_kernel(size, block_ref, full_ref, own_sem, send_sem, recv_sem):
+    place = ring_place(lax.axis_index("wide"), size)
+    left = ring_device((place + size - 1) % size, size)
+    right = ring_device((place + 1) % size, size)
+    half = block_ref.shape[0] // 2
+    hops = size // 2
+
+    def copy(way, hop, part):
+        origin = ring_device((place + size - hop if way == 0 else place + hop) % size, size)
+        target = full_ref.at[origin, pl.ds(part * half, half)]
+        source = block_ref.at[pl.ds(part * half, half)] if hop == 0 else target
+        return pltpu.make_async_remote_copy(
+            src_ref=source,
+            dst_ref=target,
+            send_sem=send_sem.at[way, hop, part],
+            recv_sem=recv_sem.at[way, hop, part],
+            device_id={"wide": right if way == 0 else left},
+            device_id_type=MESH,
+        )
+
+    enter_ring(left, right)
+    own = pltpu.make_async_copy(block_ref, full_ref.at[lax.axis_index("wide")], own_sem)
+    sent = {}
+    for hop in range(hops):
+        for part in range(2):
+            for way in range(2):
+                if hop == hops - 1 and part != way:
+                    continue
+                if hop:
+                    sent[way, hop - 1, part].wait_recv()
+                sent[way, hop, part] = copy(way, hop, part)
+                sent[way, hop, part].start()
+        if hop == 0:
+            own.start()
+    for way in range(2):
+        sent[way, hops - 2, 1 - way].wait_recv()
+        sent[way, hops - 1, way].wait_recv()
+    for transfer in sent.values():
+        transfer.wait_send()
+    own.wait()
+
+
+def gather_rows(block, size):
+    rows, width = block.shape
+    hops = size // 2
+    full = pl.pallas_call(
+        functools.partial(gather_kernel, size),
+        out_shape=jax.ShapeDtypeStruct((size, rows, width), block.dtype),
+        in_specs=[pl.BlockSpec(memory_space=pltpu.VMEM)],
+        out_specs=pl.BlockSpec(memory_space=pl.ANY),
+        scratch_shapes=[
+            pltpu.SemaphoreType.DMA,
+            pltpu.SemaphoreType.DMA((2, hops, 2)),
+            pltpu.SemaphoreType.DMA((2, hops, 2)),
+        ],
+        compiler_params=pltpu.CompilerParams(collective_id=0, has_side_effects=True),
+        cost_estimate=RING_COST,
+        name="gather_rows",
+    )(block)
+    return full.reshape(size * rows, width)
+
+
+def scatter_kernel(size, partial_ref, sum_ref, held, send_sem, recv_sem):
+    place = ring_place(lax.axis_index("wide"), size)
+    left = ring_device((place + size - 1) % size, size)
+    right = ring_device((place + 1) % size, size)
+    rows, width = sum_ref.shape
+    rows, width = rows // 2, width // 2
+
+    def cut(way, part):
+        return pl.ds(part * rows, rows), pl.ds(way * width, width)
+
+    def mine(way, hop, part):
+        block = ring_device((place + 2 * size - 1 - hop if way == 0 else place + 1 + hop) % size, size)
+        return partial_ref.at[(block, *cut(way, part))]
+
+    def copy(way, hop, part):
+        source = mine(way, hop, part) if hop == 0 else held.at[(hop - 1, *cut(way, part))]
+        return pltpu.make_async_remote_copy(
+            src_ref=source,
+            dst_ref=held.at[(hop, *cut(way, part))],
+            send_sem=send_sem.at[way, hop, part],
+            recv_sem=recv_sem.at[way, hop, part],
+            device_id={"wide": right if way == 0 else left},
+            device_id_type=MESH,
+        )
+
+    enter_ring(left, right)
+    sent = {}
+    for hop in range(size):
+        for part in range(2):
+            for way in range(2):
+                if hop:
+                    sent[way, hop - 1, part].wait_recv()
+                    arrived = held.at[(hop - 1, *cut(way, part))]
+                    total = arrived[...].astype(jnp.float32) + mine(way, hop, part)[...].astype(
+                        jnp.float32
+                    )
+                    if hop == size - 1:
+                        sum_ref[cut(way, part)] = total
+                        continue
+                    arrived[...] = total.astype(jnp.bfloat16)
+                sent[way, hop, part] = copy(way, hop, part)
+                sent[way, hop, part].start()
+    for transfer in sent.values():
+        transfer.wait_send()
+
+
+def scatter_rows(partial, size):
+    rows, width = partial.shape[0] // size, partial.shape[1]
+    steps = size - 1
+    return pl.pallas_call(
+        functools.partial(scatter_kernel, size),
+        out_shape=jax.ShapeDtypeStruct((rows, width), jnp.float32),
+        in_specs=[pl.BlockSpec(memory_space=pltpu.VMEM)],
+        out_specs=pl.BlockSpec(memory_space=pltpu.VMEM),
+        scratch_shapes=[
+            pltpu.VMEM((steps, rows, width), jnp.bfloat16),
+            pltpu.SemaphoreType.DMA((2, steps, 2)),
+            pltpu.SemaphoreType.DMA((2, steps, 2)),
+        ],
+        compiler_params=pltpu.CompilerParams(collective_id=1, has_side_effects=True),
+        cost_estimate=RING_COST,
+        name="scatter_rows",
+    )(partial.astype(jnp.bfloat16).reshape(size, rows, width))
 
 
 def to_columns(weights, wide):
@@ -387,15 +525,18 @@
     position = jnp.arange(length, dtype=jnp.int32)
     row_mask = (position[None, :] < lengths).astype(jnp.float32).reshape(rows, 1)
 
-    gains = lax.all_gather(
-        jnp.stack([norm1_gain, norm2_gain]), ("wide", "narrow"), axis=1, tiled=True
-    ).astype(jnp.float32)
+    share = norm1_gain.shape[0]
+    gains = lax.all_gather(jnp.concatenate([norm1_gain, norm2_gain]), ("wide", "narrow"))
+    gains = gains.astype(jnp.float32)
+    gains = (gains[:, :share].reshape(width), gains[:, share:].reshape(width))
     attend_columns = to_columns((query_weight, key_weight, value_weight), wide)
 
     floats = tokens.reshape(rows, width).astype(jnp.float32)
     inverse_one = lax.rsqrt(jnp.mean(floats * floats, axis=-1, keepdims=True) + epsilon)
     normed_one = floats * inverse_one
-    first_all = gather_rows((normed_one * gains[0]).astype(jnp.bfloat16))
+    floats_all = gather_rows(tokens.reshape(rows, width), wide).astype(jnp.float32)
+    inverse_all = lax.rsqrt(jnp.mean(floats_all * floats_all, axis=-1, keepdims=True) + epsilon)
+    first_all = (floats_all * inverse_all * gains[0]).astype(jnp.bfloat16)
     feed_columns = to_columns((gate_weight, up_weight), wide)
     out_rows = gather_narrow(out_weight)
     down_rows = gather_narrow(down_weight)
@@ -422,20 +563,20 @@
         .astype(jnp.bfloat16)
         .reshape(sequences * length, head_width)
     )
-    middle = floats + scatter_rows(mixed_dot(attended, out_rows))
+    middle = floats + scatter_rows(mixed_dot(attended, out_rows), wide)
 
     inverse_two = lax.rsqrt(jnp.mean(middle * middle, axis=-1, keepdims=True) + epsilon)
     normed_two = middle * inverse_two
-    second_all = gather_rows((normed_two * gains[1]).astype(jnp.bfloat16))
+    second_all = gather_rows((normed_two * gains[1]).astype(jnp.bfloat16), wide)
     upstream = cotangent.reshape(rows, width).astype(jnp.float32) * row_mask
-    upstream_all = gather_rows(upstream.astype(jnp.bfloat16))
+    upstream_all = gather_rows(upstream.astype(jnp.bfloat16), wide)
 
     front = mixed_dot(second_all, feed_columns)
     gate_value = front[:, :hidden_width]
     up_value = front[:, hidden_width:]
     gate_sig = jax.nn.sigmoid(gate_value)
     hidden = (gate_value * gate_sig * up_value).astype(jnp.bfloat16)
-    feed_out = scatter_rows(mixed_dot(hidden, down_rows))
+    feed_out = scatter_rows(mixed_dot(hidden, down_rows), wide)
     layer_output = ((middle + feed_out) * row_mask).astype(jnp.bfloat16)
 
     grad_hidden = back_dot(upstream_all, down_rows)
@@ -444,7 +585,7 @@
     ).astype(jnp.bfloat16)
     grad_up = (grad_hidden * gate_value * gate_sig).astype(jnp.bfloat16)
     grad_front = jnp.concatenate([grad_gate, grad_up], axis=1)
-    grad_second = scatter_rows(back_dot(grad_front, feed_columns))
+    grad_second = scatter_rows(back_dot(grad_front, feed_columns), wide)
     down_grad = sum_narrow(outer_dot(hidden, upstream_all))
     front_block = to_rows(outer_dot(second_all, grad_front), wide, narrow)
     gate_grad = own_rows(front_block, 0, hidden_width)
@@ -452,7 +593,7 @@
 
     gain_two = jnp.sum(grad_second * normed_two, axis=0)
     grad_middle = upstream + norm_back(grad_second * gains[1], normed_two, inverse_two)
-    middle_all = gather_rows(grad_middle.astype(jnp.bfloat16))
+    middle_all = gather_rows(grad_middle.astype(jnp.bfloat16), wide)
 
     grad_attended = back_dot(middle_all, out_rows).astype(jnp.bfloat16).reshape(by_head)
     out_grad = sum_narrow(outer_dot(attended, middle_all))
@@ -481,22 +622,24 @@
         ],
         axis=1,
     )
-    grad_first = scatter_rows(back_dot(grad_joint, attend_columns))
+    grad_first = scatter_rows(back_dot(grad_joint, attend_columns), wide)
     attend_block = to_rows(outer_dot(first_all, grad_joint), wide, narrow)
     gain_one = jnp.sum(grad_first * normed_one, axis=0)
     input_grad = grad_middle + norm_back(grad_first * gains[0], normed_one, inverse_one)
-    gain_sums = lax.psum_scatter(
-        jnp.stack([gain_one, gain_two]), ("wide", "narrow"), scatter_dimension=1, tiled=True
-    )
+    gain_terms = jnp.concatenate([gain_one.reshape(-1, share), gain_two.reshape(-1, share)], axis=1)
+    gain_terms = lax.all_to_all(
+        gain_terms, ("wide", "narrow"), split_axis=0, concat_axis=0, tiled=True
+    )
+    gain_sums = jnp.sum(gain_terms, axis=0)
     return (
         layer_output.reshape(tokens.shape),
         input_grad.reshape(tokens.shape),
-        gain_sums[0],
+        gain_sums[:share],
         own_rows(attend_block, 0, head_width),
         own_rows(attend_block, head_width, head_width),
         own_rows(attend_block, 2 * head_width, head_width),
         out_grad,
-        gain_sums[1],
+        gain_sums[share:],
         gate_grad,
         up_grad,
         down_grad,

time: 1260 us -> 760 us (0.60)
  waiting for transfers between devices: 844 us -> 110 us
  Pallas kernels: 0 us -> 337 us
  blocking collectives: 203 us -> 101 us
    pallas_call x0 -> x8, Pallas kernels: none -> 337 us  [the longest x4 172 us: scatter_rows(): pl.pallas_call(functools.partial(scatter_kernel, size), out_shape=jax.Sha...]
    reduce_scatter x4 -> x0, waiting for transfers between devices: 294 us -> none  [scatter_rows(): lax.psum_scatter(partial.astype(jnp.bfloat16), 'wide', scatter_dimension=...]
    all_gather x4 -> x0, waiting for transfers between devices: 262 us -> none  [gather_rows(): return lax.all_gather(block, 'wide', axis=0, tiled=True)]
    unnamed x18 -> x8, waiting for transfers between devices: 137 us -> 1.32 us
    all_to_all x2 -> x1, blocking collectives: 110 us -> 27.4 us  [to_columns(): lax.all_to_all(block, 'wide', split_axis=0, concat_axis=0, tiled=True)]
    all_gather x2, waiting for transfers between devices: 54.6 us -> 0.02 us  [to_columns(): full = lax.all_gather(block, 'narrow', axis=1, tiled=True)]
    all_to_all x0 -> x1, waiting for transfers between devices: none -> 47 us  [to_columns(): lax.all_to_all(block, 'wide', split_axis=0, concat_axis=0, tiled=True)]
    all_to_all x1, blocking collectives: 53.6 us -> 23.9 us  [to_rows(): lax.all_to_all(block, 'wide', split_axis=0, concat_axis=0, tiled=True)]
  transfers between devices with their start and end apart: 18 -> 10, of which waited for: 14 -> 3; matrix products, arithmetic and copies ran while one was open for 11% -> 15% of each run, Pallas kernels for 0% -> 29%
where the time goes in v2:
time: 760 us; the launch traced here: 755 us
  Pallas kernels  337 us (44%)
  waiting for transfers between devices  110 us (14%)
  matrix products  106 us (14%)
  blocking collectives  101 us (13%)
  local copies, waits for them, and re-layouts  47.8 us (6%)
  other arithmetic  29 us (4%)
  between operations  15.1 us (2%)
  starting transfers between devices  8.51 us (1%)
    pallas_call x4, Pallas kernels, scatter_rows(): pl.pallas_call(functools.partial(scatter_kernel, size), out_shape=jax.Sha...  172 us
    pallas_call x4, Pallas kernels, gather_rows(): pl.pallas_call(functools.partial(gather_kernel, size), out_shape=jax.Shap...  165 us
    reduce_scatter x2, waiting for transfers between devices, sum_narrow(): lax.psum_scatter(partial.astype(jnp.bfloat16), 'narrow', scatter_dimensio...  61.8 us
    all_to_all x1, waiting for transfers between devices, to_columns(): lax.all_to_all(block, 'wide', split_axis=0, concat_axis=0, tiled=True)  47 us
    all_gather x1, blocking collectives, split_plan(): lax.all_gather(jnp.concatenate([norm1_gain, norm2_gain]), ('wide', 'narro...  40.2 us
    dot_general x4, matrix products, back_dot(): lax.dot_general(left, right, (((1,), (1,)), ((), ())), preferred_element_...  38 us
    dot_general x4, matrix products, outer_dot(): lax.dot_general(left, right, (((0,), (0,)), ((), ())), preferred_element_...  33.2 us
    dot_general x4, matrix products, mixed_dot(): return jnp.dot(left, right, preferred_element_type=jnp.float32)  31.8 us
  transfers between devices with their start and end apart: 10, of which 3 were waited for; matrix products, arithmetic and copies ran while one was open for 15% of the time, Pallas kernels for 29%

profile of v2, /device:TPU:0, one launch (start us, length us, event | category | flops | bytes accessed | tf_op | source)
XLA Modules:
  0.0 754.7 jit_solution(10876065880881366227)
XLA Ops:
  7.2 1.0 copy.123
  8.2 1.1 copy.124
  9.3 1.0 copy.125
  10.6 27.4 %all_to_all.29 = bf16[8,64,768]{2,1,0:T(8,128)(2,1)S(1)} all-to-all(bf16[8,64,768]{2,1,0:T(8,128)(2,1)S(1)} %copy.84), channel_id=1, replica_groups=mesh['wide'=8,'narrow'=4] {'wide'}, dimensions={0} | all-to-all | bytes 1572864 | tf_op jit(solution)/shard_map/all_to_all | solution.py:463
  37.9 1.3 copy.85
  40.7 2.5 copy.93
  43.1 3.6 all-to-all-start.1
  47.6 47.0 %all-to-all-done.1 = bf16[8,64,2048]{2,1,0:T(8,128)(2,1)S(1)} async-done(((bf16[8,64,2048]{2,1,0:T(8,128)(2,1)}), bf16[8,64,2048]{2,1,0:T(8,128)(2,1)S(1)}, u32[]{:S(2)}, u32[]{:S(2)}) %all-to-all-start.1) | async-done | bytes 2097184 | tf_op jit(solution)/shard_map/all_to_all | solution.py:463
  94.6 2.5 copy.94
  98.0 40.2 %all-gather.1 = bf16[32,1,128]{2,1,0:T(2,128)(2,1)S(1)} all-gather(bf16[1,1,128]{2,1,0:T(2,128)(2,1)S(1)} %maximum_bitcast_fusion.2), channel_id=2, replica_groups=mesh['wide'=8,'narrow'=4] {'wide','narrow'}, dimensions={0}, use_global_device_ids=true | all-gather | bytes 8448 | tf_op jit(solution)/shard_map/all_gather | solution.py:529
  138.5 1.0 fusion.23.block_ref
  139.4 43.9 %gather_rows.6 = bf16[8,128,2048]{2,1,0:T(8,128)(2,1)} custom-call(bf16[128,2048]{1,0:T(8,128)(2,1)} %fusion.23.block_ref), custom_call_target="tpu_custom_call" | custom-call | bytes 150000000 | tf_op jit(solution)/shard_map/gather_rows/pallas_call | solution.py:378
  183.3 43.6 %gather_rows.4 = bf16[8,128,2048]{2,1,0:T(8,128)(2,1)} custom-call(bf16[128,2048]{1,0:T(8,128)(2,1)} %bitcast.122), custom_call_target="tpu_custom_call" | custom-call | bytes 150000000 | tf_op jit(solution)/shard_map/gather_rows/pallas_call | solution.py:378
  227.0 3.2 multiply_reduce_fusion
  230.4 3.1 fusion.1
  233.5 3.0 multiply_convert_fusion
  236.5 2.6 copy.86
  239.7 3.4 fusion.47
  243.1 1.6 copy-done.13
  244.9 2.7 fusion.42
  248.1 1.7 reshape.323
  249.8 2.4 fusion.43
  252.9 1.0 fusion.10
  253.9 1.0 copy-done.4
  255.9 0.7 copy-done.10
  256.6 4.5 convolution_convert_fusion.2
  261.1 45.5 %scatter_rows.4 = f32[128,2048]{1,0:T(8,128)} custom-call(bf16[8,128,2048]{2,1,0:T(8,128)(2,1)} %bitcast.121), custom_call_target="tpu_custom_call" | custom-call | bytes 150000000 | tf_op jit(solution)/shard_map/scatter_rows/pallas_call | solution.py:444
  306.6 1.4 multiply_reduce_fusion.4
  308.1 1.0 multiply_convert_fusion.5.block_ref
  309.1 42.3 %gather_rows.5 = bf16[8,128,2048]{2,1,0:T(8,128)(2,1)} custom-call(bf16[128,2048]{1,0:T(8,128)(2,1)} %multiply_convert_fusion.5.block_ref), custom_call_target="tpu_custom_call" | custom-call | bytes 150000000 | tf_op jit(solution)/shard_map/gather_rows/pallas_call | solution.py:378
  351.4 11.3 %copy.95 = bf16[8,256,2048]{2,1,0:T(8,128)(2,1)} copy(bf16[8,256,2048]{2,0,1:T(8,128)(2,1)} %all-gather.11.cloned.1.call-done) | data formatting | bytes 16777216 | tf_op jit(solution)/shard_map/all_gather | solution.py:464
  362.6 14.7 %fusion.48 = f32[1024,2048]{1,0:T(8,128)} fusion(bf16[1024,2048]{1,0:T(8,128)(2,1)} %bitcast.131, bf16[2048,2048]{1,0:T(8,128)(2,1)} %bitcast.124), kind=kOutput, calls=%fused_computation.116 | convolution fusion | flops 8589934592 | bytes 20971520 | tf_op jit(solution)/shard_map/dot_general | solution.py:21
  377.3 14.0 %multiply_convert_fusion.2 = (bf16[1024,1024]{1,0:T(8,128)(2,1)S(1)}, bf16[1024,1024]{1,0:T(8,128)(2,1)}, bf16[1024,1024]{1,0:T(8,128)(2,1)}) fusion(f32[1024,2048]{1,0:T(8,128)} %fusion.48, bf16[1024,2048]{1,0:T(8,128)(2,1)} %bitcast.129, bf16[1024,2048]{1,0:T(8,128)(2,1)} %all-gather.13.cloned.1.call-done), kind=kOutput, calls=%fused_computation.8 | convolution fusion | flops 4311744512 | bytes 23068672 | tf_op jit(solution)/shard_map/dot_general | solution.py:31
  391.3 12.8 %convolution_convert_fusion.1 = bf16[1024,2048]{1,0:T(8,128)(2,1)} fusion(bf16[2048,2048]{1,0:T(8,128)(2,1)S(1)} %bitcast.125, bf16[1024,1024]{1,0:T(8,128)(2,1)} %get-tuple-element.20, bf16[1024,1024]{1,0:T(8,128)(2,1)S(1)} %get-tuple-element.19), kind=kOutput, calls=%fused_computation.11 | convolution fusion | flops 8600420352 | bytes 16777216 | tf_op jit(solution)/shard_map/dot_general | solution.py:31
  404.1 43.2 %scatter_rows.6 = f32[128,2048]{1,0:T(8,128)} custom-call(bf16[8,128,2048]{2,1,0:T(8,128)(2,1)} %bitcast.127), custom_call_target="tpu_custom_call" | custom-call | bytes 150000000 | tf_op jit(solution)/shard_map/scatter_rows/pallas_call | solution.py:444
  447.3 9.3 %convolution_convert_fusion.5 = bf16[1024,2048]{1,0:T(8,128)(2,1)} fusion(bf16[1024,1024]{1,0:T(8,128)(2,1)} %get-tuple-element.21, bf16[1024,2048]{1,0:T(8,128)(2,1)} %all-gather.13.cloned.1.call-done), kind=kOutput, calls=%fused_computation.15 | convolution fusion | flops 4297064448 | bytes 10485760 | tf_op jit(solution)/shard_map/dot_general | solution.py:21
  456.6 43.2 %scatter_rows.5 = f32[128,2048]{1,0:T(8,128)} custom-call(bf16[8,128,2048]{2,1,0:T(8,128)(2,1)} %bitcast.128), custom_call_target="tpu_custom_call" | custom-call | bytes 150000000 | tf_op jit(solution)/shard_map/scatter_rows/pallas_call | solution.py:444
  500.2 3.2 fusion.40
  503.4 35.1 %gather_rows.7 = bf16[8,128,2048]{2,1,0:T(8,128)(2,1)} custom-call(bf16[128,2048]{1,0:T(8,128)(2,1)} %get-tuple-element.15.block_ref), custom_call_target="tpu_custom_call" | custom-call | bytes 150000000 | tf_op jit(solution)/shard_map/gather_rows/pallas_call | solution.py:378
  538.5 4.4 convolution_convert_fusion.10
  542.9 1.2 reshape.335
  546.8 0.7 subtract_convert_fusion
  549.8 4.9 convolution_convert_fusion.6
  554.7 14.1 %convolution_convert_fusion = bf16[2048,2048]{1,0:T(8,128)(2,1)} fusion(bf16[1024,2048]{1,0:T(8,128)(2,1)} %bitcast.132, bf16[1024,1024]{1,0:T(8,128)(2,1)} %get-tuple-element.20, bf16[1024,1024]{1,0:T(8,128)(2,1)} %copy-done.31), kind=kOutput, calls=%fused_computation.5 | convolution fusion | flops 8602517504 | bytes 16777216 | tf_op jit(solution)/shard_map/dot_general | solution.py:25
  568.9 1.0 copy-done.11
  569.9 4.9 convolution_convert_fusion.7
  575.0 9.4 %convolution_convert_fusion.4 = bf16[1024,2048]{1,0:T(8,128)(2,1)} fusion(bf16[1024,1024]{1,0:T(8,128)(2,1)} %get-tuple-element.21, bf16[1024,2048]{1,0:T(8,128)(2,1)} %bitcast.130), kind=kOutput, calls=%fused_computation.14 | convolution fusion | flops 4297064448 | bytes 10485760 | tf_op jit(solution)/shard_map/dot_general | solution.py:25
  584.8 6.9 convolution_convert_fusion.3
  591.7 40.1 %scatter_rows.7 = f32[128,2048]{1,0:T(8,128)} custom-call(bf16[8,128,2048]{2,1,0:T(8,128)(2,1)} %bitcast.126), custom_call_target="tpu_custom_call" | custom-call | bytes 150000000 | tf_op jit(solution)/shard_map/scatter_rows/pallas_call | solution.py:444
  631.8 1.8 fusion.21
  633.7 9.7 %all_to_all.30 = f32[32,1,128]{2,1,0:T(1,128)S(1)} all-to-all(f32[32,1,128]{2,1,0:T(1,128)S(1)} %bitcast.162), channel_id=1, replica_groups=mesh['wide'=8,'narrow'=4] {'wide','narrow'}, dimensions={0} | all-to-all | bytes 32768 | tf_op jit(solution)/shard_map/all_to_all | solution.py:630
  643.4 23.9 %all_to_all.31 = bf16[8,64,768]{2,1,0:T(8,128)(2,1)S(1)} all-to-all(bf16[8,64,768]{2,1,0:T(8,128)(2,1)} %reduce-scatter.5.cloned.1.call-done), channel_id=1, replica_groups=mesh['wide'=8,'narrow'=4] {'wide'}, dimensions={0} | all-to-all | bytes 1572864 | tf_op jit(solution)/shard_map/all_to_all | solution.py:472
  667.3 4.3 all-to-all-start.4
  671.7 1.3 fusion.20
  673.6 19.2 %reduce-scatter.7.cloned.1.call-done = bf16[64,2048]{1,0:T(8,128)(2,1)} async-done(((bf16[256,2048]{1,0:T(8,128)(2,1)}), bf16[64,2048]{1,0:T(8,128)(2,1)}) %reduce-scatter.7.cloned.1.call-update) | async-done | bytes 262160 | tf_op jit(solution)/shard_map/reduce_scatter | solution.py:485
  692.8 1.8 convert_element_type.274
  694.7 0.8 copy.120
  695.6 0.8 copy.119
  696.4 0.8 copy.118
  697.3 42.6 %reduce-scatter.11.cloned.1.call-done = bf16[256,2048]{1,0:T(8,128)(2,1)} async-done(((bf16[1024,2048]{1,0:T(8,128)(2,1)}), bf16[256,2048]{1,0:T(8,128)(2,1)}) %reduce-scatter.11.cloned.1.call-update) | async-done | bytes 1048592 | tf_op jit(solution)/shard_map/reduce_scatter | solution.py:485
  739.9 2.8 convert_element_type.283
  742.7 2.0 convert_bitcast_fusion
  744.7 1.5 copy.122
  746.1 1.5 copy.121
  (131 shorter events, 13.4 us)
Async XLA Ops:
  7.2 229.3 %all-gather.7.cloned.1.call-start = ((), (), s32[]{:S(2)}) async-start(), calls=%async_computation.9 | async-start | bytes 3932160 | tf_op jit(solution)/shard_map/all_gather | solution.py:464
  8.2 31.0 %copy-start.23 = (bf16[64,8192]{1,0:T(8,128)(2,1)S(1)}, bf16[64,8192]{1,0:T(8,128)(2,1)}, u32[]{:S(2)}) copy-start(bf16[64,8192]{1,0:T(8,128)(2,1)} %param.21) | copy-start | bytes 3145732
  10.4 29.5 %copy-start.24 = (bf16[64,8192]{1,0:T(8,128)(2,1)S(1)}, bf16[64,8192]{1,0:T(8,128)(2,1)}, u32[]{:S(2)}) copy-start(bf16[64,8192]{1,0:T(8,128)(2,1)} %param.22) | copy-start | bytes 3145732
  43.1 51.5 %all-to-all-start.1 = ((bf16[8,64,2048]{2,1,0:T(8,128)(2,1)}), bf16[8,64,2048]{2,1,0:T(8,128)(2,1)S(1)}, u32[]{:S(2)}, u32[]{:S(2)}) async-start(bf16[8,64,2048]{2,1,0:T(8,128)(2,1)} %copy.93), calls=%async_computation.1 | async-start | bytes 4194304 | tf_op jit(solution)/shard_map/all_to_all | solution.py:463
  46.8 51.0 %copy-start.28 = (s32[2,1]{0,1:T(1,128)S(1)}, s32[2,1]{0,1:T(1,128)}, u32[]{:S(2)}) copy-start(s32[2,1]{0,1:T(1,128)} %param.13) | copy-start | bytes 28
  46.8 51.2 %copy-start.29 = (bf16[64]{0:T(256)(128)(2,1)S(1)}, bf16[64]{0:T(256)(128)(2,1)}, u32[]{:S(2)}) copy-start(bf16[64]{0:T(256)(128)(2,1)} %param.20) | copy-start | bytes 388
  46.8 51.1 %copy-start.30 = (bf16[64]{0:T(256)(128)(2,1)S(1)}, bf16[64]{0:T(256)(128)(2,1)}, u32[]{:S(2)}) copy-start(bf16[64]{0:T(256)(128)(2,1)} %param.15) | copy-start | bytes 388
  46.8 91.6 %copy-start.22 = (bf16[2,64,2048]{2,1,0:T(8,128)(2,1)S(1)}, bf16[2,64,2048]{2,1,0:T(8,128)(2,1)}, u32[]{:S(2)}) copy-start(bf16[2,64,2048]{2,1,0:T(8,128)(2,1)} %param.14) | copy-start | bytes 1572868
  46.8 209.0 %all-gather.9.cloned.1.call-start = ((), (), s32[]{:S(2)}) async-start(), calls=%async_computation.10 | async-start | bytes 1310720 | tf_op jit(solution)/shard_map/all_gather | solution.py:481
  47.6 303.8 %all-gather.11.cloned.1.call-start = ((), (), s32[]{:S(2)}) async-start(), calls=%async_computation.11 | async-start | bytes 10485760 | tf_op jit(solution)/shard_map/all_gather | solution.py:464
  97.1 280.2 %all-gather.13.cloned.1.call-start = ((), (), s32[]{:S(2)}) async-start(), calls=%async_computation.12 | async-start | bytes 5242880 | tf_op jit(solution)/shard_map/all_gather | solution.py:481
  97.7 545.7 %reduce-scatter.5.cloned.1.call-start = ((), (), s32[]{:S(2)}) async-start(), calls=%async_computation.13 | async-start | bytes 3932160 | tf_op jit(solution)/shard_map/reduce_scatter | solution.py:471
  138.5 95.0 %copy-start.26 = (f32[2048]{0:T(1024)}, f32[2048]{0:T(1024)S(1)}, u32[]{:S(2)}) copy-start(f32[2048]{0:T(1024)S(1)} %mul.441) | copy-start | bytes 24580
  227.0 3.5 copy-start
  236.5 3.1 copy-start.8
  239.2 3.9 copy-start.12
  243.1 1.6 copy-start.13
  252.9 2.4 copy-start.14
  252.9 2.4 copy-start.16
  252.9 2.4 copy-start.18
  252.9 2.4 copy-start.20
  253.9 1.0 copy-start.4
  255.8 0.8 copy-start.10
  261.1 45.6 %copy-start.1 = (bf16[2,64,2048]{2,1,0:T(8,128)(2,1)S(1)}, bf16[2,64,2048]{2,1,0:T(8,128)(2,1)}, u32[]{:S(2)}) copy-start(bf16[2,64,2048]{2,1,0:T(8,128)(2,1)} %param.12) | copy-start | bytes 1572868
  377.3 14.0 %copy-start.6 = (bf16[8,256,2048]{2,1,0:T(8,128)(2,1)S(1)}, bf16[8,256,2048]{2,1,0:T(8,128)(2,1)}, u32[]{:S(2)}) copy-start(bf16[8,256,2048]{2,1,0:T(8,128)(2,1)} %copy.95) | copy-start | bytes 25165828
  391.3 12.8 %copy-start.31 = (bf16[1024,1024]{1,0:T(8,128)(2,1)}, bf16[1024,1024]{1,0:T(8,128)(2,1)S(1)}, u32[]{:S(2)}) copy-start(bf16[1024,1024]{1,0:T(8,128)(2,1)S(1)} %get-tuple-element.19) | copy-start | bytes 6291460
  456.6 43.2 %copy-start.2 = (f32[128,2048]{1,0:T(8,128)S(1)}, f32[128,2048]{1,0:T(8,128)}, u32[]{:S(2)}) copy-start(f32[128,2048]{1,0:T(8,128)} %scatter_rows.6) | copy-start | bytes 3145732
  503.4 35.1 %copy-start.25 = (bf16[256,2048]{1,0:T(8,128)(2,1)S(1)}, bf16[256,2048]{1,0:T(8,128)(2,1)}, u32[]{:S(2)}) copy-start(bf16[256,2048]{1,0:T(8,128)(2,1)} %all-gather.9.cloned.1.call-done) | copy-start | bytes 3145732
  538.5 5.6 copy-start.5
  542.9 3.0 copy-start.15
  544.1 1.0 copy-start.19
  544.1 1.2 copy-start.21
  544.1 1.7 copy-start.17
  547.6 2.2 copy-start.7
  554.7 112.6 %reduce-scatter.9.cloned.1.call-start = ((), (), s32[]{:S(2)}) async-start(), calls=%async_computation.15 | async-start | bytes 10485760 | tf_op jit(solution)/shard_map/reduce_scatter | solution.py:471
  568.8 1.0 copy-start.11
  568.8 123.9 %reduce-scatter.7.cloned.1.call-start = ((), (), s32[]{:S(2)}) async-start(), calls=%async_computation.14 | async-start | bytes 1310720 | tf_op jit(solution)/shard_map/reduce_scatter | solution.py:485
  574.8 165.1 %reduce-scatter.11.cloned.1.call-start = ((), (), s32[]{:S(2)}) async-start(), calls=%async_computation.16 | async-start | bytes 5242880 | tf_op jit(solution)/shard_map/reduce_scatter | solution.py:485
  591.7 40.1 %copy-start.27 = (f32[2048]{0:T(1024)S(1)}, f32[2048]{0:T(1024)}, u32[]{:S(2)}) copy-start(f32[2048]{0:T(1024)} %copy-done.26) | copy-start | bytes 24580
  631.8 39.9 %copy-start.3 = (f32[128,2048]{1,0:T(8,128)S(1)}, f32[128,2048]{1,0:T(8,128)}, u32[]{:S(2)}) copy-start(f32[128,2048]{1,0:T(8,128)} %scatter_rows.7) | copy-start | bytes 3145732
  631.8 39.9 %copy-start.9 = (f32[128,2048]{1,0:T(8,128)S(1)}, f32[128,2048]{1,0:T(8,128)}, u32[]{:S(2)}) copy-start(f32[128,2048]{1,0:T(8,128)} %get-tuple-element.16) | copy-start | bytes 3145732
  667.3 75.4 %all-to-all-start.4 = ((bf16[8,64,2048]{2,1,0:T(8,128)(2,1)}), bf16[8,64,2048]{2,1,0:T(8,128)(2,1)}, u32[]{:S(2)}, u32[]{:S(2)}) async-start(bf16[8,64,2048]{2,1,0:T(8,128)(2,1)} %reduce-scatter.9.cloned.1.call-done), calls=%async_computation.7 | async-start | bytes 4194304 | tf_op jit(solution)/shard_map/all_to_all | solution.py:472
Sparse Core Ops, SparseCore 0:
  39.4 27.5 all-gather.6
  68.5 16.6 all-gather.8
  97.2 57.4 all-gather.10
  156.2 34.4 all-gather.12
  554.8 35.9 reduce-scatter.4
  593.3 71.4 reduce-scatter.8
  667.9 24.8 reduce-scatter.6
  695.3 44.5 reduce-scatter.10

commit v3 on v2

--- a/solution.py
+++ b/solution.py
@@ -8,7 +8,10 @@
 from jax.experimental.pallas import tpu as pltpu
 from jax.sharding import PartitionSpec as P
 
+
 HEAD_DIM = 128
+AXES = ("wide", "narrow")
+WIDE, NARROW = AXES
 MESH = pl.DeviceIdType.MESH
 RING_COST = pl.CostEstimate(flops=0, bytes_accessed=150_000_000, transcendentals=0)
 
@@ -114,7 +117,7 @@
 
 def attention_backward(grad_middle, saved_state, attend_full):
     norm_gain, query_weight, key_weight, value_weight, out_weight = attend_full
-    inverse, normed, lowered, queries, keys_rot, values_all, attended = saved_state
+    inverse, normed, _, queries, keys_rot, values_all, _ = saved_state
     length, model_width = grad_middle.shape
     heads_count = model_width // HEAD_DIM
     grad_low = grad_middle.astype(jnp.bfloat16)
@@ -181,11 +184,11 @@
         for micro_index in range(micro_count)
     ]
     attend_full = (
-        lax.all_gather(norm1_gain, ("wide", "narrow"), axis=0, tiled=True),
-        lax.all_gather(query_weight, ("wide", "narrow"), axis=0, tiled=True),
-        lax.all_gather(key_weight, ("wide", "narrow"), axis=0, tiled=True),
-        lax.all_gather(value_weight, ("wide", "narrow"), axis=0, tiled=True),
-        lax.all_gather(out_weight, ("wide", "narrow"), axis=0, tiled=True),
+        lax.all_gather(norm1_gain, AXES, axis=0, tiled=True),
+        lax.all_gather(query_weight, AXES, axis=0, tiled=True),
+        lax.all_gather(key_weight, AXES, axis=0, tiled=True),
+        lax.all_gather(value_weight, AXES, axis=0, tiled=True),
+        lax.all_gather(out_weight, AXES, axis=0, tiled=True),
     )
     middles = []
     attend_states = []
@@ -194,22 +197,22 @@
         middles.append(middle)
         attend_states.append(attend_state)
     front_full = (
-        lax.all_gather(norm2_gain, ("wide", "narrow"), axis=0, tiled=True),
-        lax.all_gather(gate_weight, ("wide", "narrow"), axis=0, tiled=True),
-        lax.all_gather(up_weight, ("wide", "narrow"), axis=0, tiled=True),
+        lax.all_gather(norm2_gain, AXES, axis=0, tiled=True),
+        lax.all_gather(gate_weight, AXES, axis=0, tiled=True),
+        lax.all_gather(up_weight, AXES, axis=0, tiled=True),
     )
     feed_states = []
     for micro_index in range(micro_count):
         hidden, feed_state = feed_front(middles[micro_index], front_full)
         feed_states.append(feed_state)
-    down_full = lax.all_gather(down_weight, ("wide", "narrow"), axis=0, tiled=True)
+    down_full = lax.all_gather(down_weight, AXES, axis=0, tiled=True)
     layer_rows = []
     for micro_index in range(micro_count):
         result = (
             middles[micro_index] + mixed_dot(feed_states[micro_index][5], down_full)
         ) * row_masks[micro_index][:, None]
         layer_rows.append(result.astype(jnp.bfloat16))
-    down_back = lax.all_gather(down_weight, ("wide", "narrow"), axis=0, tiled=True)
+    down_back = lax.all_gather(down_weight, AXES, axis=0, tiled=True)
     upstreams = []
     upstream_lows = []
     grad_gates = []
@@ -232,24 +235,24 @@
     lowered_rows = joined([state[2] for state in feed_states])
     down_sum = lax.psum_scatter(
         outer_dot(hidden_rows, joined(upstream_lows)),
-        ("wide", "narrow"),
+        AXES,
         scatter_dimension=0,
         tiled=True,
     )
     gain_two, gate_back = (
-        lax.all_gather(norm2_gain, ("wide", "narrow"), axis=0, tiled=True),
-        lax.all_gather(gate_weight, ("wide", "narrow"), axis=0, tiled=True),
+        lax.all_gather(norm2_gain, AXES, axis=0, tiled=True),
+        lax.all_gather(gate_weight, AXES, axis=0, tiled=True),
     )
     grad_loweds = [
         back_dot(grad_gates[micro_index], gate_back) for micro_index in range(micro_count)
     ]
     gate_sum = lax.psum_scatter(
         outer_dot(lowered_rows, joined(grad_gates)),
-        ("wide", "narrow"),
+        AXES,
         scatter_dimension=0,
         tiled=True,
     )
-    up_back = lax.all_gather(up_weight, ("wide", "narrow"), axis=0, tiled=True)
+    up_back = lax.all_gather(up_weight, AXES, axis=0, tiled=True)
     gain_total = jnp.zeros((tokens.shape[2],), jnp.float32)
     grad_middles = []
     for micro_index in range(micro_count):
@@ -262,15 +265,15 @@
         )
     up_total = outer_dot(lowered_rows, joined(grad_ups))
     gain_two_sum, up_sum = (
-        lax.psum_scatter(gain_total, ("wide", "narrow"), scatter_dimension=0, tiled=True),
-        lax.psum_scatter(up_total, ("wide", "narrow"), scatter_dimension=0, tiled=True),
+        lax.psum_scatter(gain_total, AXES, scatter_dimension=0, tiled=True),
+        lax.psum_scatter(up_total, AXES, scatter_dimension=0, tiled=True),
     )
     attend_back = (
-        lax.all_gather(norm1_gain, ("wide", "narrow"), axis=0, tiled=True),
-        lax.all_gather(query_weight, ("wide", "narrow"), axis=0, tiled=True),
-        lax.all_gather(key_weight, ("wide", "narrow"), axis=0, tiled=True),
-        lax.all_gather(value_weight, ("wide", "narrow"), axis=0, tiled=True),
-        lax.all_gather(out_weight, ("wide", "narrow"), axis=0, tiled=True),
+        lax.all_gather(norm1_gain, AXES, axis=0, tiled=True),
+        lax.all_gather(query_weight, AXES, axis=0, tiled=True),
+        lax.all_gather(key_weight, AXES, axis=0, tiled=True),
+        lax.all_gather(value_weight, AXES, axis=0, tiled=True),
+        lax.all_gather(out_weight, AXES, axis=0, tiled=True),
     )
     input_rows = []
     gain_first = jnp.zeros((tokens.shape[2],), jnp.float32)
@@ -290,11 +293,11 @@
     value_total = outer_dot(first_rows, joined(grad_lists[2]))
     out_total = outer_dot(attended_rows, joined(grad_lists[3]))
     attend_sums = (
-        lax.psum_scatter(gain_first, ("wide", "narrow"), scatter_dimension=0, tiled=True),
-        lax.psum_scatter(query_total, ("wide", "narrow"), scatter_dimension=0, tiled=True),
-        lax.psum_scatter(key_total, ("wide", "narrow"), scatter_dimension=0, tiled=True),
-        lax.psum_scatter(value_total, ("wide", "narrow"), scatter_dimension=0, tiled=True),
-        lax.psum_scatter(out_total, ("wide", "narrow"), scatter_dimension=0, tiled=True),
+        lax.psum_scatter(gain_first, AXES, scatter_dimension=0, tiled=True),
+        lax.psum_scatter(query_total, AXES, scatter_dimension=0, tiled=True),
+        lax.psum_scatter(key_total, AXES, scatter_dimension=0, tiled=True),
+        lax.psum_scatter(value_total, AXES, scatter_dimension=0, tiled=True),
+        lax.psum_scatter(out_total, AXES, scatter_dimension=0, tiled=True),
     )
     layer_output = jnp.stack(layer_rows)
     input_grad = jnp.stack(input_rows)
@@ -326,12 +329,12 @@
 def enter_ring(left, right):
     barrier = pltpu.get_barrier_semaphore()
     for device in (left, right):
-        pl.semaphore_signal(barrier, inc=1, device_id={"wide": device}, device_id_type=MESH)
+        pl.semaphore_signal(barrier, inc=1, device_id={WIDE: device}, device_id_type=MESH)
     pl.semaphore_wait(barrier, 2)
 
 
 def gather_kernel(size, block_ref, full_ref, own_sem, send_sem, recv_sem):
-    place = ring_place(lax.axis_index("wide"), size)
+    place = ring_place(lax.axis_index(WIDE), size)
     left = ring_device((place + size - 1) % size, size)
     right = ring_device((place + 1) % size, size)
     half = block_ref.shape[0] // 2
@@ -346,12 +349,12 @@
             dst_ref=target,
             send_sem=send_sem.at[way, hop, part],
             recv_sem=recv_sem.at[way, hop, part],
-            device_id={"wide": right if way == 0 else left},
+            device_id={WIDE: right if way == 0 else left},
             device_id_type=MESH,
         )
 
     enter_ring(left, right)
-    own = pltpu.make_async_copy(block_ref, full_ref.at[lax.axis_index("wide")], own_sem)
+    own = pltpu.make_async_copy(block_ref, full_ref.at[lax.axis_index(WIDE)], own_sem)
     sent = {}
     for hop in range(hops):
         for part in range(2):
@@ -393,7 +396,7 @@
 
 
 def scatter_kernel(size, partial_ref, sum_ref, held, send_sem, recv_sem):
-    place = ring_place(lax.axis_index("wide"), size)
+    place = ring_place(lax.axis_index(WIDE), size)
     left = ring_device((place + size - 1) % size, size)
     right = ring_device((place + 1) % size, size)
     rows, width = sum_ref.shape
@@ -413,7 +416,7 @@
             dst_ref=held.at[(hop, *cut(way, part))],
             send_sem=send_sem.at[way, hop, part],
             recv_sem=recv_sem.at[way, hop, part],
-            device_id={"wide": right if way == 0 else left},
+            device_id={WIDE: right if way == 0 else left},
             device_id_type=MESH,
         )
 
@@ -457,19 +460,25 @@
     )(partial.astype(jnp.bfloat16).reshape(size, rows, width))
 
 
-def to_columns(weights, wide):
+def by_column(weights, wide):
     pieces = [w.reshape(w.shape[0], wide, w.shape[1] // wide) for w in weights]
-    block = jnp.swapaxes(jnp.concatenate(pieces, axis=2), 0, 1)
-    block = lax.all_to_all(block, "wide", split_axis=0, concat_axis=0, tiled=True)
-    full = lax.all_gather(block, "narrow", axis=1, tiled=True)
+    return jnp.swapaxes(jnp.concatenate(pieces, axis=2), 0, 1)
+
+
+def to_columns(block):
+    block = lax.all_to_all(block, WIDE, split_axis=0, concat_axis=0, tiled=True)
+    full = lax.all_gather(block, NARROW, axis=1, tiled=True)
     return full.reshape(-1, full.shape[2])
 
 
-def to_rows(columns, wide, narrow):
+def sum_blocks(columns, wide):
     rows, width = columns.shape
     block = columns.astype(jnp.bfloat16).reshape(wide, rows // wide, width)
-    block = lax.psum_scatter(block, "narrow", scatter_dimension=1, tiled=True)
-    return lax.all_to_all(block, "wide", split_axis=0, concat_axis=0, tiled=True)
+    return lax.psum_scatter(block, NARROW, scatter_dimension=1, tiled=True)
+
+
+def to_rows(block):
+    return lax.all_to_all(block, WIDE, split_axis=0, concat_axis=0, tiled=True)
 
 
 def own_rows(block, start, width):
@@ -478,12 +487,12 @@
 
 
 def gather_narrow(weight):
-    return lax.all_gather(weight, "narrow", axis=0, tiled=True)
+    return lax.all_gather(weight, NARROW, axis=0, tiled=True)
 
 
 def sum_narrow(partial):
     return lax.psum_scatter(
-        partial.astype(jnp.bfloat16), "narrow", scatter_dimension=0, tiled=True
+        partial.astype(jnp.bfloat16), NARROW, scatter_dimension=0, tiled=True
     ).astype(jnp.float32)
 
 
@@ -526,18 +535,33 @@
     row_mask = (position[None, :] < lengths).astype(jnp.float32).reshape(rows, 1)
 
     share = norm1_gain.shape[0]
-    gains = lax.all_gather(jnp.concatenate([norm1_gain, norm2_gain]), ("wide", "narrow"))
-    gains = gains.astype(jnp.float32)
+    gains = jnp.concatenate([norm1_gain, norm2_gain])[None]
+    gains = lax.all_to_all(
+        jnp.broadcast_to(gains, (wide * narrow, 2 * share)),
+        AXES,
+        split_axis=0,
+        concat_axis=0,
+        tiled=True,
+    ).astype(jnp.float32)
     gains = (gains[:, :share].reshape(width), gains[:, share:].reshape(width))
-    attend_columns = to_columns((query_weight, key_weight, value_weight), wide)
+    attend_columns = to_columns(by_column((query_weight, key_weight, value_weight), wide))
 
     floats = tokens.reshape(rows, width).astype(jnp.float32)
     inverse_one = lax.rsqrt(jnp.mean(floats * floats, axis=-1, keepdims=True) + epsilon)
     normed_one = floats * inverse_one
-    floats_all = gather_rows(tokens.reshape(rows, width), wide).astype(jnp.float32)
+    upstream = cotangent.reshape(rows, width).astype(jnp.float32) * row_mask
+    upstream_all = gather_rows(upstream.astype(jnp.bfloat16), wide)
+    feed_block, tokens_all, gains = lax.optimization_barrier(
+        (
+            by_column((gate_weight, up_weight), wide),
+            gather_rows(tokens.reshape(rows, width), wide),
+            gains,
+        )
+    )
+    floats_all = tokens_all.astype(jnp.float32)
     inverse_all = lax.rsqrt(jnp.mean(floats_all * floats_all, axis=-1, keepdims=True) + epsilon)
     first_all = (floats_all * inverse_all * gains[0]).astype(jnp.bfloat16)
-    feed_columns = to_columns((gate_weight, up_weight), wide)
+    feed_columns = to_columns(feed_block)
     out_rows = gather_narrow(out_weight)
     down_rows = gather_narrow(down_weight)
 
@@ -563,21 +587,18 @@
         .astype(jnp.bfloat16)
         .reshape(sequences * length, head_width)
     )
-    middle = floats + scatter_rows(mixed_dot(attended, out_rows), wide)
+    out_term = mixed_dot(attended, out_rows).astype(jnp.bfloat16)
+    middle = floats + scatter_rows(out_term, wide)
 
     inverse_two = lax.rsqrt(jnp.mean(middle * middle, axis=-1, keepdims=True) + epsilon)
     normed_two = middle * inverse_two
     second_all = gather_rows((normed_two * gains[1]).astype(jnp.bfloat16), wide)
-    upstream = cotangent.reshape(rows, width).astype(jnp.float32) * row_mask
-    upstream_all = gather_rows(upstream.astype(jnp.bfloat16), wide)
 
     front = mixed_dot(second_all, feed_columns)
     gate_value = front[:, :hidden_width]
     up_value = front[:, hidden_width:]
     gate_sig = jax.nn.sigmoid(gate_value)
     hidden = (gate_value * gate_sig * up_value).astype(jnp.bfloat16)
-    feed_out = scatter_rows(mixed_dot(hidden, down_rows), wide)
-    layer_output = ((middle + feed_out) * row_mask).astype(jnp.bfloat16)
 
     grad_hidden = back_dot(upstream_all, down_rows)
     grad_gate = (
@@ -585,9 +606,20 @@
     ).astype(jnp.bfloat16)
     grad_up = (grad_hidden * gate_value * gate_sig).astype(jnp.bfloat16)
     grad_front = jnp.concatenate([grad_gate, grad_up], axis=1)
-    grad_second = scatter_rows(back_dot(grad_front, feed_columns), wide)
-    down_grad = sum_narrow(outer_dot(hidden, upstream_all))
-    front_block = to_rows(outer_dot(second_all, grad_front), wide, narrow)
+    down_term, front_term, feed_term, second_term = lax.optimization_barrier(
+        (
+            outer_dot(hidden, upstream_all).astype(jnp.bfloat16),
+            outer_dot(second_all, grad_front).astype(jnp.bfloat16),
+            mixed_dot(hidden, down_rows).astype(jnp.bfloat16),
+            back_dot(grad_front, feed_columns).astype(jnp.bfloat16),
+        )
+    )
+    down_grad = sum_narrow(down_term)
+    front_block = sum_blocks(front_term, wide)
+    grad_second = scatter_rows(second_term, wide)
+    feed_out = scatter_rows(feed_term, wide)
+    front_block = to_rows(front_block)
+    layer_output = ((middle + feed_out) * row_mask).astype(jnp.bfloat16)
     gate_grad = own_rows(front_block, 0, hidden_width)
     up_grad = own_rows(front_block, hidden_width, hidden_width)
 
@@ -595,8 +627,14 @@
     grad_middle = upstream + norm_back(grad_second * gains[1], normed_two, inverse_two)
     middle_all = gather_rows(grad_middle.astype(jnp.bfloat16), wide)
 
-    grad_attended = back_dot(middle_all, out_rows).astype(jnp.bfloat16).reshape(by_head)
-    out_grad = sum_narrow(outer_dot(attended, middle_all))
+    out_term, grad_attended = lax.optimization_barrier(
+        (
+            outer_dot(attended, middle_all).astype(jnp.bfloat16),
+            back_dot(middle_all, out_rows).astype(jnp.bfloat16),
+        )
+    )
+    grad_attended = grad_attended.reshape(by_head)
+    out_grad = sum_narrow(out_term)
     grad_weights = jnp.einsum(
         "sqhd,skhd->shqk", grad_attended, values_all, preferred_element_type=jnp.float32
     )
@@ -622,13 +660,20 @@
         ],
         axis=1,
     )
-    grad_first = scatter_rows(back_dot(grad_joint, attend_columns), wide)
-    attend_block = to_rows(outer_dot(first_all, grad_joint), wide, narrow)
+    attend_term, first_term = lax.optimization_barrier(
+        (
+            outer_dot(first_all, grad_joint).astype(jnp.bfloat16),
+            back_dot(grad_joint, attend_columns).astype(jnp.bfloat16),
+        )
+    )
+    attend_block = sum_blocks(attend_term, wide)
+    grad_first = scatter_rows(first_term, wide)
+    attend_block = to_rows(attend_block)
     gain_one = jnp.sum(grad_first * normed_one, axis=0)
     input_grad = grad_middle + norm_back(grad_first * gains[0], normed_one, inverse_one)
     gain_terms = jnp.concatenate([gain_one.reshape(-1, share), gain_two.reshape(-1, share)], axis=1)
     gain_terms = lax.all_to_all(
-        gain_terms, ("wide", "narrow"), split_axis=0, concat_axis=0, tiled=True
+        gain_terms, AXES, split_axis=0, concat_axis=0, tiled=True
     )
     gain_sums = jnp.sum(gain_terms, axis=0)
     return (
@@ -654,31 +699,31 @@
 
 def solution(mesh):
     in_specs = (
-        P(None, ("wide", "narrow"), None),
-        P(None, ("wide", "narrow")),
-        P(None, ("wide", "narrow"), None),
-        P(("wide", "narrow")),
-        P(("wide", "narrow"), None),
-        P(("wide", "narrow"), None),
-        P(("wide", "narrow"), None),
-        P(("wide", "narrow"), None),
-        P(("wide", "narrow")),
-        P(("wide", "narrow"), None),
-        P(("wide", "narrow"), None),
-        P(("wide", "narrow"), None),
+        P(None, AXES, None),
+        P(None, AXES),
+        P(None, AXES, None),
+        P(AXES),
+        P(AXES, None),
+        P(AXES, None),
+        P(AXES, None),
+        P(AXES, None),
+        P(AXES),
+        P(AXES, None),
+        P(AXES, None),
+        P(AXES, None),
     )
     out_specs = (
-        P(None, ("wide", "narrow"), None),
-        P(None, ("wide", "narrow"), None),
-        P(("wide", "narrow")),
-        P(("wide", "narrow"), None),
-        P(("wide", "narrow"), None),
-        P(("wide", "narrow"), None),
-        P(("wide", "narrow"), None),
-        P(("wide", "narrow")),
-        P(("wide", "narrow"), None),
-        P(("wide", "narrow"), None),
-        P(("wide", "narrow"), None),
-    )
-    body = functools.partial(local, mesh.shape["wide"], mesh.shape["narrow"])
+        P(None, AXES, None),
+        P(None, AXES, None),
+        P(AXES),
+        P(AXES, None),
+        P(AXES, None),
+        P(AXES, None),
+        P(AXES, None),
+        P(AXES),
+        P(AXES, None),
+        P(AXES, None),
+        P(AXES, None),
+    )
+    body = functools.partial(local, mesh.shape[WIDE], mesh.shape[NARROW])
     return jax.shard_map(body, mesh=mesh, in_specs=in_specs, out_specs=out_specs, check_vma=False)

time: 760 us -> 753 us (level)
  blocking collectives: 101 us -> 62.5 us
  waiting for transfers between devices: 110 us -> 145 us
    all_gather x1 -> x0, blocking collectives: 40.2 us -> none  [split_plan(): lax.all_gather(jnp.concatenate([norm1_gain, norm2_gain]), ('wide', 'narro...]
    reduce_scatter x4, waiting for transfers between devices: 61.8 us -> 95.5 us  [the longest x2 63.1 us: sum_narrow(): lax.psum_scatter(partial.astype(jnp.bfloat16), NARROW, scatter_dimension=...]
    all_to_all x2 -> x3, waiting for transfers between devices: 47 us -> 46.4 us  [the longest x1 46.4 us: to_columns(): block = lax.all_to_all(block, WIDE, split_axis=0, concat_axis=0, tiled=True)]
  transfers between devices with their start and end apart: 10 -> 11, of which waited for: 3 -> 4; matrix products, arithmetic and copies ran while one was open for 15% -> 9% of each run, Pallas kernels for 29% -> 29%
where the time goes in v3:
time: 753 us; the launch traced here: 747 us
  Pallas kernels  341 us (45%)
  waiting for transfers between devices  145 us (19%)
  matrix products  103 us (14%)
  blocking collectives  62.5 us (8%)
  local copies, waits for them, and re-layouts  43.8 us (6%)
  other arithmetic  24.3 us (3%)
  between operations  15.1 us (2%)
  starting transfers between devices  13.4 us (2%)
    pallas_call x4, Pallas kernels, scatter_rows(): pl.pallas_call(functools.partial(scatter_kernel, size), out_shape=jax.Sha...  171 us
    pallas_call x4, Pallas kernels, gather_rows(): pl.pallas_call(functools.partial(gather_kernel, size), out_shape=jax.Shap...  170 us
    reduce_scatter x2, waiting for transfers between devices, sum_narrow(): lax.psum_scatter(partial.astype(jnp.bfloat16), NARROW, scatter_dimension=...  63.1 us
    all_to_all x1, waiting for transfers between devices, to_columns(): block = lax.all_to_all(block, WIDE, split_axis=0, concat_axis=0, tiled=True)  46.4 us
    dot_general x4, matrix products, back_dot(): lax.dot_general(left, right, (((1,), (1,)), ((), ())), preferred_element_...  36.2 us
    dot_general x4, matrix products, mixed_dot(): return jnp.dot(left, right, preferred_element_type=jnp.float32)  32.6 us
    reduce_scatter x2, waiting for transfers between devices, sum_blocks(): return lax.psum_scatter(block, NARROW, scatter_dimension=1, tiled=True)  32.4 us
    dot_general x4, matrix products, outer_dot(): lax.dot_general(left, right, (((0,), (0,)), ((), ())), preferred_element_...  31 us
  transfers between devices with their start and end apart: 11, of which 4 were waited for; matrix products, arithmetic and copies ran while one was open for 9% of the time, Pallas kernels for 29%

profile of v3, /device:TPU:0, one launch (start us, length us, event | category | flops | bytes accessed | tf_op | source)
XLA Modules:
  0.0 747.4 jit_solution(6294768199998343856)
XLA Ops:
  7.2 1.0 copy.125
  8.3 1.1 copy.126
  9.4 1.0 copy.127
  10.6 27.4 %all_to_all.35 = bf16[8,64,768]{2,1,0:T(8,128)(2,1)S(1)} all-to-all(bf16[8,64,768]{2,1,0:T(8,128)(2,1)S(1)} %copy.84), channel_id=1, replica_groups=mesh['wide'=8,'narrow'=4] {'wide'}, dimensions={0} | all-to-all | bytes 1572864 | tf_op jit(solution)/shard_map/all_to_all | solution.py:469
  37.9 1.3 copy.85
  40.0 3.6 all-to-all-start
  45.1 46.7 %gather_rows.4 = bf16[8,128,2048]{2,1,0:T(8,128)(2,1)} custom-call(bf16[128,2048]{1,0:T(8,128)(2,1)} %bitcast.113), custom_call_target="tpu_custom_call" | custom-call | bytes 150000000 | tf_op jit(solution)/shard_map/gather_rows/pallas_call | solution.py:381
  92.0 2.5 copy.93
  94.5 3.7 all-to-all-start.2
  98.3 0.7 all-gather.7.cloned.1.call-update
  99.0 46.4 %all-to-all-done.2 = bf16[8,64,2048]{2,1,0:T(8,128)(2,1)S(1)} async-done(((bf16[8,64,2048]{2,1,0:T(8,128)(2,1)}), bf16[8,64,2048]{2,1,0:T(8,128)(2,1)S(1)}, u32[]{:S(2)}, u32[]{:S(2)}) %all-to-all-start.2) | async-done | bytes 2097184 | tf_op jit(solution)/shard_map/all_to_all | solution.py:469
  145.4 2.5 copy.94
  149.2 0.9 fusion.27.block_ref
  150.2 44.5 %gather_rows.6 = bf16[8,128,2048]{2,1,0:T(8,128)(2,1)} custom-call(bf16[128,2048]{1,0:T(8,128)(2,1)} %fusion.27.block_ref), custom_call_target="tpu_custom_call" | custom-call | bytes 150000000 | tf_op jit(solution)/shard_map/gather_rows/pallas_call | solution.py:381
  194.7 3.1 fusion
  197.8 2.7 copy.86
  201.0 3.5 fusion.19
  204.5 0.8 slice.128
  206.6 1.2 convert_element_type.223
  207.7 2.4 fusion.46
  210.8 0.8 fusion.11
  211.7 1.0 copy-done.5
  213.6 0.8 copy-done.10
  214.4 5.1 convolution_convert_fusion.2
  219.5 45.3 %scatter_rows.4 = f32[128,2048]{1,0:T(8,128)} custom-call(bf16[8,128,2048]{2,1,0:T(8,128)(2,1)} %bitcast.109), custom_call_target="tpu_custom_call" | custom-call | bytes 150000000 | tf_op jit(solution)/shard_map/scatter_rows/pallas_call | solution.py:447
  264.8 1.4 multiply_reduce_fusion.3
  266.3 1.0 multiply_convert_fusion.4.block_ref
  267.2 42.9 %gather_rows.5 = bf16[8,128,2048]{2,1,0:T(8,128)(2,1)} custom-call(bf16[128,2048]{1,0:T(8,128)(2,1)} %multiply_convert_fusion.4.block_ref), custom_call_target="tpu_custom_call" | custom-call | bytes 150000000 | tf_op jit(solution)/shard_map/gather_rows/pallas_call | solution.py:381
  310.1 11.3 %copy.95 = bf16[8,256,2048]{2,1,0:T(8,128)(2,1)} copy(bf16[8,256,2048]{2,0,1:T(8,128)(2,1)} %all-gather.9.cloned.1.call-done) | data formatting | bytes 16777216 | tf_op jit(solution)/shard_map/all_gather | solution.py:470
  321.4 14.7 %fusion.50 = f32[1024,2048]{1,0:T(8,128)} fusion(bf16[1024,2048]{1,0:T(8,128)(2,1)} %bitcast.122, bf16[2048,2048]{1,0:T(8,128)(2,1)} %bitcast.115), kind=kOutput, calls=%fused_computation.115 | convolution fusion | flops 8589934592 | bytes 20971520 | tf_op jit(solution)/shard_map/dot_general | solution.py:24
  336.1 14.0 %multiply_convert_fusion.1 = (bf16[1024,1024]{1,0:T(8,128)(2,1)}, bf16[1024,1024]{1,0:T(8,128)(2,1)}, bf16[1024,1024]{1,0:T(8,128)(2,1)S(1)}) fusion(f32[1024,2048]{1,0:T(8,128)} %fusion.50, bf16[1024,2048]{1,0:T(8,128)(2,1)} %bitcast.120, bf16[1024,2048]{1,0:T(8,128)(2,1)} %all-gather.11.cloned.1.call-done), kind=kOutput, calls=%fused_computation.8 | convolution fusion | flops 4311744512 | bytes 23068672 | tf_op jit(solution)/shard_map/dot_general | solution.py:34
  350.2 12.7 %convolution_convert_fusion.1 = bf16[1024,2048]{1,0:T(8,128)(2,1)} fusion(bf16[2048,2048]{1,0:T(8,128)(2,1)S(1)} %bitcast.116, bf16[1024,1024]{1,0:T(8,128)(2,1)} %get-tuple-element.44, bf16[1024,1024]{1,0:T(8,128)(2,1)} %get-tuple-element.43), kind=kOutput, calls=%fused_computation.11 | convolution fusion | flops 8600420352 | bytes 16777216 | tf_op jit(solution)/shard_map/dot_general | solution.py:34
  362.8 14.7 %convolution_convert_fusion = bf16[2048,2048]{1,0:T(8,128)(2,1)} fusion(bf16[1024,2048]{1,0:T(8,128)(2,1)} %bitcast.123, bf16[1024,1024]{1,0:T(8,128)(2,1)} %get-tuple-element.44, bf16[1024,1024]{1,0:T(8,128)(2,1)} %get-tuple-element.43), kind=kOutput, calls=%fused_computation.5 | convolution fusion | flops 8602517504 | bytes 16777216 | tf_op jit(solution)/shard_map/dot_general | solution.py:28
  377.5 6.3 convolution_convert_fusion.5
  383.8 9.3 %convolution_convert_fusion.4 = bf16[1024,2048]{1,0:T(8,128)(2,1)} fusion(bf16[1024,1024]{1,0:T(8,128)(2,1)} %copy-done.29, bf16[1024,2048]{1,0:T(8,128)(2,1)} %all-gather.11.cloned.1.call-done), kind=kOutput, calls=%fused_computation.14 | convolution fusion | flops 4297064448 | bytes 10485760 | tf_op jit(solution)/shard_map/dot_general | solution.py:24
  393.1 43.4 %scatter_rows.6 = f32[128,2048]{1,0:T(8,128)} custom-call(bf16[8,128,2048]{2,1,0:T(8,128)(2,1)} %bitcast.118), custom_call_target="tpu_custom_call" | custom-call | bytes 150000000 | tf_op jit(solution)/shard_map/scatter_rows/pallas_call | solution.py:447
  436.5 1.7 multiply_reduce_fusion
  438.2 43.0 %scatter_rows.5 = f32[128,2048]{1,0:T(8,128)} custom-call(bf16[8,128,2048]{2,1,0:T(8,128)(2,1)} %bitcast.119), custom_call_target="tpu_custom_call" | custom-call | bytes 150000000 | tf_op jit(solution)/shard_map/scatter_rows/pallas_call | solution.py:447
  481.2 3.2 fusion.43
  484.3 35.8 %gather_rows.7 = bf16[8,128,2048]{2,1,0:T(8,128)(2,1)} custom-call(bf16[128,2048]{1,0:T(8,128)(2,1)} %get-tuple-element.39.block_ref), custom_call_target="tpu_custom_call" | custom-call | bytes 150000000 | tf_op jit(solution)/shard_map/gather_rows/pallas_call | solution.py:381
  520.2 4.5 convolution_convert_fusion.7
  524.7 4.4 convolution_convert_fusion.10
  529.0 1.2 reshape.332
  533.0 1.0 subtract_convert_fusion
  536.0 5.1 convolution_convert_fusion.3
  541.1 5.5 convolution_convert_fusion.6
  547.3 0.7 reduce-scatter.7.cloned.1.call-update
  549.0 39.1 %scatter_rows.7 = f32[128,2048]{1,0:T(8,128)} custom-call(bf16[8,128,2048]{2,1,0:T(8,128)(2,1)} %bitcast.117), custom_call_target="tpu_custom_call" | custom-call | bytes 150000000 | tf_op jit(solution)/shard_map/scatter_rows/pallas_call | solution.py:447
  588.1 1.7 fusion.25
  590.1 11.2 %all_to_all.36 = f32[32,1,128]{2,1,0:T(1,128)S(1)} all-to-all(f32[32,1,128]{2,1,0:T(1,128)S(1)} %bitcast.152), channel_id=1, replica_groups=mesh['wide'=8,'narrow'=4] {'wide','narrow'}, dimensions={0} | all-to-all | bytes 32768 | tf_op jit(solution)/shard_map/all_to_all | solution.py:675
  601.3 23.9 %all_to_all.37 = bf16[8,64,768]{2,1,0:T(8,128)(2,1)S(1)} all-to-all(bf16[8,64,768]{2,1,0:T(8,128)(2,1)} %reduce-scatter.5.cloned.1.call-done), channel_id=1, replica_groups=mesh['wide'=8,'narrow'=4] {'wide'}, dimensions={0} | all-to-all | bytes 1572864 | tf_op jit(solution)/shard_map/all_to_all | solution.py:481
  625.2 32.4 %reduce-scatter.9.cloned.1.call-done = bf16[8,64,2048]{2,1,0:T(8,128)(2,1)} async-done(((bf16[8,256,2048]{2,1,0:T(8,128)(2,1)}), bf16[8,64,2048]{2,1,0:T(8,128)(2,1)}) %reduce-scatter.9.cloned.1.call-update) | async-done | bytes 2097168 | tf_op jit(solution)/shard_map/reduce_scatter | solution.py:477
  657.6 5.5 all-to-all-start.5
  663.2 1.3 fusion.24
  665.1 20.4 %reduce-scatter.7.cloned.1.call-done = bf16[64,2048]{1,0:T(8,128)(2,1)} async-done(((bf16[256,2048]{1,0:T(8,128)(2,1)}), bf16[64,2048]{1,0:T(8,128)(2,1)}) %reduce-scatter.7.cloned.1.call-update) | async-done | bytes 262160 | tf_op jit(solution)/shard_map/reduce_scatter | solution.py:494
  685.6 1.8 convert_element_type.264
  687.5 0.8 copy.118
  688.4 0.8 copy.119
  689.2 0.8 copy.120
  690.1 42.6 %reduce-scatter.11.cloned.1.call-done = bf16[256,2048]{1,0:T(8,128)(2,1)} async-done(((bf16[1024,2048]{1,0:T(8,128)(2,1)}), bf16[256,2048]{1,0:T(8,128)(2,1)}) %reduce-scatter.11.cloned.1.call-update) | async-done | bytes 1048592 | tf_op jit(solution)/shard_map/reduce_scatter | solution.py:494
  732.7 2.8 convert_element_type.271
  735.5 2.0 convert_bitcast_fusion
  737.5 1.5 copy.121
  739.0 1.5 copy.122
  (127 shorter events, 14.6 us)
Async XLA Ops:
  7.2 190.6 %all-gather.5.cloned.1.call-start = ((), (), s32[]{:S(2)}) async-start(), calls=%async_computation.10 | async-start | bytes 3932160 | tf_op jit(solution)/shard_map/all_gather | solution.py:470
  8.2 31.1 %copy-start.26 = (bf16[64]{0:T(256)(128)(2,1)S(1)}, bf16[64]{0:T(256)(128)(2,1)}, u32[]{:S(2)}) copy-start(bf16[64]{0:T(256)(128)(2,1)} %param.20) | copy-start | bytes 388
  8.2 31.1 %copy-start.27 = (bf16[64]{0:T(256)(128)(2,1)S(1)}, bf16[64]{0:T(256)(128)(2,1)}, u32[]{:S(2)}) copy-start(bf16[64]{0:T(256)(128)(2,1)} %param.15) | copy-start | bytes 388
  8.3 35.4 %copy-start.23 = (bf16[64,8192]{1,0:T(8,128)(2,1)S(1)}, bf16[64,8192]{1,0:T(8,128)(2,1)}, u32[]{:S(2)}) copy-start(bf16[64,8192]{1,0:T(8,128)(2,1)} %param.21) | copy-start | bytes 3145732
  10.4 33.8 %copy-start.24 = (bf16[64,8192]{1,0:T(8,128)(2,1)S(1)}, bf16[64,8192]{1,0:T(8,128)(2,1)}, u32[]{:S(2)}) copy-start(bf16[64,8192]{1,0:T(8,128)(2,1)} %param.22) | copy-start | bytes 3145732
  40.0 51.8 %all-to-all-start = ((bf16[32,1,128]{2,1,0:T(2,128)(2,1)}), bf16[32,1,128]{2,1,0:T(2,128)(2,1)S(1)}, u32[]{:S(2)}, u32[]{:S(2)}) async-start(bf16[32,1,128]{2,1,0:T(2,128)(2,1)} %broadcast_in_dim.2), calls=%async_computation | async-start | bytes 32768 | tf_op jit(solution)/shard_map/all_to_all | solution.py:539
  94.5 50.9 %all-to-all-start.2 = ((bf16[8,64,2048]{2,1,0:T(8,128)(2,1)}), bf16[8,64,2048]{2,1,0:T(8,128)(2,1)S(1)}, u32[]{:S(2)}, u32[]{:S(2)}) async-start(bf16[8,64,2048]{2,1,0:T(8,128)(2,1)} %copy.93), calls=%async_computation.2 | async-start | bytes 4194304 | tf_op jit(solution)/shard_map/all_to_all | solution.py:469
  98.2 50.7 %copy-start.28 = (s32[2,1]{0,1:T(1,128)S(1)}, s32[2,1]{0,1:T(1,128)}, u32[]{:S(2)}) copy-start(s32[2,1]{0,1:T(1,128)} %param.13) | copy-start | bytes 28
  98.2 51.0 %copy-start.22 = (bf16[2,64,2048]{2,1,0:T(8,128)(2,1)S(1)}, bf16[2,64,2048]{2,1,0:T(8,128)(2,1)}, u32[]{:S(2)}) copy-start(bf16[2,64,2048]{2,1,0:T(8,128)(2,1)} %param.14) | copy-start | bytes 1572868
  98.2 115.4 %all-gather.7.cloned.1.call-start = ((), (), s32[]{:S(2)}) async-start(), calls=%async_computation.11 | async-start | bytes 1310720 | tf_op jit(solution)/shard_map/all_gather | solution.py:490
  99.0 211.1 %all-gather.9.cloned.1.call-start = ((), (), s32[]{:S(2)}) async-start(), calls=%async_computation.12 | async-start | bytes 10485760 | tf_op jit(solution)/shard_map/all_gather | solution.py:470
  147.9 188.2 %all-gather.11.cloned.1.call-start = ((), (), s32[]{:S(2)}) async-start(), calls=%async_computation.13 | async-start | bytes 5242880 | tf_op jit(solution)/shard_map/all_gather | solution.py:490
  148.5 452.8 %reduce-scatter.5.cloned.1.call-start = ((), (), s32[]{:S(2)}) async-start(), calls=%async_computation.14 | async-start | bytes 3932160 | tf_op jit(solution)/shard_map/reduce_scatter | solution.py:477
  197.8 3.2 copy-start
  200.5 4.0 copy-start.12
  210.8 2.2 copy-start.14
  210.8 2.2 copy-start.16
  210.8 2.2 copy-start.18
  210.8 2.2 copy-start.20
  211.7 1.0 copy-start.5
  213.5 0.8 copy-start.10
  219.5 45.3 %copy-start.2 = (bf16[2,64,2048]{2,1,0:T(8,128)(2,1)S(1)}, bf16[2,64,2048]{2,1,0:T(8,128)(2,1)}, u32[]{:S(2)}) copy-start(bf16[2,64,2048]{2,1,0:T(8,128)(2,1)} %param.12) | copy-start | bytes 1572868
  336.1 14.0 %copy-start.7 = (bf16[8,256,2048]{2,1,0:T(8,128)(2,1)S(1)}, bf16[8,256,2048]{2,1,0:T(8,128)(2,1)}, u32[]{:S(2)}) copy-start(bf16[8,256,2048]{2,1,0:T(8,128)(2,1)} %copy.95) | copy-start | bytes 25165828
  350.1 27.3 %copy-start.29 = (bf16[1024,1024]{1,0:T(8,128)(2,1)}, bf16[1024,1024]{1,0:T(8,128)(2,1)S(1)}, u32[]{:S(2)}) copy-start(bf16[1024,1024]{1,0:T(8,128)(2,1)S(1)} %get-tuple-element.45) | copy-start | bytes 6291460
  362.8 14.7 %copy-start.8 = (bf16[8,128,2048]{2,1,0:T(8,128)(2,1)S(1)}, bf16[8,128,2048]{2,1,0:T(8,128)(2,1)}, u32[]{:S(2)}) copy-start(bf16[8,128,2048]{2,1,0:T(8,128)(2,1)} %gather_rows.6) | copy-start | bytes 12582916
  436.5 44.7 %copy-start.3 = (f32[128,2048]{1,0:T(8,128)S(1)}, f32[128,2048]{1,0:T(8,128)}, u32[]{:S(2)}) copy-start(f32[128,2048]{1,0:T(8,128)} %scatter_rows.6) | copy-start | bytes 3145732
  484.3 35.8 %copy-start.11 = (bf16[16,64,2,128]{3,2,1,0:T(2,128)(2,1)S(1)}, bf16[16,64,2,128]{3,2,1,0:T(2,128)(2,1)}, u32[]{:S(2)}) copy-start(bf16[16,64,2,128]{3,2,1,0:T(2,128)(2,1)} %copy-done.10) | copy-start | bytes 1572868
  520.1 4.5 copy-start.25
  524.7 5.6 copy-start.6
  529.0 2.9 copy-start.15
  530.3 1.0 copy-start.19
  530.3 1.2 copy-start.21
  530.3 1.6 copy-start.17
  534.0 2.0 copy-start.13
  536.0 5.1 copy-start.1
  546.6 111.0 %reduce-scatter.9.cloned.1.call-start = ((), (), s32[]{:S(2)}) async-start(), calls=%async_computation.16 | async-start | bytes 10485760 | tf_op jit(solution)/shard_map/reduce_scatter | solution.py:477
  547.2 138.4 %reduce-scatter.7.cloned.1.call-start = ((), (), s32[]{:S(2)}) async-start(), calls=%async_computation.15 | async-start | bytes 1310720 | tf_op jit(solution)/shard_map/reduce_scatter | solution.py:494
  548.0 184.7 %reduce-scatter.11.cloned.1.call-start = ((), (), s32[]{:S(2)}) async-start(), calls=%async_computation.17 | async-start | bytes 5242880 | tf_op jit(solution)/shard_map/reduce_scatter | solution.py:494
  588.1 75.0 %copy-start.4 = (f32[128,2048]{1,0:T(8,128)S(1)}, f32[128,2048]{1,0:T(8,128)}, u32[]{:S(2)}) copy-start(f32[128,2048]{1,0:T(8,128)} %scatter_rows.7) | copy-start | bytes 3145732
  588.1 75.0 %copy-start.9 = (f32[128,2048]{1,0:T(8,128)S(1)}, f32[128,2048]{1,0:T(8,128)}, u32[]{:S(2)}) copy-start(f32[128,2048]{1,0:T(8,128)} %get-tuple-element.40) | copy-start | bytes 3145732
  657.6 77.9 %all-to-all-start.5 = ((bf16[8,64,2048]{2,1,0:T(8,128)(2,1)}), bf16[8,64,2048]{2,1,0:T(8,128)(2,1)}, u32[]{:S(2)}, u32[]{:S(2)}) async-start(bf16[8,64,2048]{2,1,0:T(8,128)(2,1)} %reduce-scatter.9.cloned.1.call-done), calls=%async_computation.8 | async-start | bytes 4194304 | tf_op jit(solution)/shard_map/all_to_all | solution.py:481
Sparse Core Ops, SparseCore 0:
  39.4 27.6 all-gather.4
  100.6 18.0 all-gather.6
  148.0 57.2 all-gather.8
  206.8 34.4 all-gather.10
  546.8 37.0 reduce-scatter.4
  586.3 71.2 reduce-scatter.8
  660.7 24.8 reduce-scatter.6
  688.1 44.5 reduce-scatter.10

commit v4 on v3

--- a/solution.py
+++ b/solution.py
@@ -395,6 +395,154 @@
     return full.reshape(size * rows, width)
 
 
+def feed_kernel(
+    size,
+    block_ref,
+    second_ref,
+    feed_ref,
+    down_ref,
+    full_ref,
+    front_ref,
+    hidden_ref,
+    whole_ref,
+    landed,
+    feed,
+    down,
+    load_sem,
+    keep_sem,
+    store_sem,
+    send_sem,
+    recv_sem,
+):
+    me = lax.axis_index(WIDE)
+    place = ring_place(me, size)
+    left = ring_device((place + size - 1) % size, size)
+    right = ring_device((place + 1) % size, size)
+    half = block_ref.shape[0] // 2
+    hops = size // 2
+    tile = front_ref.shape[1] // (2 * hops)
+    tall = second_ref.shape[0] // 2
+
+    def origin(way, hop):
+        return ring_device((place + size - hop if way == 0 else place + hop) % size, size)
+
+    def copy(way, hop, part):
+        target = landed.at[origin(way, hop), pl.ds(part * half, half)]
+        return pltpu.make_async_remote_copy(
+            src_ref=block_ref.at[pl.ds(part * half, half)] if hop == 0 else target,
+            dst_ref=target,
+            send_sem=send_sem.at[way, hop, part],
+            recv_sem=recv_sem.at[way, hop, part],
+            device_id={WIDE: right if way == 0 else left},
+            device_id_type=MESH,
+        )
+
+    loads = [
+        pltpu.make_async_copy(feed_ref.at[share], feed.at[:, share], load_sem.at[share])
+        for share in range(feed_ref.shape[0])
+    ]
+    loads.append(pltpu.make_async_copy(down_ref, down, load_sem.at[feed_ref.shape[0]]))
+    for load in loads:
+        load.start()
+    enter_ring(left, right)
+    stores = []
+
+    def front_tile(index):
+        columns = pl.ds(index * tile, tile)
+        weight = feed[:, :, :, columns].reshape(second_ref.shape[1], tile)
+
+        def step(part, carry):
+            rows = pl.ds(pl.multiple_of(part * tall, tall), tall)
+            front_ref[rows, columns] = mixed_dot(second_ref[rows, :], weight)
+            return carry
+
+        lax.fori_loop(0, 2, step, 0)
+
+    def use(source, owner, slot):
+        store = pltpu.make_async_copy(source, full_ref.at[owner], store_sem.at[slot])
+        store.start()
+        stores.append(store)
+        hidden_ref[owner] = back_dot(source[...], down[...])
+
+    sent = {}
+    for hop in range(hops):
+        for part in range(2):
+            for way in range(2):
+                if hop == hops - 1 and part != way:
+                    continue
+                if hop:
+                    sent[way, hop - 1, part].wait_recv()
+                sent[way, hop, part] = copy(way, hop, part)
+                sent[way, hop, part].start()
+            if hop == 0 and part == 0:
+                for load in loads:
+                    load.wait()
+                keep = pltpu.make_async_copy(feed, whole_ref, keep_sem)
+                keep.start()
+            front_tile(2 * hop + part)
+        if hop == 0:
+            use(block_ref, me, 0)
+        for way in range(2):
+            if hop == hops - 1:
+                sent[way, hop - 1, 1 - way].wait_recv()
+            if hop:
+                use(landed.at[origin(way, hop)], origin(way, hop), 2 * hop - 1 + way)
+    for way in range(2):
+        sent[way, hops - 1, way].wait_recv()
+    use(landed.at[origin(0, hops)], origin(0, hops), size - 1)
+    for transfer in sent.values():
+        transfer.wait_send()
+    for store in stores:
+        store.wait()
+    keep.wait()
+
+
+def gather_and_feed(block, second_all, feed_shares, down_rows, size):
+    rows, width = block.shape
+    narrow, _, share, columns = feed_shares.shape
+    hidden = down_rows.shape[0]
+    hops = size // 2
+    full, front, grad_hidden, feed = pl.pallas_call(
+        functools.partial(feed_kernel, size),
+        out_shape=(
+            jax.ShapeDtypeStruct((size, rows, width), block.dtype),
+            jax.ShapeDtypeStruct((size * rows, columns), jnp.float32),
+            jax.ShapeDtypeStruct((size, rows, hidden), jnp.float32),
+            jax.ShapeDtypeStruct((size, narrow, share, columns), block.dtype),
+        ),
+        in_specs=[
+            pl.BlockSpec(memory_space=pltpu.VMEM),
+            pl.BlockSpec(memory_space=pltpu.VMEM),
+            pl.BlockSpec(memory_space=pl.ANY),
+            pl.BlockSpec(memory_space=pl.ANY),
+        ],
+        out_specs=(
+            pl.BlockSpec(memory_space=pl.ANY),
+            pl.BlockSpec(memory_space=pltpu.VMEM),
+            pl.BlockSpec(memory_space=pltpu.VMEM),
+            pl.BlockSpec(memory_space=pl.ANY),
+        ),
+        scratch_shapes=[
+            pltpu.VMEM((size, rows, width), block.dtype),
+            pltpu.VMEM((size, narrow, share, columns), block.dtype),
+            pltpu.VMEM((hidden, width), block.dtype),
+            pltpu.SemaphoreType.DMA((narrow + 1,)),
+            pltpu.SemaphoreType.DMA,
+            pltpu.SemaphoreType.DMA((size,)),
+            pltpu.SemaphoreType.DMA((2, hops, 2)),
+            pltpu.SemaphoreType.DMA((2, hops, 2)),
+        ],
+        compiler_params=pltpu.CompilerParams(collective_id=2, has_side_effects=True),
+        cost_estimate=RING_COST,
+    )(block, second_all, feed_shares, down_rows)
+    return (
+        full.reshape(size * rows, width),
+        front,
+        grad_hidden.reshape(size * rows, hidden),
+        feed.reshape(-1, columns),
+    )
+
+
 def scatter_kernel(size, partial_ref, sum_ref, held, send_sem, recv_sem):
     place = ring_place(lax.axis_index(WIDE), size)
     left = ring_device((place + size - 1) % size, size)
@@ -550,7 +698,6 @@
     inverse_one = lax.rsqrt(jnp.mean(floats * floats, axis=-1, keepdims=True) + epsilon)
     normed_one = floats * inverse_one
     upstream = cotangent.reshape(rows, width).astype(jnp.float32) * row_mask
-    upstream_all = gather_rows(upstream.astype(jnp.bfloat16), wide)
     feed_block, tokens_all, gains = lax.optimization_barrier(
         (
             by_column((gate_weight, up_weight), wide),
@@ -561,7 +708,8 @@
     floats_all = tokens_all.astype(jnp.float32)
     inverse_all = lax.rsqrt(jnp.mean(floats_all * floats_all, axis=-1, keepdims=True) + epsilon)
     first_all = (floats_all * inverse_all * gains[0]).astype(jnp.bfloat16)
-    feed_columns = to_columns(feed_block)
+    feed_block = lax.all_to_all(feed_block, WIDE, split_axis=0, concat_axis=0, tiled=True)
+    feed_shares = lax.all_gather(feed_block, NARROW)
     out_rows = gather_narrow(out_weight)
     down_rows = gather_narrow(down_weight)
 
@@ -594,13 +742,14 @@
     normed_two = middle * inverse_two
     second_all = gather_rows((normed_two * gains[1]).astype(jnp.bfloat16), wide)
 
-    front = mixed_dot(second_all, feed_columns)
+    upstream_all, front, grad_hidden, feed_columns = gather_and_feed(
+        upstream.astype(jnp.bfloat16), second_all, feed_shares, down_rows, wide
+    )
     gate_value = front[:, :hidden_width]
     up_value = front[:, hidden_width:]
     gate_sig = jax.nn.sigmoid(gate_value)
     hidden = (gate_value * gate_sig * up_value).astype(jnp.bfloat16)
 
-    grad_hidden = back_dot(upstream_all, down_rows)
     grad_gate = (
         grad_hidden * up_value * gate_sig * (1.0 + gate_value * (1.0 - gate_sig))
     ).astype(jnp.bfloat16)

time: 753 us -> 720 us (0.956)
  blocking collectives: 62.5 us -> 114 us
  waiting for transfers between devices: 145 us -> 98.5 us
  matrix products: 103 us -> 70.4 us
  local copies, waits for them, and re-layouts: 43.8 us -> 29.9 us
    all_to_all x0 -> x1, blocking collectives: none -> 50.9 us  [split_plan(): lax.all_to_all(feed_block, WIDE, split_axis=0, concat_axis=0, tiled=True)]
    pallas_call x0 -> x1, Pallas kernels: none -> 49.5 us  [gather_and_feed(): pl.pallas_call(functools.partial(feed_kernel, size), out_shape=(jax.Shape...]
    all_to_all x1 -> x0, waiting for transfers between devices: 46.4 us -> none  [to_columns(): block = lax.all_to_all(block, WIDE, split_axis=0, concat_axis=0, tiled=True)]
    pallas_call x4 -> x3, Pallas kernels: 170 us -> 125 us  [gather_rows(): pl.pallas_call(functools.partial(gather_kernel, size), out_shape=jax.Shap...]
    dot_general x4 -> x3, matrix products: 32.6 us -> 17.3 us  [mixed_dot(): return jnp.dot(left, right, preferred_element_type=jnp.float32)]
    dot_general x4 -> x3, matrix products: 36.2 us -> 22.2 us  [back_dot(): lax.dot_general(left, right, (((1,), (1,)), ((), ())), preferred_element_...]
    all_gather x2 -> x1, local copies, waits for them, and re-layouts: 14 us -> 3.06 us  [to_columns(): full = lax.all_gather(block, NARROW, axis=1, tiled=True)]
  transfers between devices with their start and end apart: 11 -> 10, of which waited for: 4 -> 3; matrix products, arithmetic and copies ran while one was open for 9% -> 6% of each run, Pallas kernels for 29% -> 24%
where the time goes in v4:
time: 720 us; the launch traced here: 715 us
  Pallas kernels  346 us (48%)
  blocking collectives  114 us (16%)
  waiting for transfers between devices  98.5 us (14%)
  matrix products  70.4 us (10%)
  other arithmetic  30.7 us (4%)
  local copies, waits for them, and re-layouts  29.9 us (4%)
  between operations  15.4 us (2%)
  starting transfers between devices  9.67 us (1%)
    pallas_call x4, Pallas kernels, scatter_rows(): pl.pallas_call(functools.partial(scatter_kernel, size), out_shape=jax.Sha...  171 us
    pallas_call x3, Pallas kernels, gather_rows(): pl.pallas_call(functools.partial(gather_kernel, size), out_shape=jax.Shap...  125 us
    reduce_scatter x2, waiting for transfers between devices, sum_narrow(): lax.psum_scatter(partial.astype(jnp.bfloat16), NARROW, scatter_dimension=...  63 us
    all_to_all x1, blocking collectives, split_plan(): lax.all_to_all(feed_block, WIDE, split_axis=0, concat_axis=0, tiled=True)  50.9 us
    pallas_call x1, Pallas kernels, gather_and_feed(): pl.pallas_call(functools.partial(feed_kernel, size), out_shape=(jax.Shape...  49.5 us
    reduce_scatter x2, waiting for transfers between devices, sum_blocks(): return lax.psum_scatter(block, NARROW, scatter_dimension=1, tiled=True)  32 us
    dot_general x4, matrix products, outer_dot(): lax.dot_general(left, right, (((0,), (0,)), ((), ())), preferred_element_...  28.1 us
    all_to_all x1, blocking collectives, to_columns(): block = lax.all_to_all(block, WIDE, split_axis=0, concat_axis=0, tiled=True)  27.4 us
  transfers between devices with their start and end apart: 10, of which 3 were waited for; matrix products, arithmetic and copies ran while one was open for 6% of the time, Pallas kernels for 24%

profile of v4, /device:TPU:0, one launch (start us, length us, event | category | flops | bytes accessed | tf_op | source)
XLA Modules:
  0.0 714.6 jit_solution(1698288033411501663)
XLA Ops:
  7.2 1.0 copy.164
  8.2 1.0 copy.165
  9.2 1.0 copy.166
  10.5 27.4 %all_to_all.35 = bf16[8,64,768]{2,1,0:T(8,128)(2,1)S(1)} all-to-all(bf16[8,64,768]{2,1,0:T(8,128)(2,1)S(1)} %copy.128), channel_id=1, replica_groups=mesh['wide'=8,'narrow'=4] {'wide'}, dimensions={0} | all-to-all | bytes 1572864 | tf_op jit(solution)/shard_map/all_to_all | solution.py:617
  37.9 1.3 copy.129
  39.2 0.7 all-gather.8.cloned.1.call-update
  40.0 0.7 all-gather.10.cloned.1.call-update
  41.4 3.6 all-to-all-start
  46.5 46.7 %gather_rows.3 = bf16[8,128,2048]{2,1,0:T(8,128)(2,1)} custom-call(bf16[128,2048]{1,0:T(8,128)(2,1)} %bitcast.125), custom_call_target="tpu_custom_call" | custom-call | bytes 150000000 | tf_op jit(solution)/shard_map/gather_rows/pallas_call | solution.py:381
  93.5 1.2 copy.137
  94.7 50.9 %all_to_all.36 = bf16[8,64,2048]{2,1,0:T(8,128)(2,1)} all-to-all(bf16[8,64,2048]{2,1,0:T(8,128)(2,1)S(1)} %copy.137), channel_id=1, replica_groups=mesh['wide'=8,'narrow'=4] {'wide'}, dimensions={0} | all-to-all | bytes 4194304 | tf_op jit(solution)/shard_map/all_to_all | solution.py:711
  146.3 0.9 fusion.32.block_ref
  147.2 3.1 fusion
  150.3 3.1 copy.130
  153.4 1.4 copy-done
  154.8 3.5 fusion.24
  158.3 0.8 slice.126
  160.4 1.2 convert_element_type.223
  161.6 2.4 fusion.51
  163.9 0.7 subtract_convert_fusion.3
  164.6 0.8 fusion.16
  165.5 1.0 copy-done.6
  167.4 0.8 copy-done.9
  168.2 4.6 convolution_convert_fusion.2
  172.7 45.3 %scatter_rows.4 = f32[128,2048]{1,0:T(8,128)} custom-call(bf16[8,128,2048]{2,1,0:T(8,128)(2,1)} %bitcast.119), custom_call_target="tpu_custom_call" | custom-call | bytes 150000000 | tf_op jit(solution)/shard_map/scatter_rows/pallas_call | solution.py:595
  218.0 1.4 multiply_reduce_fusion.3
  219.5 1.0 multiply_convert_fusion.2.block_ref
  220.4 42.7 %gather_rows.4 = bf16[8,128,2048]{2,1,0:T(8,128)(2,1)} custom-call(bf16[128,2048]{1,0:T(8,128)(2,1)} %multiply_convert_fusion.2.block_ref), custom_call_target="tpu_custom_call" | custom-call | bytes 150000000 | tf_op jit(solution)/shard_map/gather_rows/pallas_call | solution.py:381
  263.2 49.5 %shard_map.203 = (bf16[8,128,2048]{2,1,0:T(8,128)(2,1)}, f32[1024,2048]{1,0:T(8,128)}, f32[8,128,1024]{2,1,0:T(8,128)}, bf16[8,4,64,2048]{3,2,1,0:T(8,128)(2,1)}) custom-call(bf16[128,2048]{1,0:T(8,128)(2,1)} %fusion.32.block_ref, bf16[1024,2048]{1,0:T(8,128)(2,1)} %bitcast.123, bf16[4,8,64,2048]{3,2,1,0:T(8,128)(2,1)} %bitcast.127, ...), custom_call_target="tpu_custom_call" | custom-call | bytes 150000000 | tf_op jit(solution)/shard_map/pallas_call | solution.py:505
  312.7 6.4 fusion.5
  319.1 11.7 %convolution_convert_fusion = bf16[2048,2048]{1,0:T(8,128)(2,1)} fusion(bf16[1024,2048]{1,0:T(8,128)(2,1)S(1)} %bitcast.124, bf16[1024,1024]{1,0:T(8,128)(2,1)S(1)} %get-tuple-element.52, bf16[1024,1024]{1,0:T(8,128)(2,1)S(1)} %get-tuple-element.51), kind=kOutput, calls=%fused_computation.5 | convolution fusion | flops 8602517504 | bytes 16777216 | tf_op jit(solution)/shard_map/dot_general | solution.py:28
  330.8 12.8 %convolution_convert_fusion.1 = bf16[1024,2048]{1,0:T(8,128)(2,1)} fusion(bf16[2048,2048]{1,0:T(8,128)(2,1)} %bitcast.160, bf16[1024,1024]{1,0:T(8,128)(2,1)S(1)} %get-tuple-element.52, bf16[1024,1024]{1,0:T(8,128)(2,1)S(1)} %get-tuple-element.51), kind=kOutput, calls=%fused_computation.16 | convolution fusion | flops 8600420352 | bytes 16777216 | tf_op jit(solution)/shard_map/dot_general | solution.py:34
  343.6 6.3 convolution_convert_fusion.5
  350.0 9.2 %convolution_convert_fusion.4 = bf16[1024,2048]{1,0:T(8,128)(2,1)} fusion(bf16[1024,1024]{1,0:T(8,128)(2,1)} %copy-done.13, bf16[1024,2048]{1,0:T(8,128)(2,1)} %all-gather.10.cloned.1.call-done.down_ref), kind=kOutput, calls=%fused_computation.19 | convolution fusion | flops 4297064448 | bytes 10485760 | tf_op jit(solution)/shard_map/dot_general | solution.py:24
  359.2 43.5 %scatter_rows.6 = f32[128,2048]{1,0:T(8,128)} custom-call(bf16[8,128,2048]{2,1,0:T(8,128)(2,1)} %bitcast.129), custom_call_target="tpu_custom_call" | custom-call | bytes 150000000 | tf_op jit(solution)/shard_map/scatter_rows/pallas_call | solution.py:595
  402.7 1.7 multiply_reduce_fusion
  404.4 43.0 %scatter_rows.5 = f32[128,2048]{1,0:T(8,128)} custom-call(bf16[8,128,2048]{2,1,0:T(8,128)(2,1)} %bitcast.130), custom_call_target="tpu_custom_call" | custom-call | bytes 150000000 | tf_op jit(solution)/shard_map/scatter_rows/pallas_call | solution.py:595
  447.4 3.2 fusion.48
  450.5 35.8 %gather_rows.5 = bf16[8,128,2048]{2,1,0:T(8,128)(2,1)} custom-call(bf16[128,2048]{1,0:T(8,128)(2,1)} %get-tuple-element.47.block_ref), custom_call_target="tpu_custom_call" | custom-call | bytes 150000000 | tf_op jit(solution)/shard_map/gather_rows/pallas_call | solution.py:381
  486.4 4.5 convolution_convert_fusion.7
  490.9 4.4 convolution_convert_fusion.10
  495.2 1.2 reshape.336
  499.2 1.1 subtract_convert_fusion
  502.3 5.0 convolution_convert_fusion.3
  507.3 5.5 convolution_convert_fusion.6
  513.5 0.7 reduce-scatter.7.cloned.1.call-update
  514.2 0.7 reduce-scatter.11.cloned.1.call-update
  515.2 39.1 %scatter_rows.7 = f32[128,2048]{1,0:T(8,128)} custom-call(bf16[8,128,2048]{2,1,0:T(8,128)(2,1)} %bitcast.128), custom_call_target="tpu_custom_call" | custom-call | bytes 150000000 | tf_op jit(solution)/shard_map/scatter_rows/pallas_call | solution.py:595
  554.4 1.7 fusion.30
  556.3 12.4 %all_to_all.37 = f32[32,1,128]{2,1,0:T(1,128)S(1)} all-to-all(f32[32,1,128]{2,1,0:T(1,128)S(1)} %bitcast.159), channel_id=1, replica_groups=mesh['wide'=8,'narrow'=4] {'wide','narrow'}, dimensions={0} | all-to-all | bytes 32768 | tf_op jit(solution)/shard_map/all_to_all | solution.py:824
  568.7 23.9 %all_to_all.38 = bf16[8,64,768]{2,1,0:T(8,128)(2,1)S(1)} all-to-all(bf16[8,64,768]{2,1,0:T(8,128)(2,1)} %reduce-scatter.5.cloned.1.call-done), channel_id=1, replica_groups=mesh['wide'=8,'narrow'=4] {'wide'}, dimensions={0} | all-to-all | bytes 1572864 | tf_op jit(solution)/shard_map/all_to_all | solution.py:629
  592.6 32.0 %reduce-scatter.9.cloned.1.call-done = bf16[8,64,2048]{2,1,0:T(8,128)(2,1)} async-done(((bf16[8,256,2048]{2,1,0:T(8,128)(2,1)}), bf16[8,64,2048]{2,1,0:T(8,128)(2,1)}) %reduce-scatter.9.cloned.1.call-update) | async-done | bytes 2097168 | tf_op jit(solution)/shard_map/reduce_scatter | solution.py:625
  624.6 5.5 all-to-all-start.5
  630.1 1.3 fusion.29
  632.1 20.4 %reduce-scatter.7.cloned.1.call-done = bf16[64,2048]{1,0:T(8,128)(2,1)} async-done(((bf16[256,2048]{1,0:T(8,128)(2,1)}), bf16[64,2048]{1,0:T(8,128)(2,1)}) %reduce-scatter.7.cloned.1.call-update) | async-done | bytes 262160 | tf_op jit(solution)/shard_map/reduce_scatter | solution.py:642
  652.5 1.8 convert_element_type.264
  654.5 0.8 copy.157
  655.3 0.8 copy.158
  656.1 0.8 copy.159
  657.0 42.6 %reduce-scatter.11.cloned.1.call-done = bf16[256,2048]{1,0:T(8,128)(2,1)} async-done(((bf16[1024,2048]{1,0:T(8,128)(2,1)}), bf16[256,2048]{1,0:T(8,128)(2,1)}) %reduce-scatter.11.cloned.1.call-update) | async-done | bytes 1048592 | tf_op jit(solution)/shard_map/reduce_scatter | solution.py:642
  699.6 2.8 convert_element_type.271
  702.4 2.0 convert_bitcast_fusion
  704.4 1.5 copy.160
  705.9 1.5 copy.161
  (123 shorter events, 12.1 us)
Async XLA Ops:
  7.2 143.1 %all-gather.6.cloned.1.call-start = ((), (), s32[]{:S(2)}) async-start(), calls=%async_computation.10 | async-start | bytes 3932160 | tf_op jit(solution)/shard_map/all_gather | solution.py:618
  10.2 30.4 %copy-start.27 = (bf16[64]{0:T(256)(128)(2,1)S(1)}, bf16[64]{0:T(256)(128)(2,1)}, u32[]{:S(2)}) copy-start(bf16[64]{0:T(256)(128)(2,1)} %param.20) | copy-start | bytes 388
  10.3 30.4 %copy-start.28 = (bf16[64]{0:T(256)(128)(2,1)S(1)}, bf16[64]{0:T(256)(128)(2,1)}, u32[]{:S(2)}) copy-start(bf16[64]{0:T(256)(128)(2,1)} %param.15) | copy-start | bytes 388
  10.3 34.8 %copy-start.23 = (bf16[64,8192]{1,0:T(8,128)(2,1)S(1)}, bf16[64,8192]{1,0:T(8,128)(2,1)}, u32[]{:S(2)}) copy-start(bf16[64,8192]{1,0:T(8,128)(2,1)} %param.21) | copy-start | bytes 3145732
  10.3 35.4 %copy-start.24 = (bf16[64,8192]{1,0:T(8,128)(2,1)S(1)}, bf16[64,8192]{1,0:T(8,128)(2,1)}, u32[]{:S(2)}) copy-start(bf16[64,8192]{1,0:T(8,128)(2,1)} %param.22) | copy-start | bytes 3145732
  39.2 128.2 %all-gather.8.cloned.1.call-start = ((), (), s32[]{:S(2)}) async-start(), calls=%async_computation.11 | async-start | bytes 1310720 | tf_op jit(solution)/shard_map/all_gather | solution.py:638
  39.9 223.2 %all-gather.10.cloned.1.call-start = ((), (), s32[]{:S(2)}) async-start(), calls=%async_computation.12 | async-start | bytes 5242880 | tf_op jit(solution)/shard_map/all_gather | solution.py:638
  41.4 51.9 %all-to-all-start = ((bf16[32,1,128]{2,1,0:T(2,128)(2,1)}), bf16[32,1,128]{2,1,0:T(2,128)(2,1)S(1)}, u32[]{:S(2)}, u32[]{:S(2)}) async-start(bf16[32,1,128]{2,1,0:T(2,128)(2,1)} %broadcast_in_dim.2), calls=%async_computation | async-start | bytes 32768 | tf_op jit(solution)/shard_map/all_to_all | solution.py:687
  45.0 218.1 %all-gather.12.cloned.1.call-start = ((), (), s32[]{:S(2)}) async-start(), calls=%async_computation.17 | async-start | bytes 10485760 | tf_op jit(solution)/shard_map/all_gather | solution.py:712
  94.7 51.2 %copy-start.29 = (s32[2,1]{0,1:T(1,128)S(1)}, s32[2,1]{0,1:T(1,128)}, u32[]{:S(2)}) copy-start(s32[2,1]{0,1:T(1,128)} %param.13) | copy-start | bytes 28
  94.7 51.6 %copy-start.22 = (bf16[2,64,2048]{2,1,0:T(8,128)(2,1)S(1)}, bf16[2,64,2048]{2,1,0:T(8,128)(2,1)}, u32[]{:S(2)}) copy-start(bf16[2,64,2048]{2,1,0:T(8,128)(2,1)} %param.14) | copy-start | bytes 1572868
  145.6 423.1 %reduce-scatter.5.cloned.1.call-start = ((), (), s32[]{:S(2)}) async-start(), calls=%async_computation.13 | async-start | bytes 3932160 | tf_op jit(solution)/shard_map/reduce_scatter | solution.py:625
  150.3 4.5 copy-start
  153.4 4.9 copy-start.11
  164.6 2.2 copy-start.14
  164.6 2.2 copy-start.16
  164.6 2.2 copy-start.18
  164.6 2.2 copy-start.20
  165.5 1.0 copy-start.6
  167.4 0.8 copy-start.9
  172.7 45.3 %copy-start.3 = (bf16[2,64,2048]{2,1,0:T(8,128)(2,1)S(1)}, bf16[2,64,2048]{2,1,0:T(8,128)(2,1)}, u32[]{:S(2)}) copy-start(bf16[2,64,2048]{2,1,0:T(8,128)(2,1)} %param.12) | copy-start | bytes 1572868
  312.7 6.4 copy-start.2
  319.1 24.5 %copy-start.13 = (bf16[1024,1024]{1,0:T(8,128)(2,1)}, bf16[1024,1024]{1,0:T(8,128)(2,1)S(1)}, u32[]{:S(2)}) copy-start(bf16[1024,1024]{1,0:T(8,128)(2,1)S(1)} %get-tuple-element.53) | copy-start | bytes 6291460
  330.8 12.8 %copy-start.26 = (bf16[8,128,2048]{2,1,0:T(8,128)(2,1)S(1)}, bf16[8,128,2048]{2,1,0:T(8,128)(2,1)}, u32[]{:S(2)}) copy-start(bf16[8,128,2048]{2,1,0:T(8,128)(2,1)} %get-tuple-element.32) | copy-start | bytes 12582916
  402.7 44.6 %copy-start.4 = (f32[128,2048]{1,0:T(8,128)S(1)}, f32[128,2048]{1,0:T(8,128)}, u32[]{:S(2)}) copy-start(f32[128,2048]{1,0:T(8,128)} %scatter_rows.6) | copy-start | bytes 3145732
  450.5 35.8 %copy-start.10 = (bf16[16,64,2,128]{3,2,1,0:T(2,128)(2,1)S(1)}, bf16[16,64,2,128]{3,2,1,0:T(2,128)(2,1)}, u32[]{:S(2)}) copy-start(bf16[16,64,2,128]{3,2,1,0:T(2,128)(2,1)} %copy-done.9) | copy-start | bytes 1572868
  486.3 4.5 copy-start.25
  490.9 5.6 copy-start.7
  495.2 2.9 copy-start.15
  496.5 1.0 copy-start.19
  496.5 1.2 copy-start.21
  496.5 1.6 copy-start.17
  500.3 2.0 copy-start.12
  502.3 5.0 copy-start.1
  512.9 111.7 %reduce-scatter.9.cloned.1.call-start = ((), (), s32[]{:S(2)}) async-start(), calls=%async_computation.15 | async-start | bytes 10485760 | tf_op jit(solution)/shard_map/reduce_scatter | solution.py:625
  513.4 139.1 %reduce-scatter.7.cloned.1.call-start = ((), (), s32[]{:S(2)}) async-start(), calls=%async_computation.14 | async-start | bytes 1310720 | tf_op jit(solution)/shard_map/reduce_scatter | solution.py:642
  514.2 185.4 %reduce-scatter.11.cloned.1.call-start = ((), (), s32[]{:S(2)}) async-start(), calls=%async_computation.16 | async-start | bytes 5242880 | tf_op jit(solution)/shard_map/reduce_scatter | solution.py:642
  554.4 75.7 %copy-start.5 = (f32[128,2048]{1,0:T(8,128)S(1)}, f32[128,2048]{1,0:T(8,128)}, u32[]{:S(2)}) copy-start(f32[128,2048]{1,0:T(8,128)} %scatter_rows.7) | copy-start | bytes 3145732
  554.4 75.7 %copy-start.8 = (f32[128,2048]{1,0:T(8,128)S(1)}, f32[128,2048]{1,0:T(8,128)}, u32[]{:S(2)}) copy-start(f32[128,2048]{1,0:T(8,128)} %get-tuple-element.48) | copy-start | bytes 3145732
  624.6 77.8 %all-to-all-start.5 = ((bf16[8,64,2048]{2,1,0:T(8,128)(2,1)}), bf16[8,64,2048]{2,1,0:T(8,128)(2,1)}, u32[]{:S(2)}, u32[]{:S(2)}) async-start(bf16[8,64,2048]{2,1,0:T(8,128)(2,1)} %reduce-scatter.9.cloned.1.call-done), calls=%async_computation.8 | async-start | bytes 4194304 | tf_op jit(solution)/shard_map/all_to_all | solution.py:629
Sparse Core Ops, SparseCore 0:
  39.3 27.6 all-gather.5
  68.6 16.5 all-gather.7
  86.8 34.4 all-gather.9
  145.7 57.1 all-gather.11
  513.0 37.7 reduce-scatter.4
  553.3 71.2 reduce-scatter.8
  627.7 24.7 reduce-scatter.6
  655.0 44.5 reduce-scatter.10

commit v5 on v4

--- a/solution.py
+++ b/solution.py
@@ -543,24 +543,36 @@
     )
 
 
-def scatter_kernel(size, partial_ref, sum_ref, held, send_sem, recv_sem):
+def scatter_kernel(size, flipped, left_ref, right_ref, sum_ref, term, first, held, send_sem, recv_sem):
     place = ring_place(lax.axis_index(WIDE), size)
     left = ring_device((place + size - 1) % size, size)
     right = ring_device((place + 1) % size, size)
-    rows, width = sum_ref.shape
-    rows, width = rows // 2, width // 2
+    tall, wide = sum_ref.shape
+    rows, width = tall // 2, wide // 2
+    tile = width // 4
 
     def cut(way, part):
         return pl.ds(part * rows, rows), pl.ds(way * width, width)
 
-    def mine(way, hop, part):
+    def compute(way, hop):
         block = ring_device((place + 2 * size - 1 - hop if way == 0 else place + 1 + hop) % size, size)
-        return partial_ref.at[(block, *cut(way, part))]
+        own = pl.ds(pl.multiple_of(block * tall, tall), tall)
+
+        def step(index, carry):
+            columns = pl.ds(pl.multiple_of(way * width + index * tile, tile), tile)
+            target = pl.ds(pl.multiple_of(index * tile, tile), tile)
+            if flipped:
+                term[way, :, target] = back_dot(left_ref[own, :], right_ref[columns, :])
+            else:
+                term[way, :, target] = mixed_dot(left_ref[own, :], right_ref[:, columns])
+            return carry
+
+        lax.fori_loop(0, width // tile, step, 0)
 
     def copy(way, hop, part):
-        source = mine(way, hop, part) if hop == 0 else held.at[(hop - 1, *cut(way, part))]
+        source = first if hop == 0 else held.at[hop - 1]
         return pltpu.make_async_remote_copy(
-            src_ref=source,
+            src_ref=source.at[cut(way, part)],
             dst_ref=held.at[(hop, *cut(way, part))],
             send_sem=send_sem.at[way, hop, part],
             recv_sem=recv_sem.at[way, hop, part],
@@ -571,41 +583,45 @@
     enter_ring(left, right)
     sent = {}
     for hop in range(size):
+        for way in range(2):
+            compute(way, hop)
         for part in range(2):
             for way in range(2):
+                total = term[way, pl.ds(part * rows, rows), :]
                 if hop:
                     sent[way, hop - 1, part].wait_recv()
-                    arrived = held.at[(hop - 1, *cut(way, part))]
-                    total = arrived[...].astype(jnp.float32) + mine(way, hop, part)[...].astype(
-                        jnp.float32
-                    )
-                    if hop == size - 1:
-                        sum_ref[cut(way, part)] = total
-                        continue
-                    arrived[...] = total.astype(jnp.bfloat16)
+                    total += held[(hop - 1, *cut(way, part))].astype(jnp.float32)
+                if hop == size - 1:
+                    sum_ref[cut(way, part)] = total
+                    continue
+                source = first if hop == 0 else held.at[hop - 1]
+                source[cut(way, part)] = total.astype(jnp.bfloat16)
                 sent[way, hop, part] = copy(way, hop, part)
                 sent[way, hop, part].start()
     for transfer in sent.values():
         transfer.wait_send()
 
 
-def scatter_rows(partial, size):
-    rows, width = partial.shape[0] // size, partial.shape[1]
+def scatter_rows(left, right, size, flipped, identity):
+    rows = left.shape[0] // size
+    width = right.shape[0 if flipped else 1]
     steps = size - 1
     return pl.pallas_call(
-        functools.partial(scatter_kernel, size),
+        functools.partial(scatter_kernel, size, flipped),
         out_shape=jax.ShapeDtypeStruct((rows, width), jnp.float32),
-        in_specs=[pl.BlockSpec(memory_space=pltpu.VMEM)],
+        in_specs=[pl.BlockSpec(memory_space=pltpu.VMEM)] * 2,
         out_specs=pl.BlockSpec(memory_space=pltpu.VMEM),
         scratch_shapes=[
+            pltpu.VMEM((2, rows, width // 2), jnp.float32),
+            pltpu.VMEM((rows, width), jnp.bfloat16),
             pltpu.VMEM((steps, rows, width), jnp.bfloat16),
             pltpu.SemaphoreType.DMA((2, steps, 2)),
             pltpu.SemaphoreType.DMA((2, steps, 2)),
         ],
-        compiler_params=pltpu.CompilerParams(collective_id=1, has_side_effects=True),
+        compiler_params=pltpu.CompilerParams(collective_id=identity, has_side_effects=True),
         cost_estimate=RING_COST,
         name="scatter_rows",
-    )(partial.astype(jnp.bfloat16).reshape(size, rows, width))
+    )(left, right)
 
 
 def by_column(weights, wide):
@@ -735,8 +751,7 @@
         .astype(jnp.bfloat16)
         .reshape(sequences * length, head_width)
     )
-    out_term = mixed_dot(attended, out_rows).astype(jnp.bfloat16)
-    middle = floats + scatter_rows(out_term, wide)
+    middle = floats + scatter_rows(attended, out_rows, wide, False, 1)
 
     inverse_two = lax.rsqrt(jnp.mean(middle * middle, axis=-1, keepdims=True) + epsilon)
     normed_two = middle * inverse_two
@@ -755,20 +770,12 @@
     ).astype(jnp.bfloat16)
     grad_up = (grad_hidden * gate_value * gate_sig).astype(jnp.bfloat16)
     grad_front = jnp.concatenate([grad_gate, grad_up], axis=1)
-    down_term, front_term, feed_term, second_term = lax.optimization_barrier(
-        (
-            outer_dot(hidden, upstream_all).astype(jnp.bfloat16),
-            outer_dot(second_all, grad_front).astype(jnp.bfloat16),
-            mixed_dot(hidden, down_rows).astype(jnp.bfloat16),
-            back_dot(grad_front, feed_columns).astype(jnp.bfloat16),
-        )
-    )
+    down_term = outer_dot(hidden, upstream_all).astype(jnp.bfloat16)
+    front_term = outer_dot(second_all, grad_front).astype(jnp.bfloat16)
     down_grad = sum_narrow(down_term)
     front_block = sum_blocks(front_term, wide)
-    grad_second = scatter_rows(second_term, wide)
-    feed_out = scatter_rows(feed_term, wide)
+    grad_second = scatter_rows(grad_front, feed_columns, wide, True, 3)
     front_block = to_rows(front_block)
-    layer_output = ((middle + feed_out) * row_mask).astype(jnp.bfloat16)
     gate_grad = own_rows(front_block, 0, hidden_width)
     up_grad = own_rows(front_block, hidden_width, hidden_width)
 
@@ -809,14 +816,11 @@
         ],
         axis=1,
     )
-    attend_term, first_term = lax.optimization_barrier(
-        (
-            outer_dot(first_all, grad_joint).astype(jnp.bfloat16),
-            back_dot(grad_joint, attend_columns).astype(jnp.bfloat16),
-        )
-    )
+    attend_term = outer_dot(first_all, grad_joint).astype(jnp.bfloat16)
     attend_block = sum_blocks(attend_term, wide)
-    grad_first = scatter_rows(first_term, wide)
+    grad_first = scatter_rows(grad_joint, attend_columns, wide, True, 5)
+    feed_out = scatter_rows(hidden, down_rows, wide, False, 4)
+    layer_output = ((middle + feed_out) * row_mask).astype(jnp.bfloat16)
     attend_block = to_rows(attend_block)
     gain_one = jnp.sum(grad_first * normed_one, axis=0)
     input_grad = grad_middle + norm_back(grad_first * gains[0], normed_one, inverse_one)

time: 720 us -> 685 us (0.951)
  waiting for transfers between devices: 98.5 us -> 70.5 us
  matrix products: 70.4 us -> 47.4 us
  Pallas kernels: 346 us -> 366 us
    reduce_scatter x2, waiting for transfers between devices: 32 us -> 5.78 us  [sum_blocks(): return lax.psum_scatter(block, NARROW, scatter_dimension=1, tiled=True)]
    dot_general x3 -> x1, matrix products: 22.2 us -> 4.57 us  [back_dot(): lax.dot_general(left, right, (((1,), (1,)), ((), ())), preferred_element_...]
    pallas_call x4, Pallas kernels: 171 us -> 186 us  [scatter_rows(): pl.pallas_call(functools.partial(scatter_kernel, size, flipped), out_shap...]
    dot_general x3 -> x1, matrix products: 17.3 us -> 7.4 us  [mixed_dot(): return jnp.dot(left, right, preferred_element_type=jnp.float32)]
  transfers between devices with their start and end apart: 10 -> 10, of which waited for: 3 -> 3; matrix products, arithmetic and copies ran while one was open for 6% -> 9% of each run, Pallas kernels for 24% -> 26%
where the time goes in v5:
time: 685 us; the launch traced here: 680 us
  Pallas kernels  366 us (53%)
  blocking collectives  113 us (16%)
  waiting for transfers between devices  70.5 us (10%)
  matrix products  47.4 us (7%)
  other arithmetic  34.2 us (5%)
  local copies, waits for them, and re-layouts  24.7 us (4%)
  between operations  15.2 us (2%)
  starting transfers between devices  9.49 us (1%)
    pallas_call x4, Pallas kernels, scatter_rows(): pl.pallas_call(functools.partial(scatter_kernel, size, flipped), out_shap...  186 us
    pallas_call x3, Pallas kernels, gather_rows(): pl.pallas_call(functools.partial(gather_kernel, size), out_shape=jax.Shap...  127 us
    reduce_scatter x2, waiting for transfers between devices, sum_narrow(): lax.psum_scatter(partial.astype(jnp.bfloat16), NARROW, scatter_dimension=...  62.5 us
    pallas_call x1, Pallas kernels, gather_and_feed(): pl.pallas_call(functools.partial(feed_kernel, size), out_shape=(jax.Shape...  52 us
    all_to_all x1, blocking collectives, split_plan(): lax.all_to_all(feed_block, WIDE, split_axis=0, concat_axis=0, tiled=True)  50.9 us
    dot_general x4, matrix products, outer_dot(): lax.dot_general(left, right, (((0,), (0,)), ((), ())), preferred_element_...  32.6 us
    all_to_all x1, blocking collectives, to_columns(): block = lax.all_to_all(block, WIDE, split_axis=0, concat_axis=0, tiled=True)  27.3 us
    all_to_all x1, blocking collectives, to_rows(): return lax.all_to_all(block, WIDE, split_axis=0, concat_axis=0, tiled=True)  23.9 us
  transfers between devices with their start and end apart: 10, of which 3 were waited for; matrix products, arithmetic and copies ran while one was open for 9% of the time, Pallas kernels for 26%

profile of v5, /device:TPU:0, one launch (start us, length us, event | category | flops | bytes accessed | tf_op | source)
XLA Modules:
  0.0 679.6 jit_solution(5677773620039919491)
XLA Ops:
  7.3 1.0 copy.160
  8.3 1.2 copy_bitcast_fusion.1
  9.6 27.3 %all_to_all.35 = bf16[8,64,768]{2,1,0:T(8,128)(2,1)} all-to-all(bf16[8,64,768]{2,1,0:T(8,128)(2,1)S(1)} %maximum_bitcast_fusion.1), channel_id=1, replica_groups=mesh['wide'=8,'narrow'=4] {'wide'}, dimensions={0} | all-to-all | bytes 1572864 | tf_op jit(solution)/shard_map/all_to_all | solution.py:633
  37.0 0.7 all-gather.8.cloned.1.call-update
  37.7 0.7 all-gather.10.cloned.1.call-update
  38.5 0.6 broadcast_in_dim.2
  39.1 3.6 all-to-all-start
  42.8 0.6 copy.129
  43.4 0.6 copy.130
  44.2 46.7 %gather_rows.3 = bf16[8,128,2048]{2,1,0:T(8,128)(2,1)} custom-call(bf16[128,2048]{1,0:T(8,128)(2,1)} %bitcast.117), custom_call_target="tpu_custom_call" | custom-call | bytes 150000000 | tf_op jit(solution)/shard_map/gather_rows/pallas_call | solution.py:381
  91.2 1.2 copy.101
  92.4 50.9 %all_to_all.36 = bf16[8,64,2048]{2,1,0:T(8,128)(2,1)} all-to-all(bf16[8,64,2048]{2,1,0:T(8,128)(2,1)S(1)} %copy.101), channel_id=1, replica_groups=mesh['wide'=8,'narrow'=4] {'wide'}, dimensions={0} | all-to-all | bytes 4194304 | tf_op jit(solution)/shard_map/all_to_all | solution.py:727
  143.8 0.9 fusion.32.block_ref
  144.7 3.1 fusion
  147.8 7.4 %fusion.24 = f32[1024,768]{1,0:T(8,128)S(1)} fusion(bf16[2048,768]{1,0:T(8,128)(2,1)} %bitcast.126, bf16[1024,2048]{1,0:T(8,128)(2,1)} %bitcast.113, f32[2048]{0:T(1024)S(1)} %reshape.306, f32[1024]{0:T(1024)S(1)} %add_rsqrt_fusion), kind=kOutput, calls=%fused_computation.46 | convolution fusion | flops 3229614080 | bytes 10498048 | tf_op jit(solution)/shard_map/dot_general | solution.py:24
  155.2 0.8 slice.126
  157.3 1.2 convert_element_type.211
  158.5 1.2 fusion.45
  159.7 1.2 fusion.46
  160.8 0.6 subtract_convert_fusion.3
  161.5 0.8 fusion.16
  163.3 0.8 copy-done.18
  164.1 0.9 copy.159
  165.0 45.6 %scatter_rows.4 = f32[128,2048]{1,0:T(8,128)} custom-call(bf16[1024,256]{1,0:T(8,128)(2,1)} %bitcast.128, bf16[256,2048]{1,0:T(8,128)(2,1)} %all-gather.8.cloned.1.call-done.right_ref), custom_call_target="tpu_custom_call" | custom-call | bytes 150000000 | tf_op jit(solution)/shard_map/scatter_rows/pallas_call | solution.py:609
  210.6 1.4 multiply_reduce_fusion.3
  212.1 1.0 multiply_convert_fusion.2.block_ref
  213.0 41.8 %gather_rows.4 = bf16[8,128,2048]{2,1,0:T(8,128)(2,1)} custom-call(bf16[128,2048]{1,0:T(8,128)(2,1)} %multiply_convert_fusion.2.block_ref), custom_call_target="tpu_custom_call" | custom-call | bytes 150000000 | tf_op jit(solution)/shard_map/gather_rows/pallas_call | solution.py:381
  254.9 52.0 %shard_map.203 = (bf16[8,128,2048]{2,1,0:T(8,128)(2,1)}, f32[1024,2048]{1,0:T(8,128)}, f32[8,128,1024]{2,1,0:T(8,128)}, bf16[8,4,64,2048]{3,2,1,0:T(8,128)(2,1)}) custom-call(bf16[128,2048]{1,0:T(8,128)(2,1)} %fusion.32.block_ref, bf16[1024,2048]{1,0:T(8,128)(2,1)} %bitcast.115, bf16[4,8,64,2048]{3,2,1,0:T(8,128)(2,1)} %bitcast.118, ...), custom_call_target="tpu_custom_call" | custom-call | bytes 150000000 | tf_op jit(solution)/shard_map/pallas_call | solution.py:505
  306.9 7.2 %fusion.5 = (bf16[1024,1024]{1,0:T(8,128)(2,1)S(1)}, bf16[1024,1024]{1,0:T(8,128)(2,1)S(1)}, bf16[1024,1024]{1,0:T(8,128)(2,1)}) fusion(f32[8,128,1024]{2,1,0:T(8,128)} %get-tuple-element.26, f32[1024,2048]{1,0:T(8,128)} %get-tuple-element.25), kind=kLoop, calls=%fused_computation.11 | loop fusion | flops 16777216 | bytes 18874368 | tf_op jit(solution)/shard_map/convert_element_type | solution.py:770
  314.2 2.7 pad_maximum_fusion.left_ref
  316.9 0.6 copy-done.6
  317.4 51.0 %scatter_rows.6 = f32[128,2048]{1,0:T(8,128)} custom-call(bf16[1024,2048]{1,0:T(8,128)(2,1)} %pad_maximum_fusion.left_ref, bf16[2048,2048]{1,0:T(8,128)(2,1)} %bitcast.120), custom_call_target="tpu_custom_call" | custom-call | bytes 150000000 | tf_op jit(solution)/shard_map/scatter_rows/pallas_call | solution.py:609
  368.5 1.6 multiply_reduce_fusion
  370.0 45.8 %scatter_rows.5 = f32[128,2048]{1,0:T(8,128)} custom-call(bf16[1024,1024]{1,0:T(8,128)(2,1)} %get-tuple-element.41.left_ref, bf16[1024,2048]{1,0:T(8,128)(2,1)} %all-gather.10.cloned.1.call-done.down_ref.right_ref), custom_call_target="tpu_custom_call" | custom-call | bytes 150000000 | tf_op jit(solution)/shard_map/scatter_rows/pallas_call | solution.py:609
  415.8 3.5 fusion.42
  419.3 38.5 %gather_rows.5 = bf16[8,128,2048]{2,1,0:T(8,128)(2,1)} custom-call(bf16[128,2048]{1,0:T(8,128)(2,1)} %get-tuple-element.35.block_ref), custom_call_target="tpu_custom_call" | custom-call | bytes 150000000 | tf_op jit(solution)/shard_map/gather_rows/pallas_call | solution.py:381
  457.8 4.4 convolution_convert_fusion.3
  462.3 4.6 convolution_convert_fusion.6
  466.8 1.2 reshape.320
  470.2 0.5 copy.109
  470.8 0.8 subtract_convert_fusion
  473.8 5.5 convolution_convert_fusion.2
  479.4 13.9 %convolution_convert_fusion = bf16[2048,2048]{1,0:T(8,128)(2,1)} fusion(bf16[1024,2048]{1,0:T(8,128)(2,1)} %bitcast.116, bf16[1024,1024]{1,0:T(8,128)(2,1)} %copy-done.6, bf16[1024,1024]{1,0:T(8,128)(2,1)S(1)} %copy-done.5), kind=kOutput, calls=%fused_computation.5 | convolution fusion | flops 8602517504 | bytes 16777216 | tf_op jit(solution)/shard_map/dot_general | solution.py:28
  493.3 0.7 reduce-scatter.7.cloned.1.call-update
  494.0 0.8 copy-done.3
  494.8 8.9 %convolution_convert_fusion.1 = bf16[1024,2048]{1,0:T(8,128)(2,1)} fusion(bf16[1024,1024]{1,0:T(8,128)(2,1)S(1)} %copy-done.3, bf16[1024,2048]{1,0:T(8,128)(2,1)} %bitcast.149), kind=kOutput, calls=%fused_computation.16 | convolution fusion | flops 4297064448 | bytes 10485760 | tf_op jit(solution)/shard_map/dot_general | solution.py:28
  504.0 44.1 %scatter_rows.7 = f32[128,2048]{1,0:T(8,128)} custom-call(bf16[1024,768]{1,0:T(8,128)(2,1)} %copy-done.8, bf16[2048,768]{1,0:T(8,128)(2,1)} %bitcast.127), custom_call_target="tpu_custom_call" | custom-call | bytes 150000000 | tf_op jit(solution)/shard_map/scatter_rows/pallas_call | solution.py:609
  548.1 1.7 fusion.30
  550.1 10.4 %all_to_all.37 = f32[32,1,128]{2,1,0:T(1,128)S(1)} all-to-all(f32[32,1,128]{2,1,0:T(1,128)S(1)} %bitcast.148), channel_id=1, replica_groups=mesh['wide'=8,'narrow'=4] {'wide','narrow'}, dimensions={0} | all-to-all | bytes 32768 | tf_op jit(solution)/shard_map/all_to_all | solution.py:828
  560.5 23.9 %all_to_all.38 = bf16[8,64,768]{2,1,0:T(8,128)(2,1)S(1)} all-to-all(bf16[8,64,768]{2,1,0:T(8,128)(2,1)} %reduce-scatter.5.cloned.1.call-done), channel_id=1, replica_groups=mesh['wide'=8,'narrow'=4] {'wide'}, dimensions={0} | all-to-all | bytes 1572864 | tf_op jit(solution)/shard_map/all_to_all | solution.py:645
  584.4 5.8 reduce-scatter.9.cloned.1.call-done
  590.2 5.5 all-to-all-start.5
  595.7 1.3 fusion.29
  597.1 0.6 fusion.48
  597.7 19.8 %reduce-scatter.7.cloned.1.call-done = bf16[64,2048]{1,0:T(8,128)(2,1)} async-done(((bf16[256,2048]{1,0:T(8,128)(2,1)}), bf16[64,2048]{1,0:T(8,128)(2,1)}) %reduce-scatter.7.cloned.1.call-update) | async-done | bytes 262160 | tf_op jit(solution)/shard_map/reduce_scatter | solution.py:658
  617.5 1.8 convert_element_type.246
  619.5 0.8 copy.124
  620.3 0.8 copy.125
  621.2 0.8 copy.126
  622.0 42.6 %reduce-scatter.11.cloned.1.call-done = bf16[256,2048]{1,0:T(8,128)(2,1)} async-done(((bf16[1024,2048]{1,0:T(8,128)(2,1)}), bf16[256,2048]{1,0:T(8,128)(2,1)}) %reduce-scatter.11.cloned.1.call-update) | async-done | bytes 1048592 | tf_op jit(solution)/shard_map/reduce_scatter | solution.py:658
  664.6 2.8 convert_element_type.255
  667.4 2.0 convert_bitcast_fusion
  669.4 1.5 copy.127
  670.9 1.5 copy.128
  (108 shorter events, 8.6 us)
Async XLA Ops:
  7.2 31.2 %copy-start.23 = (bf16[64]{0:T(256)(128)(2,1)S(1)}, bf16[64]{0:T(256)(128)(2,1)}, u32[]{:S(2)}) copy-start(bf16[64]{0:T(256)(128)(2,1)} %param.15) | copy-start | bytes 388
  7.2 31.2 %copy-start.22 = (bf16[64]{0:T(256)(128)(2,1)S(1)}, bf16[64]{0:T(256)(128)(2,1)}, u32[]{:S(2)}) copy-start(bf16[64]{0:T(256)(128)(2,1)} %param.20) | copy-start | bytes 388
  7.2 35.6 %copy-start.20 = (bf16[64,8192]{1,0:T(8,128)(2,1)S(1)}, bf16[64,8192]{1,0:T(8,128)(2,1)}, u32[]{:S(2)}) copy-start(bf16[64,8192]{1,0:T(8,128)(2,1)} %param.21) | copy-start | bytes 3145732
  7.2 140.6 %all-gather.6.cloned.1.call-start = ((), (), s32[]{:S(2)}) async-start(), calls=%async_computation.10 | async-start | bytes 3932160 | tf_op jit(solution)/shard_map/all_gather | solution.py:634
  8.3 35.1 %copy-start.21 = (bf16[64,8192]{1,0:T(8,128)(2,1)S(1)}, bf16[64,8192]{1,0:T(8,128)(2,1)}, u32[]{:S(2)}) copy-start(bf16[64,8192]{1,0:T(8,128)(2,1)} %param.22) | copy-start | bytes 3145732
  36.9 128.1 %all-gather.8.cloned.1.call-start = ((), (), s32[]{:S(2)}) async-start(), calls=%async_computation.11 | async-start | bytes 1310720 | tf_op jit(solution)/shard_map/all_gather | solution.py:654
  37.7 217.2 %all-gather.10.cloned.1.call-start = ((), (), s32[]{:S(2)}) async-start(), calls=%async_computation.12 | async-start | bytes 5242880 | tf_op jit(solution)/shard_map/all_gather | solution.py:654
  39.1 51.9 %all-to-all-start = ((bf16[32,1,128]{2,1,0:T(2,128)(2,1)}), bf16[32,1,128]{2,1,0:T(2,128)(2,1)S(1)}, u32[]{:S(2)}, u32[]{:S(2)}) async-start(bf16[32,1,128]{2,1,0:T(2,128)(2,1)} %broadcast_in_dim.2), calls=%async_computation | async-start | bytes 32768 | tf_op jit(solution)/shard_map/all_to_all | solution.py:703
  42.8 212.2 %all-gather.12.cloned.1.call-start = ((), (), s32[]{:S(2)}) async-start(), calls=%async_computation.17 | async-start | bytes 10485760 | tf_op jit(solution)/shard_map/all_gather | solution.py:728
  92.4 51.0 %copy-start.24 = (s32[2,1]{0,1:T(1,128)S(1)}, s32[2,1]{0,1:T(1,128)}, u32[]{:S(2)}) copy-start(s32[2,1]{0,1:T(1,128)} %param.13) | copy-start | bytes 28
  92.4 51.4 %copy-start.17 = (bf16[2,64,2048]{2,1,0:T(8,128)(2,1)S(1)}, bf16[2,64,2048]{2,1,0:T(8,128)(2,1)}, u32[]{:S(2)}) copy-start(bf16[2,64,2048]{2,1,0:T(8,128)(2,1)} %param.14) | copy-start | bytes 1572868
  143.3 417.2 %reduce-scatter.5.cloned.1.call-start = ((), (), s32[]{:S(2)}) async-start(), calls=%async_computation.13 | async-start | bytes 3932160 | tf_op jit(solution)/shard_map/reduce_scatter | solution.py:641
  161.5 1.2 copy-start.9
  161.5 1.2 copy-start.11
  161.5 1.2 copy-start.13
  161.5 1.3 copy-start.15
  162.4 48.2 %copy-start.1 = (bf16[2,64,2048]{2,1,0:T(8,128)(2,1)S(1)}, bf16[2,64,2048]{2,1,0:T(8,128)(2,1)}, u32[]{:S(2)}) copy-start(bf16[2,64,2048]{2,1,0:T(8,128)(2,1)} %param.12) | copy-start | bytes 1572868
  163.3 0.8 copy-start.18
  314.2 2.7 copy-start.4
  314.2 3.3 copy-start.6
  419.3 38.5 %copy-start.19 = (bf16[16,64,2,128]{3,2,1,0:T(2,128)(2,1)S(1)}, bf16[16,64,2,128]{3,2,1,0:T(2,128)(2,1)}, u32[]{:S(2)}) copy-start(bf16[16,64,2,128]{3,2,1,0:T(2,128)(2,1)} %copy-done.18) | copy-start | bytes 1572868
  466.8 2.9 copy-start.10
  468.1 1.0 copy-start.14
  468.1 1.2 copy-start.16
  468.1 1.6 copy-start.12
  471.6 2.2 copy-start
  473.8 5.5 copy-start.8
  473.8 5.6 copy-start.5
  479.3 110.9 %reduce-scatter.9.cloned.1.call-start = ((), (), s32[]{:S(2)}) async-start(), calls=%async_computation.15 | async-start | bytes 10485760 | tf_op jit(solution)/shard_map/reduce_scatter | solution.py:641
  493.2 1.6 copy-start.3
  493.2 124.3 %reduce-scatter.7.cloned.1.call-start = ((), (), s32[]{:S(2)}) async-start(), calls=%async_computation.14 | async-start | bytes 1310720 | tf_op jit(solution)/shard_map/reduce_scatter | solution.py:658
  494.0 170.7 %reduce-scatter.11.cloned.1.call-start = ((), (), s32[]{:S(2)}) async-start(), calls=%async_computation.16 | async-start | bytes 5242880 | tf_op jit(solution)/shard_map/reduce_scatter | solution.py:658
  548.1 47.6 %copy-start.2 = (f32[128,2048]{1,0:T(8,128)S(1)}, f32[128,2048]{1,0:T(8,128)}, u32[]{:S(2)}) copy-start(f32[128,2048]{1,0:T(8,128)} %scatter_rows.7) | copy-start | bytes 3145732
  548.1 47.6 %copy-start.7 = (f32[128,2048]{1,0:T(8,128)S(1)}, f32[128,2048]{1,0:T(8,128)}, u32[]{:S(2)}) copy-start(f32[128,2048]{1,0:T(8,128)} %get-tuple-element.36) | copy-start | bytes 3145732
  590.2 77.3 %all-to-all-start.5 = ((bf16[8,64,2048]{2,1,0:T(8,128)(2,1)}), bf16[8,64,2048]{2,1,0:T(8,128)(2,1)}, u32[]{:S(2)}, u32[]{:S(2)}) async-start(bf16[8,64,2048]{2,1,0:T(8,128)(2,1)} %reduce-scatter.9.cloned.1.call-done), calls=%async_computation.8 | async-start | bytes 4194304 | tf_op jit(solution)/shard_map/all_to_all | solution.py:645
Sparse Core Ops, SparseCore 0:
  37.0 27.6 all-gather.5
  66.3 16.5 all-gather.7
  84.5 34.4 all-gather.9
  143.4 57.2 all-gather.11
  479.4 36.7 reduce-scatter.4
  518.6 71.4 reduce-scatter.8
  592.7 24.7 reduce-scatter.6
  620.0 44.5 reduce-scatter.10
